TPU v7x, 32 devices: a whole 2x2x4 slice. The times are simulated.
32 devices in a mesh: group: 2 (over x), region: 16 (over z, y, core).
Axes of the slice: x: 2, y: 2, z: 4, core: 2. Of those that a mesh axis runs over, the one named last changes fastest.
Arguments:
- first_map: bfloat16 [64, 512, 256], P('region', 'group'), parts along dimension 1, may hold values from -6 to 6
- second_map: bfloat16 [64, 512, 256], P('region', 'group'), parts along dimension 1, may hold values from -6 to 6
- flow_target: float32 [2, 64, 512], P(None, 'region', 'group'), parts along dimension 2, may hold values from -48 to 48
- valid_tiles: int32 [4, 32], P(None, 'group'), parts along dimension 1, may hold values 0 or 1
- conv_weight: bfloat16 [9, 81, 256], replicated, may hold values from -0.21875 to 0.21875
- conv_bias: float32 [256], replicated, may hold values from -3 to 3
- head_weight: bfloat16 [2, 256], replicated, may hold values from -4 to 4
Outputs:
- first_grad: bfloat16 [64, 512, 256], P('region', 'group'), parts along dimension 1
- second_grad: bfloat16 [64, 512, 256], P('region', 'group'), parts along dimension 1
- conv_grad: float32 [18, 81, 256], P('group', None, 'region'), parts along dimension 0
- bias_grad: float32 [512], P(('group', 'region')), parts along dimension 0
- head_grad: float32 [4, 256], P('group', 'region'), parts along dimension 0
There are 2 independent parts, one for each index of `group`. A program takes and returns all parts, laid end to end along the dimension named above; an argument that names none is the same for every part. Nothing has to cross between parts.
All inputs are finite; a program needn't handle non-finite values.
Results may differ from a plain program's by a relative error of at most 0.007.
Values may be sent and summed in bfloat16 or wider, within the bound.
No kernel may reach another device: no remote copies, remote signals or barrier semaphores. Data moves between devices by JAX's collectives and lax.ppermute only.
A program may use at most 64 MiB of HBM per device.

v0:
```python
import math

import jax
import jax.numpy as jnp
from jax import lax
from jax.sharding import PartitionSpec as P

C = 256
RADIUS = 4
TILE = 16
K = 81


clip_fraction = 0.25


def extended(block, sides, width):
    for axis, dim in sides:
        count = lax.axis_size(axis)
        forward = [(i, i + 1) for i in range(count - 1)]
        backward = [(target, source) for source, target in forward]
        low = lax.ppermute(
            lax.slice_in_dim(block, block.shape[dim] - width, None, axis=dim), axis, forward
        )
        high = lax.ppermute(lax.slice_in_dim(block, 0, width, axis=dim), axis, backward)
        block = jnp.concatenate([low, block, high], axis=dim)
    return block


def shifted(value, axis, steps):
    count = lax.axis_size(axis)
    first, last = (max(0, -steps), min(count, count - steps))
    return lax.ppermute(value, axis, [(source, source + steps) for source in range(first, last)])


def diagonals(products, window):
    leading = products.shape[:-2]
    block_width, wide_cols = (products.shape[-2], products.shape[-1])
    flattened = products.reshape(leading + (block_width * wide_cols,))
    flattened = jnp.concatenate(
        [flattened, jnp.zeros(leading + (block_width,), flattened.dtype)], axis=-1
    )
    return flattened.reshape(leading + (block_width, wide_cols + 1))[..., :window]


def undiagonals(planes, wide_cols):
    leading = planes.shape[:-2]
    block_width, window = (planes.shape[-2], planes.shape[-1])
    filler = jnp.zeros(leading + (block_width, wide_cols + 1 - window), planes.dtype)
    padded = jnp.concatenate([planes, filler], axis=-1)
    flattened = padded.reshape(leading + (block_width * (wide_cols + 1),))[
        ..., : block_width * wide_cols
    ]
    return flattened.reshape(leading + (block_width, wide_cols))


def widen(padded, col_count, block_width):
    row_total, channels = (padded.shape[0], padded.shape[2])
    block_count = col_count // block_width
    main_part = padded[:, :col_count].reshape(row_total, block_count, block_width, channels)
    tail_part = padded[:, block_width : block_width + col_count].reshape(
        row_total, block_count, block_width, channels
    )
    return jnp.concatenate([main_part, tail_part[:, :, : 2 * RADIUS]], axis=2)


def fold(wide_total, col_count, block_width):
    row_total, block_count, wide_cols, channels = wide_total.shape
    main_part = wide_total[:, :, :block_width].reshape(row_total, col_count, channels)
    tail_part = wide_total[:, :, block_width:]
    filler = jnp.zeros(
        (row_total, block_count, 2 * block_width - wide_cols, channels), wide_total.dtype
    )
    tail_part = jnp.concatenate([tail_part, filler], axis=2).reshape(row_total, col_count, channels)
    folded = jnp.zeros((row_total, col_count + block_width, channels), wide_total.dtype)
    folded = folded.at[:, :col_count].add(main_part)
    return folded.at[:, block_width:].add(tail_part)


def on_device(first_map, second_map, flow_target, valid_tiles, conv_weight, conv_bias, head_weight):
    row_count, col_count = (first_map.shape[0], first_map.shape[1])
    hidden_width = conv_weight.shape[2]
    window = 2 * RADIUS + 1
    block_width = math.gcd(col_count, 16)
    block_count = col_count // block_width
    wide_cols = block_width + 2 * RADIUS
    inverse_root = C ** (-0.5)
    second_rows = extended(second_map, (("region", 0),), RADIUS)
    second_pad = jnp.pad(second_rows, ((0, 0), (RADIUS, block_width - RADIUS), (0, 0)))
    second_wide = widen(second_pad, col_count, block_width)
    first_blocks = first_map.reshape(row_count, block_count, block_width, C)
    diagonal_list = []
    for vertical in range(window):
        products = jnp.einsum(
            "rnic,rnjc->rnij",
            first_blocks,
            second_wide[vertical : vertical + row_count],
            preferred_element_type=jnp.float32,
        )
        diagonal_list.append(diagonals(products, window))
    correlation = jnp.concatenate(diagonal_list, axis=3).reshape(row_count, col_count, K)
    correlation = (correlation * inverse_root).astype(jnp.bfloat16)
    correlation = jnp.transpose(correlation, (0, 2, 1))
    corr_rows = extended(correlation, (("region", 0),), 1)
    corr_pad = jnp.pad(corr_rows, ((0, 0), (0, 0), (1, 1)))
    preact = jnp.zeros((row_count, hidden_width, col_count), jnp.float32) + conv_bias[None, :, None]
    for offset in range(9):
        tap_row, tap_col = (offset // 3, offset % 3)
        window_corr = corr_pad[tap_row : tap_row + row_count, :, tap_col : tap_col + col_count]
        preact = preact + jnp.einsum(
            "kh,rkw->rhw", conv_weight[offset], window_corr, preferred_element_type=jnp.float32
        )
    hidden = jax.nn.silu(preact).astype(jnp.bfloat16)
    flow_pred = jnp.einsum("jh,rhw->jrw", head_weight, hidden, preferred_element_type=jnp.float32)
    tile_rows = jnp.repeat(valid_tiles, TILE, axis=0)
    own_start = lax.axis_index("region") * row_count
    own_tiles = lax.dynamic_slice_in_dim(tile_rows, own_start, row_count, 0)
    cell_mask = jnp.repeat(own_tiles, TILE, axis=1).astype(jnp.float32)
    flow_error = (cell_mask[None] * (flow_pred - flow_target)).astype(jnp.bfloat16)
    head_sum = jnp.einsum("jrw,rhw->jh", flow_error, hidden, preferred_element_type=jnp.float32)
    hidden_error = jnp.einsum(
        "jh,jrw->rhw", head_weight, flow_error, preferred_element_type=jnp.float32
    )
    sigmoid_pre = jax.nn.sigmoid(preact)
    preact_error = (hidden_error * sigmoid_pre * (1.0 + preact * (1.0 - sigmoid_pre))).astype(
        jnp.bfloat16
    )
    bias_sum = jnp.sum(preact_error.astype(jnp.float32), axis=(0, 2))
    error_rows = extended(preact_error, (("region", 0),), 1)
    error_pad = jnp.pad(error_rows, ((0, 0), (0, 0), (1, 1)))
    conv_list = []
    corr_error = jnp.zeros((row_count, K, col_count), jnp.float32)
    for offset in range(9):
        tap_row, tap_col = (offset // 3, offset % 3)
        window_corr = corr_pad[tap_row : tap_row + row_count, :, tap_col : tap_col + col_count]
        conv_list.append(
            jnp.einsum("rkw,rhw->kh", window_corr, preact_error, preferred_element_type=jnp.float32)
        )
        window_error = error_pad[
            2 - tap_row : 2 - tap_row + row_count, :, 2 - tap_col : 2 - tap_col + col_count
        ]
        corr_error = corr_error + jnp.einsum(
            "kh,rhw->rkw", conv_weight[offset], window_error, preferred_element_type=jnp.float32
        )
    conv_sum = jnp.stack(conv_list, axis=0)
    corr_error = (corr_error * inverse_root).astype(jnp.bfloat16)
    error_planes = jnp.transpose(corr_error, (0, 2, 1))
    error_blocks = error_planes.reshape(row_count, block_count, block_width, K)
    first_total = jnp.zeros((row_count, block_count, block_width, C), jnp.float32)
    for vertical in range(window):
        spread = undiagonals(
            error_blocks[..., vertical * window : (vertical + 1) * window], wide_cols
        )
        first_total = first_total + jnp.einsum(
            "rnij,rnjc->rnic",
            spread,
            second_wide[vertical : vertical + row_count],
            preferred_element_type=jnp.float32,
        )
    first_total = first_total.reshape(row_count, col_count, C)
    second_total = jnp.zeros((row_count + 2 * RADIUS, block_count, wide_cols, C), jnp.float32)
    for vertical in range(window):
        spread = undiagonals(
            error_blocks[..., vertical * window : (vertical + 1) * window], wide_cols
        )
        second_total = second_total.at[vertical : vertical + row_count].add(
            jnp.einsum("rnij,rnic->rnjc", spread, first_blocks, preferred_element_type=jnp.float32)
        )
    second_fold = fold(second_total, col_count, block_width)
    upper_rim = second_fold[:RADIUS, RADIUS : RADIUS + col_count]
    lower_rim = second_fold[row_count + RADIUS :, RADIUS : RADIUS + col_count]
    own_rows = second_fold[RADIUS : RADIUS + row_count, RADIUS : RADIUS + col_count]
    from_below = shifted(upper_rim, "region", -1)
    from_above = shifted(lower_rim, "region", 1)
    own_rows = own_rows.at[row_count - RADIUS :].add(from_below)
    own_rows = own_rows.at[:RADIUS].add(from_above)
    param_count = 9 * K * hidden_width + 3 * hidden_width
    clip_limit = clip_fraction * param_count**0.5
    totals = lax.psum((conv_sum, bias_sum, head_sum), "region")
    squares_all = (
        jnp.sum(totals[0] * totals[0])
        + jnp.sum(totals[1] * totals[1])
        + jnp.sum(totals[2] * totals[2])
    )
    share_size = hidden_width // lax.axis_size("region")
    first_hid = lax.axis_index("region") * share_size
    conv_piece = lax.dynamic_slice_in_dim(totals[0], first_hid, share_size, 2)
    bias_piece = lax.dynamic_slice_in_dim(totals[1], first_hid, share_size, 0)
    head_piece = lax.dynamic_slice_in_dim(totals[2], first_hid, share_size, 1)
    clip_factor = jnp.minimum(1.0, clip_limit / jnp.sqrt(squares_all + 1e-06))
    return (
        first_total.astype(jnp.bfloat16),
        own_rows.astype(jnp.bfloat16),
        conv_piece * clip_factor,
        bias_piece * clip_factor,
        head_piece * clip_factor,
    )


def solution(mesh):
    return jax.shard_map(
        on_device,
        mesh=mesh,
        in_specs=(
            P("region", "group", None),
            P("region", "group", None),
            P(None, "region", "group"),
            P(None, "group"),
            P(),
            P(),
            P(),
        ),
        out_specs=(
            P("region", "group", None),
            P("region", "group", None),
            P("group", None, "region"),
            P(("group", "region")),
            P("group", "region"),
        ),
        check_vma=False,
    )
```

profile of v0, /device:TPU:0, one launch (start us, length us, event | category | flops | bytes accessed | tf_op | source)
XLA Modules:
  0.0 245.5 jit_solution(7116153970787172597)
XLA Ops:
  7.2 2.5 %collective-permute-start = (bf16[4,256,256]{2,1,0:T(8,128)(2,1)}, bf16[4,256,256]{2,1,0:T(8,128)(2,1)S(1)}, u32[]{:S(2)}, u32[]{:S(2)}) collective-permute-start(bf16[4,256,256]{2,1,0:T(8,128)(2,1)} %param.38), channel_id=1, source_target_pairs={{0,1},{1,2},{2,3},{3,4},{4,5},{5,6},{6,7},{7,8},{8,9},{9,10},{10,1... | collective-permute-start | bytes 1572872 | tf_op jit(solution)/shard_map/ppermute | solution.py:22
  11.5 4.4 %collective-permute-done.1 = bf16[4,256,256]{2,1,0:T(8,128)(2,1)S(1)} collective-permute-done((bf16[4,256,256]{2,1,0:T(8,128)(2,1)}, bf16[4,256,256]{2,1,0:T(8,128)(2,1)S(1)}, u32[]{:S(2)}, u32[]{:S(2)}) %collective-permute-start.1) | collective-permute-done | bytes 524320 | tf_op jit(solution)/shard_map/ppermute | solution.py:25
  29.1 1.9 reshape.608
  33.0 1.9 reshape.606
  37.0 1.9 reshape.604
  40.9 1.9 reshape.602
  44.9 1.9 reshape.600
  48.8 1.9 reshape.598
  52.8 1.9 reshape.596
  56.7 1.9 reshape.612
  60.7 4.5 %concatenate.130 = f32[4,16,16,81]{3,2,1,0:T(8,128)} concatenate(f32[4,16,16,9]{3,2,1,0:T(8,128)} %bitcast.308, f32[4,16,16,9]{3,2,1,0:T(8,128)} %bitcast.307, f32[4,16,16,9]{3,2,1,0:T(8,128)} %bitcast.306, f32[4,16,16,9]{3,2,1,0:T(8,128)} %bitcast.305, f32[4,16,16,9]{3,2,1,0:T(8,128)} %bitcast.304, f32[4,16,16,9]{3,2,1,0:T(8,128)} %bitcast.303, f32[4,16,16,9]{3,2,1,0:T(8,128)} %bitcast.302, ...), dimensions={3} | concatenate | bytes 663552 | tf_op jit(solution)/shard_map/concatenate | solution.py:101
  67.1 10.4 %collective-permute-start.2 = (bf16[1,81,256]{2,1,0:T(8,128)(2,1)}, bf16[1,81,256]{2,1,0:T(8,128)(2,1)S(1)}, u32[]{:S(2)}, u32[]{:S(2)}) collective-permute-start(bf16[1,81,256]{2,1,0:T(8,128)(2,1)} %get-tuple-element.203), channel_id=1, source_target_pairs={{0,1},{1,2},{2,3},{3,4},{4,5},{5,6},{6,7},{7,8},{8,9},{9,10},{10,1... | collective-permute-start | bytes 124424 | tf_op jit(solution)/shard_map/ppermute | solution.py:22
  79.2 3.6 %collective-permute-done.3 = bf16[1,81,256]{2,1,0:T(8,128)(2,1)} collective-permute-done((bf16[1,81,256]{2,1,0:T(8,128)(2,1)}, bf16[1,81,256]{2,1,0:T(8,128)(2,1)}, u32[]{:S(2)}, u32[]{:S(2)}) %collective-permute-start.3) | collective-permute-done | bytes 41504 | tf_op jit(solution)/shard_map/ppermute | solution.py:25
  92.5 4.6 %collective-permute-start.4 = (bf16[1,256,256]{1,2,0:T(8,128)(2,1)}, bf16[1,256,256]{1,2,0:T(8,128)(2,1)S(1)}, u32[]{:S(2)}, u32[]{:S(2)}) collective-permute-start(bf16[1,256,256]{1,2,0:T(8,128)(2,1)} %get-tuple-element.193), channel_id=1, source_target_pairs={{0,1},{1,2},{2,3},{3,4},{4,5},{5,6},{6,7},{7,8},{8,9},{9,10},{10,1... | collective-permute-start | bytes 393224 | tf_op jit(solution)/shard_map/ppermute | solution.py:22
  106.3 32.8 %all-reduce.23 = (f32[256]{0:T(256)S(1)}, f32[2,256]{1,0:T(2,128)S(1)}) all-reduce(f32[256]{0:T(256)S(1)} %get-tuple-element.207, f32[2,256]{1,0:T(2,128)S(1)} %convolution_bitcast_fusion.20), channel_id=1, replica_groups=mesh['group'=2,'region'=16] {'region'}, use_global_device_ids=true, to_apply=%region_3.4 | all-reduce | flops 768 | bytes 6144 | tf_op jit(solution)/shard_map/psum | solution.py:179
  151.2 1.7 fusion.156
  163.9 1.7 concatenate.141
  174.8 1.7 concatenate.138
  178.3 1.8 reshape.618
  181.3 1.9 scatter-add.36
  197.1 4.0 %collective-permute-start.7 = (f32[4,256,256]{2,1,0:T(8,128)}, f32[4,256,256]{2,1,0:T(8,128)}, u32[]{:S(2)}, u32[]{:S(2)}) collective-permute-start(f32[4,256,256]{2,1,0:T(8,128)} %get-tuple-element.190), channel_id=1, source_target_pairs={{0,1},{1,2},{2,3},{3,4},{4,5},{5,6},{6,7},{7,8},{8,9},{9,10},{10,1... | collective-permute-start | bytes 3145736 | tf_op jit(solution)/shard_map/ppermute | solution.py:33
  202.9 25.8 %all-reduce.26.cloned.1.call-done = f32[9,81,256]{2,1,0:T(8,128)} async-done(((f32[9,81,256]{2,1,0:T(8,128)}), f32[9,81,256]{2,1,0:T(8,128)}) %all-reduce.26.cloned.1.call-update) | async-done | bytes 746512 | tf_op jit(solution)/shard_map/psum | solution.py:179
  228.7 2.0 multiply_reduce_fusion
  235.8 2.9 %fusion.36 = bf16[4,256,256]{2,1,0:T(8,128)(2,1)} fusion(f32[4,256,256]{2,1,0:T(8,128)} %collective-permute-done.7, f32[4,256,256]{2,1,0:T(8,128)} %collective-permute-done.6, f32[12,272,256]{2,1,0:T(8,128)} %copy-done.1), kind=kLoop, calls=%fused_computation.113 | loop fusion | flops 786432 | bytes 3670016 | tf_op jit(solution)/shard_map/convert_element_type | solution.py:193
  (187 shorter events, 107.1 us)
Async XLA Ops:
  7.2 10.5 %copy-start = (bf16[4,256,256]{2,1,0:T(8,128)(2,1)S(1)}, bf16[4,256,256]{2,1,0:T(8,128)(2,1)}, u32[]{:S(2)}) copy-start(bf16[4,256,256]{2,1,0:T(8,128)(2,1)} %param.37) | copy-start | bytes 1572868
  7.2 221.5 %all-reduce.26.cloned.1.call-start = ((), (), s32[]{:S(2)}) async-start(), calls=%async_computation | async-start | bytes 1622016 | tf_op jit(solution)/shard_map/psum | solution.py:179
  7.2 4.2 %collective-permute-start = (bf16[4,256,256]{2,1,0:T(8,128)(2,1)}, bf16[4,256,256]{2,1,0:T(8,128)(2,1)S(1)}, u32[]{:S(2)}, u32[]{:S(2)}) collective-permute-start(bf16[4,256,256]{2,1,0:T(8,128)(2,1)} %param.38), channel_id=1, source_target_pairs={{0,1},{1,2},{2,3},{3,4},{4,5},{5,6},{6,7},{7,8},{8,9},{9,10},{10,1... | collective-permute-start | bytes 1572872 | tf_op jit(solution)/shard_map/ppermute | solution.py:22
  9.8 6.1 %collective-permute-start.1 = (bf16[4,256,256]{2,1,0:T(8,128)(2,1)}, bf16[4,256,256]{2,1,0:T(8,128)(2,1)S(1)}, u32[]{:S(2)}, u32[]{:S(2)}) collective-permute-start(bf16[4,256,256]{2,1,0:T(8,128)(2,1)} %param.38), channel_id=1, source_target_pairs={{1,0},{2,1},{3,2},{4,3},{5,4},{6,5},{7,6},{8,7},{9,8},{10,9},{11,1... | collective-permute-start | bytes 1572872 | tf_op jit(solution)/shard_map/ppermute | solution.py:25
  60.7 18.3 %copy-start.16 = (s32[4,16]{1,0:T(4,128)S(1)}, s32[4,16]{1,0:T(4,128)}, u32[]{:S(2)}) copy-start(s32[4,16]{1,0:T(4,128)} %param.40) | copy-start | bytes 772
  66.4 22.1 %copy-start.2 = (bf16[4,256,81]{1,2,0:T(8,128)(2,1)}, bf16[4,256,81]{1,2,0:T(8,128)(2,1)S(1)}, u32[]{:S(2)}) copy-start(bf16[4,256,81]{1,2,0:T(8,128)(2,1)S(1)} %copy.43) | copy-start | bytes 497668
  66.4 19.8 %copy-start.11 = (bf16[9,81,256]{2,1,0:T(8,128)(2,1)S(1)}, bf16[9,81,256]{2,1,0:T(8,128)(2,1)}, u32[]{:S(2)}) copy-start(bf16[9,81,256]{2,1,0:T(8,128)(2,1)} %param.41) | copy-start | bytes 1119748
  66.4 20.2 %copy-start.18 = (f32[256]{0:T(256)S(1)}, f32[256]{0:T(256)}, u32[]{:S(2)}) copy-start(f32[256]{0:T(256)} %param.42) | copy-start | bytes 3076
  67.1 12.1 %collective-permute-start.2 = (bf16[1,81,256]{2,1,0:T(8,128)(2,1)}, bf16[1,81,256]{2,1,0:T(8,128)(2,1)S(1)}, u32[]{:S(2)}, u32[]{:S(2)}) collective-permute-start(bf16[1,81,256]{2,1,0:T(8,128)(2,1)} %get-tuple-element.203), channel_id=1, source_target_pairs={{0,1},{1,2},{2,3},{3,4},{4,5},{5,6},{6,7},{7,8},{8,9},{9,10},{10,1... | collective-permute-start | bytes 124424 | tf_op jit(solution)/shard_map/ppermute | solution.py:22
  77.5 5.3 %collective-permute-start.3 = (bf16[1,81,256]{2,1,0:T(8,128)(2,1)}, bf16[1,81,256]{2,1,0:T(8,128)(2,1)}, u32[]{:S(2)}, u32[]{:S(2)}) collective-permute-start(bf16[1,81,256]{2,1,0:T(8,128)(2,1)} %get-tuple-element.204), channel_id=1, source_target_pairs={{1,0},{2,1},{3,2},{4,3},{5,4},{6,5},{7,6},{8,7},{9,8},{10,9},{11,1... | collective-permute-start | bytes 124424 | tf_op jit(solution)/shard_map/ppermute | solution.py:25
  79.2 7.8 %copy-start.13 = (bf16[1,81,256]{2,1,0:T(8,128)(2,1)}, bf16[1,81,256]{2,1,0:T(8,128)(2,1)S(1)}, u32[]{:S(2)}) copy-start(bf16[1,81,256]{2,1,0:T(8,128)(2,1)S(1)} %collective-permute-done.2) | copy-start | bytes 124420
  88.5 1.4 copy-start.15
  88.5 1.4 copy-start.17
  90.3 8.1 %copy-start.3 = (bf16[4,256,81]{1,2,0:T(8,128)(2,1)S(1)}, bf16[4,256,81]{1,2,0:T(8,128)(2,1)}, u32[]{:S(2)}) copy-start(bf16[4,256,81]{1,2,0:T(8,128)(2,1)} %copy-done.2) | copy-start | bytes 497668
  90.4 8.1 %copy-start.14 = (bf16[1,81,256]{2,1,0:T(8,128)(2,1)S(1)}, bf16[1,81,256]{2,1,0:T(8,128)(2,1)}, u32[]{:S(2)}) copy-start(bf16[1,81,256]{2,1,0:T(8,128)(2,1)} %copy-done.13) | copy-start | bytes 124420
  92.5 47.8 %collective-permute-start.4 = (bf16[1,256,256]{1,2,0:T(8,128)(2,1)}, bf16[1,256,256]{1,2,0:T(8,128)(2,1)S(1)}, u32[]{:S(2)}, u32[]{:S(2)}) collective-permute-start(bf16[1,256,256]{1,2,0:T(8,128)(2,1)} %get-tuple-element.193), channel_id=1, source_target_pairs={{0,1},{1,2},{2,3},{3,4},{4,5},{5,6},{6,7},{7,8},{8,9},{9,10},{10,1... | collective-permute-start | bytes 393224 | tf_op jit(solution)/shard_map/ppermute | solution.py:22
  97.2 43.2 %collective-permute-start.5 = (bf16[1,256,256]{1,2,0:T(8,128)(2,1)}, bf16[1,256,256]{1,2,0:T(8,128)(2,1)}, u32[]{:S(2)}, u32[]{:S(2)}) collective-permute-start(bf16[1,256,256]{1,2,0:T(8,128)(2,1)} %get-tuple-element.194), channel_id=1, source_target_pairs={{1,0},{2,1},{3,2},{4,3},{5,4},{6,5},{7,6},{8,7},{9,8},{10,9},{11,1... | collective-permute-start | bytes 393224 | tf_op jit(solution)/shard_map/ppermute | solution.py:25
  139.7 2.8 %copy-start.12 = (bf16[9,81,256]{2,1,0:T(8,128)(2,1)S(1)}, bf16[9,81,256]{2,1,0:T(8,128)(2,1)}, u32[]{:S(2)}) copy-start(bf16[9,81,256]{2,1,0:T(8,128)(2,1)} %param.41) | copy-start | bytes 1119748
  144.9 2.7 %copy-start.19 = (pred[25]{0:T(512)(128)(4,1)S(1)}, pred[25]{0:T(512)(128)(4,1)}, u32[]{:S(2)}) copy-start(pred[25]{0:T(512)(128)(4,1)} %constant.382.clone.1) | copy-start | bytes 79
  181.3 1.9 copy-start.9
  190.0 1.2 copy-start.4
  194.1 7.3 %copy-start.1 = (f32[12,272,256]{2,1,0:T(8,128)}, f32[12,272,256]{2,1,0:T(8,128)S(1)}, u32[]{:S(2)}) copy-start(f32[12,272,256]{2,1,0:T(8,128)S(1)} %constant_dynamic-update-slice_fusion) | copy-start | bytes 10027012
  195.8 39.9 %collective-permute-start.6 = (f32[4,256,256]{2,1,0:T(8,128)}, f32[4,256,256]{2,1,0:T(8,128)}, u32[]{:S(2)}, u32[]{:S(2)}) collective-permute-start(f32[4,256,256]{2,1,0:T(8,128)} %get-tuple-element.189), channel_id=1, source_target_pairs={{1,0},{2,1},{3,2},{4,3},{5,4},{6,5},{7,6},{8,7},{9,8},{10,9},{11,1... | collective-permute-start | bytes 3145736 | tf_op jit(solution)/shard_map/ppermute | solution.py:33
  197.1 38.7 %collective-permute-start.7 = (f32[4,256,256]{2,1,0:T(8,128)}, f32[4,256,256]{2,1,0:T(8,128)}, u32[]{:S(2)}, u32[]{:S(2)}) collective-permute-start(f32[4,256,256]{2,1,0:T(8,128)} %get-tuple-element.190), channel_id=1, source_target_pairs={{0,1},{1,2},{2,3},{3,4},{4,5},{5,6},{6,7},{7,8},{8,9},{9,10},{10,1... | collective-permute-start | bytes 3145736 | tf_op jit(solution)/shard_map/ppermute | solution.py:33
  (5 other events, 4.8 us)
Sparse Core Ops, SparseCore 0:
  139.8 88.8 all-reduce.25
where the time goes:
time: 248 us; the launch traced here: 246 us
  local copies, waits for them, and re-layouts  80.4 us (32%)
  matrix products  40.8 us (16%)
  waiting for transfers between devices  34.3 us (14%)
  blocking collectives  32.8 us (13%)
  starting transfers between devices  27 us (11%)
  between operations  16.7 us (7%)
  other arithmetic  13.6 us (5%)
    psum x1, blocking collectives, on_device(): totals = lax.psum((conv_sum, bias_sum, head_sum), 'region')  32.8 us
    psum x1, waiting for transfers between devices, on_device(): totals = lax.psum((conv_sum, bias_sum, head_sum), 'region')  25.8 us
    ppermute x3, starting transfers between devices, extended(): lax.ppermute(lax.slice_in_dim(block, block.shape[dim] - width, None, axis...  17.6 us
    reshape x9, local copies, waits for them, and re-layouts, diagonals(): flattened = products.reshape(leading + (block_width * wide_cols,))  16.1 us
    concatenate x8, local copies, waits for them, and re-layouts, undiagonals(): padded = jnp.concatenate([planes, filler], axis=-1)  11 us
    reshape x9, local copies, waits for them, and re-layouts, diagonals(): flattened.reshape(leading + (block_width, wide_cols + 1))[..., :window]  9.48 us
    dot_general x9, matrix products, on_device(): jnp.einsum('rnic,rnjc->rnij', first_blocks, second_wide[vertical:vertical...  9.32 us
    reshape x9, local copies, waits for them, and re-layouts, undiagonals(): padded.reshape(leading + (block_width * (wide_cols + 1),))  9.02 us
  transfers between devices with their start and end apart: 9, of which 4 were waited for; matrix products, arithmetic and copies ran while one was open for 28% of the time, Pallas kernels for 0%

commit v1 on v0

v1 whole, which is shorter than its diff:
```python
import functools

import jax
import jax.numpy as jnp
from jax import lax
from jax.experimental import pallas as pl
from jax.experimental.pallas import tpu as pltpu
from jax.sharding import PartitionSpec as P

C = 256
RADIUS = 4
TILE = 16
K = 81
WIN = 9
LANES = 128

clip_fraction = 0.25

f32 = jnp.float32
bf16 = jnp.bfloat16

NT = (((1,), (1,)), ((), ()))
TN = (((0,), (0,)), ((), ()))


def dot(a, b, dims=None):
    if dims is None:
        return jnp.dot(a, b, preferred_element_type=f32)
    return lax.dot_general(a, b, dims, preferred_element_type=f32)


def iota(shape, dim):
    return lax.broadcasted_iota(jnp.int32, shape, dim)


def full(shape):
    return pl.BlockSpec(shape, lambda *_: (0,) * len(shape))


SMEM = pl.BlockSpec(memory_space=pltpu.SMEM)


def call(body, outs, args, scratch=(), specs=None):
    specs = specs or [full(a.shape) for a in args]
    return pl.pallas_call(
        body,
        out_shape=[jax.ShapeDtypeStruct(s, d) for s, d in outs],
        in_specs=specs,
        out_specs=[full(s) for s, _ in outs],
        scratch_shapes=list(scratch),
    )(*args)


def band_of(products, dyi):
    band = pltpu.roll(products, 8, 1, stride=1, stride_axis=0)[:, :LANES]
    return pltpu.roll(band, (9 * dyi - 3) % LANES, 1)


def spread_of(bands, dyi, cols):
    moved = pltpu.roll(bands, (4 - 9 * dyi) % LANES, 1)
    lane = iota(bands.shape, 1)
    own = jnp.where((lane >= 4) & (lane < 13), moved, 0.0)
    wide = jnp.concatenate([own, jnp.zeros((bands.shape[0], cols - LANES), own.dtype)], axis=1)
    return pltpu.roll(wide, cols - 8, 1, stride=1, stride_axis=0).astype(bf16)


def lane_valid(rows):
    lane = iota((rows, LANES), 1)
    col = iota((rows, LANES), 0) + lane % WIN - RADIUS
    return (col >= 0) & (col < rows) & (lane < K)


def corr_body(par_ref, first_ref, own_ref, low_ref, high_ref, corr_ref, ea_ref, eb_ref):
    rows, cols = first_ref.shape[0], first_ref.shape[1]
    par = par_ref[0]
    valid = lane_valid(cols)
    lane = iota((cols, LANES), 1)
    mirror = (iota((cols, cols), 0) + iota((cols, cols), 1) == cols - 1).astype(bf16)
    for r in range(rows):
        acc = jnp.zeros((cols, LANES), f32)
        turned = dot(mirror, first_ref[r]).astype(bf16)
        for dyi in range(WIN):
            q = r + dyi - RADIUS
            src = low_ref[q + RADIUS] if q < 0 else (high_ref[q - rows] if q >= rows else own_ref[q])
            band = band_of(dot(turned, src, NT), dyi)
            acc = jnp.where((lane >= 9 * dyi) & (lane < 9 * dyi + 9), band, acc)
        acc = dot(mirror, (acc * (C ** -0.5)).astype(bf16))
        acc = jnp.where(valid, acc, 0.0)
        acc = jnp.where(lane == K, 1.0, acc)
        corr_ref[r] = acc.astype(bf16)
    ea_ref[...] = corr_ref[(1 - par) * (rows - 1)]
    eb_ref[...] = corr_ref[par * (rows - 1)]


def shift_down(x, steps):
    zero = jnp.zeros((abs(steps), x.shape[1]), x.dtype)
    if steps > 0:
        return jnp.concatenate([zero, x[:-steps]], axis=0)
    return jnp.concatenate([x[-steps:], zero], axis=0)


def conv_body(par_ref, corr_ref, ha_ref, hb_ref, w_ref, bias_ref, head_ref, target_ref, mask_ref,
              pe_ref, pa_ref, pb_ref, sums_ref, x_ref, pt_ref):
    rows, cols = corr_ref.shape[0], corr_ref.shape[1]
    hid = w_ref.shape[2]
    par = par_ref[0]

    def put(slot, value):
        wide = value.astype(f32)
        x_ref[slot, :, 0:LANES] = shift_down(wide, 1).astype(bf16)
        x_ref[slot, :, LANES:2 * LANES] = value
        x_ref[slot, :, 2 * LANES:] = shift_down(wide, -1).astype(bf16)

    for r in range(rows):
        put(r + 1, corr_ref[r])
    put((1 - par) * (rows + 1), ha_ref[...])
    put(par * (rows + 1), hb_ref[...])
    head = head_ref[...]
    head_sum = jnp.zeros((head.shape[0], hid), f32)
    for r in range(rows):
        pre = bias_ref[...] + (dot(x_ref[r], w_ref[0]) + dot(x_ref[r + 1], w_ref[1]) + dot(x_ref[r + 2], w_ref[2]))
        sig = lax.logistic(pre)
        hidden = (pre * sig).astype(bf16)
        pred = dot(head, hidden, NT)
        err = mask_ref[pl.ds(r, 1), :] * (pred[0:2] - target_ref[:, r, :])
        err = jnp.concatenate([err, jnp.zeros((head.shape[0] - 2, cols), f32)], axis=0).astype(bf16)
        head_sum = head_sum + dot(err, hidden)
        herr = dot(err, head, TN)
        pe = (herr * sig * (1.0 + pre * (1.0 - sig))).astype(bf16)
        pe_ref[r] = pe
        pt_ref[:, r * cols:(r + 1) * cols] = pe.astype(f32).T.astype(bf16)
    pa_ref[...] = pe_ref[(1 - par) * (rows - 1)]
    pb_ref[...] = pe_ref[par * (rows - 1)]
    pieces = []
    bias_col = None
    for ty in range(3):
        x = x_ref[ty:ty + rows].reshape(rows * cols, 3 * LANES)
        part = dot(pt_ref[...], x)
        for tx in range(3):
            pieces.append(part[:, tx * LANES:tx * LANES + K])
        if ty == 1:
            bias_col = part[:, LANES + K:LANES + K + 1]
    head_cols = jnp.concatenate([head_sum, jnp.zeros((LANES - head.shape[0], hid), f32)], axis=0).T
    used = 9 * K + 3
    pad = jnp.zeros((hid, sums_ref.shape[1] - used), f32)
    sums_ref[...] = jnp.concatenate(pieces + [bias_col, head_cols[:, 0:2], pad], axis=1)


def cerr_body(par_ref, pe_ref, ha_ref, hb_ref, w_ref, ce_ref, ea_ref, eb_ref, ext_ref):
    rows, cols = pe_ref.shape[0], pe_ref.shape[1]
    par = par_ref[0]
    for r in range(rows):
        ext_ref[r + 1] = pe_ref[r]
    ext_ref[(1 - par) * (rows + 1)] = ha_ref[...]
    ext_ref[par * (rows + 1)] = hb_ref[...]
    valid = lane_valid(cols)
    lane = iota((cols, LANES), 1)
    to_low = jnp.zeros((cols, LANES), f32)
    to_high = jnp.zeros((cols, LANES), f32)
    low_at = high_at = 0
    for r in range(rows):
        z = dot(ext_ref[r + 2], w_ref[0], NT) + dot(ext_ref[r + 1], w_ref[1], NT) + dot(ext_ref[r], w_ref[2], NT)
        total = shift_down(z[:, 0:LANES], -1) + z[:, LANES:2 * LANES] + shift_down(z[:, 2 * LANES:], 1)
        total = jnp.where(valid, total * (C ** -0.5), 0.0)
        ce_ref[r] = total.astype(bf16)
        count = 9 * (RADIUS - r)
        moved = pltpu.roll(total, low_at, 1) if low_at else total
        to_low = jnp.where((lane >= low_at) & (lane < low_at + count), moved, to_low)
        low_at += count
        count = 9 * (r + 1 + RADIUS - rows)
        start = K - count
        moved = pltpu.roll(total, (high_at - start) % LANES, 1)
        to_high = jnp.where((lane >= high_at) & (lane < high_at + count), moved, to_high)
        high_at += count
    up = to_low.astype(bf16)
    down = to_high.astype(bf16)

    @pl.when(par == 0)
    def _():
        ea_ref[...] = down
        eb_ref[...] = up

    @pl.when(par != 0)
    def _():
        ea_ref[...] = up
        eb_ref[...] = down


def own_grad_body(ce_ref, first_ref, second_ref, low_ref, high_ref, fg_ref, part_ref):
    rows, cols = ce_ref.shape[0], ce_ref.shape[1]
    parts = [jnp.zeros((cols, C), f32) for _ in range(rows)]
    for r in range(rows):
        bands = ce_ref[r].astype(f32)
        acc = jnp.zeros((cols, C), f32)
        for dyi in range(WIN):
            q = r + dyi - RADIUS
            src = low_ref[q + RADIUS] if q < 0 else (high_ref[q - rows] if q >= rows else second_ref[q])
            spread = spread_of(bands, dyi, cols)
            acc = acc + dot(spread, src)
            if 0 <= q < rows:
                parts[q] = parts[q] + dot(spread, first_ref[r], TN)
        fg_ref[r] = acc.astype(bf16)
    for r in range(rows):
        part_ref[r] = parts[r]


def halo_grad_body(par_ref, part_ref, ca_ref, cb_ref, low_ref, high_ref, sg_ref, c_ref):
    rows, cols = part_ref.shape[0], part_ref.shape[1]
    par = par_ref[0]
    c_ref[1 - par] = ca_ref[...].astype(f32)
    c_ref[par] = cb_ref[...].astype(f32)
    parts = [part_ref[r] for r in range(rows)]
    above = c_ref[0]
    below = c_ref[1]
    at = 0
    for a in range(rows):
        for i, dy in enumerate(range(rows - a, RADIUS + 1)):
            spread = spread_of(above, at // 9 + i, cols)
            q = a + dy - rows
            parts[q] = parts[q] + dot(spread, low_ref[a], TN)
        at += 9 * (RADIUS + 1 - rows + a)
    at = 0
    for b in range(rows):
        for i, dy in enumerate(range(-RADIUS, -b)):
            spread = spread_of(below, at // 9 + i, cols)
            q = rows + b + dy
            parts[q] = parts[q] + dot(spread, high_ref[b], TN)
        at += 9 * (RADIUS - b)
    for r in range(rows):
        sg_ref[r] = parts[r].astype(bf16)


def final_body(sq_ref, piece_ref, conv_ref, bias_ref, head_ref, *, limit):
    factor = jnp.minimum(1.0, limit / jnp.sqrt(sq_ref[0:1, 0:1] + 1e-06))
    piece = piece_ref[...] * factor
    share = conv_ref.shape[2]
    height = -(-piece.shape[0] // LANES) * LANES
    if height != piece.shape[0]:
        piece = jnp.concatenate([piece, jnp.zeros((height - piece.shape[0], piece.shape[1]), f32)], axis=0)
    turned = piece.T
    for tap in range(9):
        conv_ref[tap] = turned[tap * K:(tap + 1) * K, 0:share]
    bias_ref[...] = turned[9 * K:9 * K + 1, 0:share]
    head_ref[...] = turned[9 * K + 1:9 * K + 3, 0:share]


def square_body(piece_ref, out_ref):
    piece = piece_ref[...]
    out_ref[...] = jnp.broadcast_to(jnp.sum(piece * piece).reshape(1, 1), out_ref.shape)


def on_device(first_map, second_map, flow_target, valid_tiles, conv_weight, conv_bias, head_weight):
    rows, cols = first_map.shape[0], first_map.shape[1]
    hid = conv_weight.shape[2]
    count = lax.axis_size("region")
    index = lax.axis_index("region")
    par = (index % 2).reshape(1)
    forward = [(i, i + 1) for i in range(count - 1)]
    backward = [(b, a) for a, b in forward]
    inner = [(i, i ^ 1) for i in range(count)]
    outer = [(i, i + 1) for i in range(1, count - 1, 2)]
    outer = outer + [(b, a) for a, b in outer]

    def permute(x, pairs):
        return lax.ppermute(x, "region", pairs)

    second_low = permute(second_map, forward)
    second_high = permute(second_map, backward)

    share = hid // count
    radix = [2] * (count.bit_length() - 1)
    turn = tuple(reversed(range(len(radix)))) + (len(radix),)

    def reorder(x):
        return jnp.transpose(x.reshape(tuple(radix) + (share,)), turn).reshape(hid)

    order = reorder(jnp.arange(hid))
    select = (jnp.arange(hid)[:, None] == order[None, :]).astype(bf16)
    weight = jnp.einsum("tkh,hg->tkg", conv_weight, select, preferred_element_type=bf16)
    weight = jnp.pad(weight, ((0, 0), (0, LANES - K), (0, 0))).reshape(3, 3 * LANES, hid)
    head = jnp.einsum("jh,hg->jg", head_weight, select, preferred_element_type=bf16)
    head = jnp.pad(head, ((0, 14), (0, 0)))
    bias = reorder(conv_bias).reshape(1, hid)
    tile_rows = jnp.repeat(valid_tiles, TILE, axis=0)
    own_tiles = lax.dynamic_slice_in_dim(tile_rows, index * rows, rows, 0)
    mask = jnp.repeat(own_tiles, TILE, axis=1).astype(f32)

    vector = lambda *s: pltpu.VMEM(s, bf16)
    corr, edge_a, edge_b = call(
        corr_body,
        [((rows, cols, LANES), bf16), ((cols, LANES), bf16), ((cols, LANES), bf16)],
        (par, first_map, second_map, second_low, second_high),
        specs=[SMEM, full(first_map.shape)] + [full(second_map.shape), full(second_low.shape), full(second_high.shape)],
    )
    halo_a = permute(edge_a, inner)
    halo_b = permute(edge_b, outer)
    args = (par, corr, halo_a, halo_b, weight, bias, head, flow_target, mask)
    pe, pe_a, pe_b, sums = call(
        conv_body,
        [((rows, cols, hid), bf16), ((cols, hid), bf16), ((cols, hid), bf16), ((hid, 768), f32)],
        args,
        scratch=[vector(rows + 2, cols, 3 * LANES), vector(hid, rows * cols)],
        specs=[SMEM] + [full(a.shape) for a in args[1:]],
    )
    pe_halo_a = permute(pe_a, inner)
    pe_halo_b = permute(pe_b, outer)

    piece = sums
    early = None
    for step in range(len(radix)):
        half = piece.shape[0] // 2
        bit = (index >> step) & 1
        halves = piece.reshape(2, half, piece.shape[1])
        keep = lax.dynamic_index_in_dim(halves, bit, 0, False)
        send = lax.dynamic_index_in_dim(halves, 1 - bit, 0, False)
        piece = keep + permute(send, [(i, i ^ (1 << step)) for i in range(count)])
        if step == 1:
            early = piece

    first_tied, _ = lax.optimization_barrier((first_map, early))
    first_low = permute(first_tied, forward)
    first_high = permute(first_tied, backward)

    args = (par, pe, pe_halo_a, pe_halo_b, weight)
    cerr, ce_a, ce_b = call(
        cerr_body,
        [((rows, cols, LANES), bf16), ((cols, LANES), bf16), ((cols, LANES), bf16)],
        args,
        scratch=[vector(rows + 2, cols, hid)],
        specs=[SMEM] + [full(a.shape) for a in args[1:]],
    )
    ce_halo_a = permute(ce_a, inner)
    ce_halo_b = permute(ce_b, outer)
    first_grad, part = call(
        own_grad_body,
        [((rows, cols, C), bf16), ((rows, cols, C), f32)],
        (cerr, first_map, second_map, second_low, second_high),
    )
    args = (par, part, ce_halo_a, ce_halo_b, first_low, first_high)
    (second_grad,) = call(
        halo_grad_body,
        [((rows, cols, C), bf16)],
        args,
        scratch=[pltpu.VMEM((2, cols, LANES), f32)],
        specs=[SMEM] + [full(a.shape) for a in args[1:]],
    )

    (square,) = call(square_body, [((8, LANES), f32)], (piece,))
    for step in range(len(radix)):
        square = square + permute(square, [(i, i ^ (1 << step)) for i in range(count)])
    param_count = 9 * K * hid + 3 * hid
    conv_piece, bias_piece, head_piece = call(
        functools.partial(final_body, limit=clip_fraction * param_count ** 0.5),
        [((9, K, share), f32), ((1, share), f32), ((2, share), f32)],
        (square, piece),
    )
    return first_grad, second_grad, conv_piece, bias_piece.reshape(share), head_piece


def solution(mesh):
    return jax.shard_map(
        on_device,
        mesh=mesh,
        in_specs=(
            P("region", "group", None),
            P("region", "group", None),
            P(None, "region", "group"),
            P(None, "group"),
            P(),
            P(),
            P(),
        ),
        out_specs=(
            P("region", "group", None),
            P("region", "group", None),
            P("group", None, "region"),
            P(("group", "region")),
            P("group", "region"),
        ),
        check_vma=False,
    )
```

time: 248 us -> 111 us (0.45)
  local copies, waits for them, and re-layouts: 80.4 us -> 9.73 us
  matrix products: 40.8 us -> 0.44 us
  Pallas kernels: 0 us -> 39 us
  blocking collectives: 32.8 us -> 0 us
  waiting for transfers between devices: 34.3 us -> 16.4 us
  between operations: 16.7 us -> 0.94 us
  starting transfers between devices: 27 us -> 41.9 us
  other arithmetic: 13.6 us -> 2.02 us
    reshape x36 -> x2, local copies, waits for them, and re-layouts: 42.7 us -> 0.17 us  [reorder(): return jnp.transpose(x.reshape(tuple(radix) + (share,)), turn).reshape(hid)]
    dot_general x57 -> x2, matrix products: 40.8 us -> 0.44 us  [the longest x1 0.28 us: on_device(): jnp.einsum('tkh,hg->tkg', conv_weight, select, preferred_element_type=bf16)]
    pallas_call x0 -> x7, Pallas kernels: none -> 39 us  [call(): pl.pallas_call(body, out_shape=[jax.ShapeDtypeStruct(s, d) for s, d in ou...]
    psum x1 -> x0, blocking collectives: 32.8 us -> none  [on_device(): totals = lax.psum((conv_sum, bias_sum, head_sum), 'region')]
    psum x1 -> x0, waiting for transfers between devices: 25.8 us -> none  [on_device(): totals = lax.psum((conv_sum, bias_sum, head_sum), 'region')]
    concatenate x19 -> x0, local copies, waits for them, and re-layouts: 24 us -> none  [the longest x8 11 us: undiagonals(): padded = jnp.concatenate([planes, filler], axis=-1)]
    ppermute x8 -> x18, starting transfers between devices: 26.9 us -> 41.9 us  [permute(): return lax.ppermute(x, 'region', pairs)]
    ppermute x8 -> x18, waiting for transfers between devices: 8.47 us -> 16.4 us  [permute(): return lax.ppermute(x, 'region', pairs)]
  transfers between devices with their start and end apart: 9 -> 18, of which waited for: 4 -> 7; matrix products, arithmetic and copies ran while one was open for 28% -> 7% of each run, Pallas kernels for 0% -> 16%
where the time goes in v1:
time: 111 us; the launch traced here: 110 us
  starting transfers between devices  41.9 us (38%)
  Pallas kernels  39 us (35%)
  waiting for transfers between devices  16.4 us (15%)
  local copies, waits for them, and re-layouts  9.73 us (9%)
  other arithmetic  2.02 us (2%)
    ppermute x18, starting transfers between devices, permute(): return lax.ppermute(x, 'region', pairs)  41.9 us
    pallas_call x7, Pallas kernels, call(): pl.pallas_call(body, out_shape=[jax.ShapeDtypeStruct(s, d) for s, d in ou...  39 us
    ppermute x18, waiting for transfers between devices, permute(): return lax.ppermute(x, 'region', pairs)  16.4 us
    unnamed x37, local copies, waits for them, and re-layouts  5.52 us
  transfers between devices with their start and end apart: 18, of which 7 were waited for; matrix products, arithmetic and copies ran while one was open for 7% of the time, Pallas kernels for 16%

profile of v1, /device:TPU:0, one launch (start us, length us, event | category | flops | bytes accessed | tf_op | source)
XLA Modules:
  0.0 110.4 jit_solution(11139355563259297234)
XLA Ops:
  0.6 2.5 %collective-permute-start = (bf16[4,256,256]{2,1,0:T(8,128)(2,1)}, bf16[4,256,256]{2,1,0:T(8,128)(2,1)S(1)}, u32[]{:S(2)}, u32[]{:S(2)}) collective-permute-start(bf16[4,256,256]{2,1,0:T(8,128)(2,1)} %second_ref.1), channel_id=1, source_target_pairs={{0,1},{1,2},{2,3},{3,4},{4,5},{5,6},{6,7},{7,8},{8,9},{9,10},{10,1... | collective-permute-start | bytes 1572872 | tf_op jit(solution)/shard_map/ppermute | solution.py:265
  7.9 1.4 %collective-permute-done.1.high_ref = bf16[4,256,256]{2,1,0:T(8,128)(2,1)S(1)} collective-permute-done((bf16[4,256,256]{2,1,0:T(8,128)(2,1)}, bf16[4,256,256]{2,1,0:T(8,128)(2,1)S(1)}, u32[]{:S(2)}, u32[]{:S(2)}) %collective-permute-start.1) | collective-permute-done | bytes 524320 | tf_op jit(solution)/shard_map/ppermute | solution.py:265
  10.1 8.2 %shard_map.110 = (bf16[4,256,128]{2,1,0:T(8,128)(2,1)}, bf16[256,128]{1,0:T(8,128)(2,1)}, bf16[256,128]{1,0:T(8,128)(2,1)}) custom-call(s32[1]{0:T(128)} %bitcast.par_ref, bf16[4,256,256]{2,1,0:T(8,128)(2,1)} %first_ref.3, bf16[4,256,256]{2,1,0:T(8,128)(2,1)} %second_ref.1, bf16[4,256,256]{2,1,0:T(8,128)(2,1)} %copy-done.2, bf16[4,256,256]{2,1,0:T(8,128)(2,1)} %copy-done.3), custom_call_target="tpu_custom_call" | custom-call | tf_op jit(solution)/shard_map/pallas_call | solution.py:45
  18.3 8.7 %collective-permute-start.2 = (bf16[256,128]{1,0:T(8,128)(2,1)}, bf16[256,128]{1,0:T(8,128)(2,1)S(1)}, u32[]{:S(2)}, u32[]{:S(2)}) collective-permute-start(bf16[256,128]{1,0:T(8,128)(2,1)} %get-tuple-element.22), channel_id=1, source_target_pairs={{0,1},{1,0},{2,3},{3,2},{4,5},{5,4},{6,7},{7,6},{8,9},{9,8},{10,11... | collective-permute-start | bytes 196616 | tf_op jit(solution)/shard_map/ppermute | solution.py:265
  29.1 6.2 %shard_map.111 = (bf16[4,256,256]{2,1,0:T(8,128)(2,1)}, bf16[256,256]{1,0:T(8,128)(2,1)}, bf16[256,256]{1,0:T(8,128)(2,1)}, f32[256,768]{1,0:T(8,128)}) custom-call(s32[1]{0:T(128)} %bitcast.par_ref, bf16[4,256,128]{2,1,0:T(8,128)(2,1)} %get-tuple-element.21.corr_ref, bf16[256,128]{1,0:T(8,128)(2,1)} %copy-done.11, bf16[256,128]{1,0:T(8,128)(2,1)} %copy-done.12, ...), custom_call_target="tpu_custom_call" | custom-call | tf_op jit(solution)/shard_map/pallas_call | solution.py:45
  36.4 5.1 %collective-permute-start.8 = (f32[128,768]{1,0:T(8,128)S(1)}, f32[128,768]{1,0:T(8,128)S(1)}, u32[]{:S(2)}, u32[]{:S(2)}) collective-permute-start(f32[128,768]{1,0:T(8,128)S(1)} %dynamic-slice_bitcast_fusion), channel_id=1, source_target_pairs={{0,1},{1,0},{2,3},{3,2},{4,5},{5,4},{6,7},{7,6},{8,9},{9,8},{10,11... | collective-permute-start | bytes 1179656 | tf_op jit(solution)/shard_map/ppermute | solution.py:265
  41.5 1.3 %collective-permute-done.8 = f32[128,768]{1,0:T(8,128)S(1)} collective-permute-done((f32[128,768]{1,0:T(8,128)S(1)}, f32[128,768]{1,0:T(8,128)S(1)}, u32[]{:S(2)}, u32[]{:S(2)}) %collective-permute-start.8) | collective-permute-done | bytes 393248 | tf_op jit(solution)/shard_map/ppermute | solution.py:265
  43.0 3.0 %collective-permute-start.9 = (f32[64,768]{1,0:T(8,128)S(1)}, f32[64,768]{1,0:T(8,128)S(1)}, u32[]{:S(2)}, u32[]{:S(2)}) collective-permute-start(f32[64,768]{1,0:T(8,128)S(1)} %dynamic-slice_bitcast_fusion.1), channel_id=1, source_target_pairs={{0,2},{1,3},{2,0},{3,1},{4,6},{5,7},{6,4},{7,5},{8,10},{9,11},{10,... | collective-permute-start | bytes 589832 | tf_op jit(solution)/shard_map/ppermute | solution.py:265
  46.0 5.4 %collective-permute-done.9 = f32[64,768]{1,0:T(8,128)S(1)} collective-permute-done((f32[64,768]{1,0:T(8,128)S(1)}, f32[64,768]{1,0:T(8,128)S(1)}, u32[]{:S(2)}, u32[]{:S(2)}) %collective-permute-start.9) | collective-permute-done | bytes 196640 | tf_op jit(solution)/shard_map/ppermute | solution.py:265
  51.5 2.1 %collective-permute-start.12 = (f32[32,768]{1,0:T(8,128)S(1)}, f32[32,768]{1,0:T(8,128)S(1)}, u32[]{:S(2)}, u32[]{:S(2)}) collective-permute-start(f32[32,768]{1,0:T(8,128)S(1)} %dynamic-slice_bitcast_fusion.2), channel_id=1, source_target_pairs={{0,4},{1,5},{2,6},{3,7},{4,0},{5,1},{6,2},{7,3},{8,12},{9,13},{10,... | collective-permute-start | bytes 294920 | tf_op jit(solution)/shard_map/ppermute | solution.py:265
  54.3 4.5 %collective-permute-start.10 = (bf16[4,256,256]{2,1,0:T(8,128)(2,1)S(1)}, bf16[4,256,256]{2,1,0:T(8,128)(2,1)S(1)}, u32[]{:S(2)}, u32[]{:S(2)}) collective-permute-start(bf16[4,256,256]{2,1,0:T(8,128)(2,1)S(1)} %copy-done.1), channel_id=1, source_target_pairs={{0,1},{1,2},{2,3},{3,4},{4,5},{5,6},{6,7},{7,8},{8,9},{9,10},{10,1... | collective-permute-start | bytes 1572872 | tf_op jit(solution)/shard_map/ppermute | solution.py:265
  60.2 5.0 %collective-permute-start.13 = (f32[16,768]{1,0:T(8,128)S(1)}, f32[16,768]{1,0:T(8,128)S(1)}, u32[]{:S(2)}, u32[]{:S(2)}) collective-permute-start(f32[16,768]{1,0:T(8,128)S(1)} %dynamic-slice_bitcast_fusion.3), channel_id=1, source_target_pairs={{0,8},{1,9},{2,10},{3,11},{4,12},{5,13},{6,14},{7,15},{8,0},{9,1},... | collective-permute-start | bytes 147464 | tf_op jit(solution)/shard_map/ppermute | solution.py:265
  65.9 3.2 %shard_map.112 = (bf16[4,256,128]{2,1,0:T(8,128)(2,1)}, bf16[256,128]{1,0:T(8,128)(2,1)}, bf16[256,128]{1,0:T(8,128)(2,1)}) custom-call(s32[1]{0:T(128)} %bitcast.par_ref, bf16[4,256,256]{2,1,0:T(8,128)(2,1)} %get-tuple-element.24.pe_ref, bf16[256,256]{1,0:T(8,128)(2,1)} %copy-done.7, bf16[256,256]{1,0:T(8,128)(2,1)} %copy-done.8, bf16[3,384,256]{2,1,0:T(8,128)(2,1)} %bitcast.35), custom_call_target="tpu_custom_call" | custom-call | tf_op jit(solution)/shard_map/pallas_call | solution.py:45
  69.9 2.8 %collective-permute-done.13 = f32[16,768]{1,0:T(8,128)S(1)} collective-permute-done((f32[16,768]{1,0:T(8,128)S(1)}, f32[16,768]{1,0:T(8,128)S(1)}, u32[]{:S(2)}, u32[]{:S(2)}) %collective-permute-start.13) | collective-permute-done | bytes 49184 | tf_op jit(solution)/shard_map/ppermute | solution.py:265
  73.4 1.5 %shard_map.115 = f32[8,128]{1,0:T(8,128)} custom-call(f32[16,768]{1,0:T(8,128)} %bitcast_add_fusion.3.piece_ref), custom_call_target="tpu_custom_call" | custom-call | tf_op jit(solution)/shard_map/pallas_call | solution.py:45
  74.9 1.4 %collective-permute-done.14 = f32[8,128]{1,0:T(8,128)S(1)} collective-permute-done((f32[8,128]{1,0:T(8,128)}, f32[8,128]{1,0:T(8,128)S(1)}, u32[]{:S(2)}, u32[]{:S(2)}) %collective-permute-start.14) | collective-permute-done | bytes 4128 | tf_op jit(solution)/shard_map/ppermute | solution.py:265
  78.2 2.4 %collective-permute-done.15 = f32[8,128]{1,0:T(8,128)S(1)} collective-permute-done((f32[8,128]{1,0:T(8,128)S(1)}, f32[8,128]{1,0:T(8,128)S(1)}, u32[]{:S(2)}, u32[]{:S(2)}) %collective-permute-start.15) | collective-permute-done | bytes 4128 | tf_op jit(solution)/shard_map/ppermute | solution.py:265
  80.5 2.7 %collective-permute-start.16 = (f32[8,128]{1,0:T(8,128)S(1)}, f32[8,128]{1,0:T(8,128)S(1)}, u32[]{:S(2)}, u32[]{:S(2)}) collective-permute-start(f32[8,128]{1,0:T(8,128)S(1)} %add.109), channel_id=1, source_target_pairs={{0,4},{1,5},{2,6},{3,7},{4,0},{5,1},{6,2},{7,3},{8,12},{9,13},{10,... | collective-permute-start | bytes 12296 | tf_op jit(solution)/shard_map/ppermute | solution.py:265
  83.3 1.6 %collective-permute-done.16 = f32[8,128]{1,0:T(8,128)S(1)} collective-permute-done((f32[8,128]{1,0:T(8,128)S(1)}, f32[8,128]{1,0:T(8,128)S(1)}, u32[]{:S(2)}, u32[]{:S(2)}) %collective-permute-start.16) | collective-permute-done | bytes 4128 | tf_op jit(solution)/shard_map/ppermute | solution.py:265
  84.8 2.3 %collective-permute-start.17 = (f32[8,128]{1,0:T(8,128)S(1)}, f32[8,128]{1,0:T(8,128)S(1)}, u32[]{:S(2)}, u32[]{:S(2)}) collective-permute-start(f32[8,128]{1,0:T(8,128)S(1)} %add.110), channel_id=1, source_target_pairs={{0,8},{1,9},{2,10},{3,11},{4,12},{5,13},{6,14},{7,15},{8,0},{9,1},... | collective-permute-start | bytes 12296 | tf_op jit(solution)/shard_map/ppermute | solution.py:265
  87.1 11.7 %shard_map.113 = (bf16[4,256,256]{2,1,0:T(8,128)(2,1)}, f32[4,256,256]{2,1,0:T(8,128)}) custom-call(bf16[4,256,128]{2,1,0:T(8,128)(2,1)} %get-tuple-element.27.ce_ref, bf16[4,256,256]{2,1,0:T(8,128)(2,1)} %first_ref.3, bf16[4,256,256]{2,1,0:T(8,128)(2,1)} %second_ref.1, bf16[4,256,256]{2,1,0:T(8,128)(2,1)} %copy-done.2, bf16[4,256,256]{2,1,0:T(8,128)(2,1)} %copy-done.3), custom_call_target="tpu_custom_call" | custom-call | tf_op jit(solution)/shard_map/pallas_call | solution.py:45
  99.4 1.8 %shard_map.116 = (f32[9,81,16]{2,1,0:T(8,128)}, f32[1,16]{1,0:T(1,128)}, f32[2,16]{1,0:T(2,128)}) custom-call(f32[8,128]{1,0:T(8,128)} %add.111.sq_ref, f32[16,768]{1,0:T(8,128)} %bitcast_add_fusion.3.piece_ref), custom_call_target="tpu_custom_call" | custom-call | tf_op jit(solution)/shard_map/pallas_call | solution.py:45
  101.1 1.8 %copy.14 = f32[9,81,16]{1,2,0:T(8,128)} copy(f32[9,81,16]{2,1,0:T(8,128)} %get-tuple-element.44) | data formatting | bytes 93312
  104.0 6.4 %shard_map.114 = bf16[4,256,256]{2,1,0:T(8,128)(2,1)} custom-call(s32[1]{0:T(128)} %bitcast.par_ref, f32[4,256,256]{2,1,0:T(8,128)} %get-tuple-element.29.part_ref, bf16[256,128]{1,0:T(8,128)(2,1)} %copy-done.9, bf16[256,128]{1,0:T(8,128)(2,1)} %copy-done.10, bf16[4,256,256]{2,1,0:T(8,128)(2,1)} %copy-done.5, bf16[4,256,256]{2,1,0:T(8,128)(2,1)} %copy-done.6), custom_call_target="tpu_custom_call" | custom-call | tf_op jit(solution)/shard_map/pallas_call | solution.py:45
  (81 shorter events, 16.4 us)
Async XLA Ops:
  0.6 5.3 %copy-start = (bf16[9,81,256]{2,1,0:T(8,128)(2,1)S(1)}, bf16[9,81,256]{2,1,0:T(8,128)(2,1)}, u32[]{:S(2)}) copy-start(bf16[9,81,256]{2,1,0:T(8,128)(2,1)} %param.11) | copy-start | bytes 1119748
  0.6 7.2 %collective-permute-start = (bf16[4,256,256]{2,1,0:T(8,128)(2,1)}, bf16[4,256,256]{2,1,0:T(8,128)(2,1)S(1)}, u32[]{:S(2)}, u32[]{:S(2)}) collective-permute-start(bf16[4,256,256]{2,1,0:T(8,128)(2,1)} %second_ref.1), channel_id=1, source_target_pairs={{0,1},{1,2},{2,3},{3,4},{4,5},{5,6},{6,7},{7,8},{8,9},{9,10},{10,1... | collective-permute-start | bytes 1572872 | tf_op jit(solution)/shard_map/ppermute | solution.py:265
  3.2 6.1 %collective-permute-start.1 = (bf16[4,256,256]{2,1,0:T(8,128)(2,1)}, bf16[4,256,256]{2,1,0:T(8,128)(2,1)S(1)}, u32[]{:S(2)}, u32[]{:S(2)}) collective-permute-start(bf16[4,256,256]{2,1,0:T(8,128)(2,1)} %second_ref.1), channel_id=1, source_target_pairs={{1,0},{2,1},{3,2},{4,3},{5,4},{6,5},{7,6},{8,7},{9,8},{10,9},{11,1... | collective-permute-start | bytes 1572872 | tf_op jit(solution)/shard_map/ppermute | solution.py:265
  18.3 9.4 %copy-start.13 = (s32[4,16]{1,0:T(4,128)S(1)}, s32[4,16]{1,0:T(4,128)}, u32[]{:S(2)}) copy-start(s32[4,16]{1,0:T(4,128)} %param.10) | copy-start | bytes 772
  18.3 10.2 %collective-permute-start.2 = (bf16[256,128]{1,0:T(8,128)(2,1)}, bf16[256,128]{1,0:T(8,128)(2,1)S(1)}, u32[]{:S(2)}, u32[]{:S(2)}) collective-permute-start(bf16[256,128]{1,0:T(8,128)(2,1)} %get-tuple-element.22), channel_id=1, source_target_pairs={{0,1},{1,0},{2,3},{3,2},{4,5},{5,4},{6,7},{7,6},{8,9},{9,8},{10,11... | collective-permute-start | bytes 196616 | tf_op jit(solution)/shard_map/ppermute | solution.py:265
  27.0 1.5 %collective-permute-start.3 = (bf16[256,128]{1,0:T(8,128)(2,1)}, bf16[256,128]{1,0:T(8,128)(2,1)S(1)}, u32[]{:S(2)}, u32[]{:S(2)}) collective-permute-start(bf16[256,128]{1,0:T(8,128)(2,1)} %get-tuple-element.23), channel_id=1, source_target_pairs={{1,2},{3,4},{5,6},{7,8},{9,10},{11,12},{13,14},{2,1},{4,3},{6,5},{... | collective-permute-start | bytes 196616 | tf_op jit(solution)/shard_map/ppermute | solution.py:265
  35.3 7.6 %copy-start.4 = (f32[256,768]{1,0:T(8,128)S(1)}, f32[256,768]{1,0:T(8,128)}, u32[]{:S(2)}) copy-start(f32[256,768]{1,0:T(8,128)} %get-tuple-element.32) | copy-start | bytes 2359300
  36.4 6.5 %collective-permute-start.8 = (f32[128,768]{1,0:T(8,128)S(1)}, f32[128,768]{1,0:T(8,128)S(1)}, u32[]{:S(2)}, u32[]{:S(2)}) collective-permute-start(f32[128,768]{1,0:T(8,128)S(1)} %dynamic-slice_bitcast_fusion), channel_id=1, source_target_pairs={{0,1},{1,0},{2,3},{3,2},{4,5},{5,4},{6,7},{7,6},{8,9},{9,8},{10,11... | collective-permute-start | bytes 1179656 | tf_op jit(solution)/shard_map/ppermute | solution.py:265
  42.9 11.3 %copy-start.1 = (bf16[4,256,256]{2,1,0:T(8,128)(2,1)S(1)}, bf16[4,256,256]{2,1,0:T(8,128)(2,1)}, u32[]{:S(2)}) copy-start(bf16[4,256,256]{2,1,0:T(8,128)(2,1)} %first_ref.3) | copy-start | bytes 1572868
  43.0 8.4 %collective-permute-start.9 = (f32[64,768]{1,0:T(8,128)S(1)}, f32[64,768]{1,0:T(8,128)S(1)}, u32[]{:S(2)}, u32[]{:S(2)}) collective-permute-start(f32[64,768]{1,0:T(8,128)S(1)} %dynamic-slice_bitcast_fusion.1), channel_id=1, source_target_pairs={{0,2},{1,3},{2,0},{3,1},{4,6},{5,7},{6,4},{7,5},{8,10},{9,11},{10,... | collective-permute-start | bytes 589832 | tf_op jit(solution)/shard_map/ppermute | solution.py:265
  51.4 2.2 %copy-start.16 = (bf16[256,256]{1,0:T(8,128)(2,1)S(1)}, bf16[256,256]{1,0:T(8,128)(2,1)}, u32[]{:S(2)}) copy-start(bf16[256,256]{1,0:T(8,128)(2,1)} %get-tuple-element.25) | copy-start | bytes 393220
  51.4 2.2 %copy-start.15 = (bf16[256,256]{1,0:T(8,128)(2,1)S(1)}, bf16[256,256]{1,0:T(8,128)(2,1)}, u32[]{:S(2)}) copy-start(bf16[256,256]{1,0:T(8,128)(2,1)} %get-tuple-element.26) | copy-start | bytes 393220
  51.5 8.7 %collective-permute-start.12 = (f32[32,768]{1,0:T(8,128)S(1)}, f32[32,768]{1,0:T(8,128)S(1)}, u32[]{:S(2)}, u32[]{:S(2)}) collective-permute-start(f32[32,768]{1,0:T(8,128)S(1)} %dynamic-slice_bitcast_fusion.2), channel_id=1, source_target_pairs={{0,4},{1,5},{2,6},{3,7},{4,0},{5,1},{6,2},{7,3},{8,12},{9,13},{10,... | collective-permute-start | bytes 294920 | tf_op jit(solution)/shard_map/ppermute | solution.py:265
  53.6 11.5 %collective-permute-start.4 = (bf16[256,256]{1,0:T(8,128)(2,1)S(1)}, bf16[256,256]{1,0:T(8,128)(2,1)S(1)}, u32[]{:S(2)}, u32[]{:S(2)}) collective-permute-start(bf16[256,256]{1,0:T(8,128)(2,1)S(1)} %copy-done.16), channel_id=1, source_target_pairs={{0,1},{1,0},{2,3},{3,2},{4,5},{5,4},{6,7},{7,6},{8,9},{9,8},{10,11... | collective-permute-start | bytes 393224 | tf_op jit(solution)/shard_map/ppermute | solution.py:265
  53.6 11.5 %collective-permute-start.5 = (bf16[256,256]{1,0:T(8,128)(2,1)S(1)}, bf16[256,256]{1,0:T(8,128)(2,1)S(1)}, u32[]{:S(2)}, u32[]{:S(2)}) collective-permute-start(bf16[256,256]{1,0:T(8,128)(2,1)S(1)} %copy-done.15), channel_id=1, source_target_pairs={{1,2},{3,4},{5,6},{7,8},{9,10},{11,12},{13,14},{2,1},{4,3},{6,5},{... | collective-permute-start | bytes 393224 | tf_op jit(solution)/shard_map/ppermute | solution.py:265
  54.3 48.7 %collective-permute-start.10 = (bf16[4,256,256]{2,1,0:T(8,128)(2,1)S(1)}, bf16[4,256,256]{2,1,0:T(8,128)(2,1)S(1)}, u32[]{:S(2)}, u32[]{:S(2)}) collective-permute-start(bf16[4,256,256]{2,1,0:T(8,128)(2,1)S(1)} %copy-done.1), channel_id=1, source_target_pairs={{0,1},{1,2},{2,3},{3,4},{4,5},{5,6},{6,7},{7,8},{8,9},{9,10},{10,1... | collective-permute-start | bytes 1572872 | tf_op jit(solution)/shard_map/ppermute | solution.py:265
  58.8 44.1 %collective-permute-start.11 = (bf16[4,256,256]{2,1,0:T(8,128)(2,1)S(1)}, bf16[4,256,256]{2,1,0:T(8,128)(2,1)S(1)}, u32[]{:S(2)}, u32[]{:S(2)}) collective-permute-start(bf16[4,256,256]{2,1,0:T(8,128)(2,1)S(1)} %copy-done.1), channel_id=1, source_target_pairs={{1,0},{2,1},{3,2},{4,3},{5,4},{6,5},{7,6},{8,7},{9,8},{10,9},{11,1... | collective-permute-start | bytes 1572872 | tf_op jit(solution)/shard_map/ppermute | solution.py:265
  60.2 12.5 %collective-permute-start.13 = (f32[16,768]{1,0:T(8,128)S(1)}, f32[16,768]{1,0:T(8,128)S(1)}, u32[]{:S(2)}, u32[]{:S(2)}) collective-permute-start(f32[16,768]{1,0:T(8,128)S(1)} %dynamic-slice_bitcast_fusion.3), channel_id=1, source_target_pairs={{0,8},{1,9},{2,10},{3,11},{4,12},{5,13},{6,14},{7,15},{8,0},{9,1},... | collective-permute-start | bytes 147464 | tf_op jit(solution)/shard_map/ppermute | solution.py:265
  69.0 33.9 %collective-permute-start.6 = (bf16[256,128]{1,0:T(8,128)(2,1)}, bf16[256,128]{1,0:T(8,128)(2,1)S(1)}, u32[]{:S(2)}, u32[]{:S(2)}) collective-permute-start(bf16[256,128]{1,0:T(8,128)(2,1)} %get-tuple-element.30), channel_id=1, source_target_pairs={{0,1},{1,0},{2,3},{3,2},{4,5},{5,4},{6,7},{7,6},{8,9},{9,8},{10,11... | collective-permute-start | bytes 196616 | tf_op jit(solution)/shard_map/ppermute | solution.py:265
  69.0 33.9 %collective-permute-start.7 = (bf16[256,128]{1,0:T(8,128)(2,1)}, bf16[256,128]{1,0:T(8,128)(2,1)S(1)}, u32[]{:S(2)}, u32[]{:S(2)}) collective-permute-start(bf16[256,128]{1,0:T(8,128)(2,1)} %get-tuple-element.31), channel_id=1, source_target_pairs={{1,2},{3,4},{5,6},{7,8},{9,10},{11,12},{13,14},{2,1},{4,3},{6,5},{... | collective-permute-start | bytes 196616 | tf_op jit(solution)/shard_map/ppermute | solution.py:265
  74.9 1.4 %collective-permute-start.14 = (f32[8,128]{1,0:T(8,128)}, f32[8,128]{1,0:T(8,128)S(1)}, u32[]{:S(2)}, u32[]{:S(2)}) collective-permute-start(f32[8,128]{1,0:T(8,128)} %shard_map.115), channel_id=1, source_target_pairs={{0,1},{1,0},{2,3},{3,2},{4,5},{5,4},{6,7},{7,6},{8,9},{9,8},{10,11... | collective-permute-start | bytes 12296 | tf_op jit(solution)/shard_map/ppermute | solution.py:265
  76.9 3.6 %collective-permute-start.15 = (f32[8,128]{1,0:T(8,128)S(1)}, f32[8,128]{1,0:T(8,128)S(1)}, u32[]{:S(2)}, u32[]{:S(2)}) collective-permute-start(f32[8,128]{1,0:T(8,128)S(1)} %add.108), channel_id=1, source_target_pairs={{0,2},{1,3},{2,0},{3,1},{4,6},{5,7},{6,4},{7,5},{8,10},{9,11},{10,... | collective-permute-start | bytes 12296 | tf_op jit(solution)/shard_map/ppermute | solution.py:265
  80.5 4.3 %collective-permute-start.16 = (f32[8,128]{1,0:T(8,128)S(1)}, f32[8,128]{1,0:T(8,128)S(1)}, u32[]{:S(2)}, u32[]{:S(2)}) collective-permute-start(f32[8,128]{1,0:T(8,128)S(1)} %add.109), channel_id=1, source_target_pairs={{0,4},{1,5},{2,6},{3,7},{4,0},{5,1},{6,2},{7,3},{8,12},{9,13},{10,... | collective-permute-start | bytes 12296 | tf_op jit(solution)/shard_map/ppermute | solution.py:265
  84.8 13.9 %collective-permute-start.17 = (f32[8,128]{1,0:T(8,128)S(1)}, f32[8,128]{1,0:T(8,128)S(1)}, u32[]{:S(2)}, u32[]{:S(2)}) collective-permute-start(f32[8,128]{1,0:T(8,128)S(1)} %add.110), channel_id=1, source_target_pairs={{0,8},{1,9},{2,10},{3,11},{4,12},{5,13},{6,14},{7,15},{8,0},{9,1},... | collective-permute-start | bytes 12296 | tf_op jit(solution)/shard_map/ppermute | solution.py:265
  (12 other events, 9.5 us)

commit v2 on v1

v2 whole, which is shorter than its diff:
```python
import functools

import jax
import jax.numpy as jnp
from jax import lax
from jax.experimental import pallas as pl
from jax.experimental.pallas import tpu as pltpu
from jax.sharding import PartitionSpec as P

C = 256
RADIUS = 4
TILE = 16
K = 81
WIN = 9
LANES = 128

clip_fraction = 0.25
WIDTH = 768
VMEM_LIMIT = 24 * 1024 * 1024

f32 = jnp.float32
bf16 = jnp.bfloat16

NT = (((1,), (1,)), ((), ()))
TN = (((0,), (0,)), ((), ()))


def dot(a, b, dims=None):
    if dims is None:
        return jnp.dot(a, b, preferred_element_type=f32)
    return lax.dot_general(a, b, dims, preferred_element_type=f32)


def iota(shape, dim):
    return lax.broadcasted_iota(jnp.int32, shape, dim)


SMEM = pl.BlockSpec(memory_space=pltpu.SMEM)
VMEM = pl.BlockSpec(memory_space=pltpu.VMEM)


def call(body, outs, args, scratch=(), scalar=False):
    specs = [VMEM] * len(args)
    if scalar:
        specs[0] = SMEM
    return pl.pallas_call(
        body,
        out_shape=[jax.ShapeDtypeStruct(s, d) for s, d in outs],
        in_specs=specs,
        out_specs=[VMEM] * len(outs),
        scratch_shapes=list(scratch),
        compiler_params=pltpu.CompilerParams(vmem_limit_bytes=VMEM_LIMIT),
    )(*args)


def after(value, *others):
    return lax.optimization_barrier((value,) + others)[0]


HALF = LANES


def band_of(products, dyi):
    lane = iota((8, HALF), 1)
    near = jnp.where(lane >= HALF - 8, products[HALF - 8:HALF, :HALF], products[HALF - 8:HALF, HALF:])
    far = jnp.where(lane < 8, products[HALF:HALF + 8, HALF:], products[HALF:HALF + 8, :HALF])
    ring = jnp.concatenate([products[:HALF - 8, HALF:], near, far, products[HALF + 8:, :HALF]], axis=0)
    band = pltpu.roll(ring, 8, 1, stride=1, stride_axis=0)
    return pltpu.roll(band, (9 * dyi - 3) % LANES, 1)


def spread_of(bands, dyi):
    moved = pltpu.roll(bands, (4 - 9 * dyi) % LANES, 1)
    lane = iota(bands.shape, 1)
    own = jnp.where((lane >= 4) & (lane < 13), moved, 0.0)
    ring = pltpu.roll(own, HALF - 8, 1, stride=1, stride_axis=0)
    edge = iota((8, HALF), 1)
    none = jnp.zeros((8, HALF), f32)
    near = ring[HALF - 8:HALF]
    far = ring[HALF:HALF + 8]
    left = jnp.concatenate([ring[HALF - 16:HALF - 8], jnp.where(edge < 8, 0.0, near), jnp.where(edge >= HALF - 8, far, 0.0), none], axis=0)
    right = jnp.concatenate([none, jnp.where(edge < 8, near, 0.0), jnp.where(edge >= HALF - 8, 0.0, far), ring[HALF + 8:HALF + 16]], axis=0)
    zero = jnp.zeros((HALF - 16, HALF), bf16)
    left = jnp.concatenate([ring[:HALF - 16].astype(bf16), left.astype(bf16), zero], axis=0)
    right = jnp.concatenate([zero, right.astype(bf16), ring[HALF + 16:].astype(bf16)], axis=0)
    return jnp.concatenate([left, right], axis=1)


def lane_valid(rows):
    lane = iota((rows, LANES), 1)
    col = iota((rows, LANES), 0) + lane % WIN - RADIUS
    return (col >= 0) & (col < rows) & (lane < K)


def corr_rows(first_ref, second_ref, start, before, put):
    rows, cols = first_ref.shape[0], first_ref.shape[1]
    count = second_ref.shape[0]
    lane = iota((cols, LANES), 1)
    valid = lane_valid(cols)
    mirror = (iota((cols, cols), 0) + iota((cols, cols), 1) == cols - 1).astype(bf16)
    for r in range(rows):
        dys = [q - r + RADIUS for q in range(start, start + count) if abs(q - r) <= RADIUS]
        if not dys:
            put(r, before[r])
            continue
        turned = dot(mirror, first_ref[r]).astype(bf16)
        acc = jnp.zeros((cols, LANES), f32)
        for dyi in dys:
            band = band_of(dot(turned, second_ref[r + dyi - RADIUS - start], NT), dyi)
            acc = jnp.where((lane >= 9 * dyi) & (lane < 9 * dyi + 9), band, acc)
        acc = jnp.where(valid, dot(mirror, (acc * (C ** -0.5)).astype(bf16)), 0.0)
        if before is None:
            acc = jnp.where(lane == K, 1.0, acc)
        else:
            inside = (lane >= 9 * dys[0]) & (lane < 9 * dys[-1] + 9)
            acc = jnp.where(inside, acc, before[r].astype(f32))
        put(r, acc.astype(bf16))


def corr_own_body(first_ref, own_ref, corr_ref):
    corr_rows(first_ref, own_ref, 0, None, lambda r, v: corr_ref.__setitem__(r, v))


def corr_halo_body(par_ref, first_ref, old_ref, low_ref, high_ref, corr_ref, ea_ref, eb_ref, mid_ref):
    rows = first_ref.shape[0]
    par = par_ref[0]
    corr_rows(first_ref, low_ref, -low_ref.shape[0], old_ref, lambda r, v: mid_ref.__setitem__(r, v))
    corr_rows(first_ref, high_ref, rows, mid_ref, lambda r, v: corr_ref.__setitem__(r, v))
    ea_ref[...] = corr_ref[(1 - par) * (rows - 1)]
    eb_ref[...] = corr_ref[par * (rows - 1)]


def shift_down(x, steps):
    zero = jnp.zeros((abs(steps), x.shape[1]), x.dtype)
    if steps > 0:
        return jnp.concatenate([zero, x[:-steps]], axis=0)
    return jnp.concatenate([x[-steps:], zero], axis=0)


def put_taps(x_ref, slot, value):
    wide = value.astype(f32)
    x_ref[slot, :, 0:LANES] = shift_down(wide, 1).astype(bf16)
    x_ref[slot, :, LANES:2 * LANES] = value
    x_ref[slot, :, 2 * LANES:] = shift_down(wide, -1).astype(bf16)


def cell_row(pre, r, head, target_ref, mask_ref):
    cols = pre.shape[0]
    sig = lax.logistic(pre)
    hidden = (pre * sig).astype(bf16)
    pred = dot(head, hidden, NT)
    err = mask_ref[r:r + 1, :] * (pred[0:2] - target_ref[:, r, :])
    err = jnp.concatenate([err, jnp.zeros((head.shape[0] - 2, cols), f32)], axis=0).astype(bf16)
    herr = dot(err, head, TN)
    pe = (herr * sig * (1.0 + pre * (1.0 - sig))).astype(bf16)
    return pe, dot(err, hidden)


def conv_own_body(corr_ref, w_ref, bias_ref, head_ref, target_ref, mask_ref, x_ref, pre_ref, pe_ref, part_ref, hsum_ref, pt_ref):
    rows, cols = corr_ref.shape[0], corr_ref.shape[1]
    for r in range(rows):
        put_taps(x_ref, r, corr_ref[r])
    head = head_ref[...]
    pre_ref[0] = bias_ref[...] + (dot(x_ref[0], w_ref[1]) + dot(x_ref[1], w_ref[2]))
    pre_ref[1] = bias_ref[...] + (dot(x_ref[rows - 2], w_ref[0]) + dot(x_ref[rows - 1], w_ref[1]))
    total = jnp.zeros(hsum_ref.shape, f32)
    for r in range(1, rows - 1):
        pre = bias_ref[...] + (dot(x_ref[r - 1], w_ref[0]) + dot(x_ref[r], w_ref[1]) + dot(x_ref[r + 1], w_ref[2]))
        pe, head_sum = cell_row(pre, r, head, target_ref, mask_ref)
        total = total + head_sum
        pe_ref[r - 1] = pe
        pt_ref[:, (r - 1) * cols:r * cols] = pe.T
    hsum_ref[...] = total
    for ty in range(3):
        x = x_ref[ty:ty + rows - 2].reshape((rows - 2) * cols, 3 * LANES)
        part_ref[:, ty * 3 * LANES:(ty + 1) * 3 * LANES] = dot(pt_ref[...], x)


def conv_edge_body(par_ref, x_ref, pre_ref, part_ref, hsum_ref, ha_ref, hb_ref, w_ref, head_ref, target_ref, mask_ref,
                   pe_ref, pa_ref, pb_ref, keep_ref, send_ref, h_ref, pt_ref):
    rows, cols = x_ref.shape[0], x_ref.shape[1]
    hid = w_ref.shape[2]
    par = par_ref[0]
    put_taps(h_ref, 1 - par, ha_ref[...])
    put_taps(h_ref, par, hb_ref[...])
    head = head_ref[...]
    head_sum = hsum_ref[...]
    for i, r in enumerate((0, rows - 1)):
        pre = pre_ref[i] + dot(h_ref[i], w_ref[2 * i])
        pe, own_sum = cell_row(pre, r, head, target_ref, mask_ref)
        head_sum = head_sum + own_sum
        pe_ref[i] = pe
        pt_ref[i] = pe.T
    pa_ref[...] = pe_ref[1 - par]
    pb_ref[...] = pe_ref[par]
    top, bottom = pt_ref[0], pt_ref[1]
    pieces = []
    bias_col = None
    for ty in range(3):
        low = h_ref[0] if ty == 0 else x_ref[ty - 1]
        high = h_ref[1] if ty == 2 else x_ref[rows - 2 + ty]
        part = part_ref[:, ty * 3 * LANES:(ty + 1) * 3 * LANES] + (dot(top, low) + dot(bottom, high))
        for tx in range(3):
            pieces.append(part[:, tx * LANES:tx * LANES + K])
        if ty == 1:
            bias_col = part[:, LANES + K:LANES + K + 1]
    head_cols = jnp.concatenate([head_sum, jnp.zeros((LANES - head.shape[0], hid), f32)], axis=0).T
    pad = jnp.zeros((hid, WIDTH - 9 * K - 3), f32)
    sums = jnp.concatenate(pieces + [bias_col, head_cols[:, 0:2], pad], axis=1)
    upper, lower = sums[:hid // 2], sums[hid // 2:]
    keep_ref[...] = jnp.where(par == 0, upper, lower)
    send_ref[...] = jnp.where(par == 0, lower, upper)


def halve_body(bit_ref, own_ref, got_ref, keep_ref, send_ref):
    half = keep_ref.shape[0]
    bit = bit_ref[0]
    upper = own_ref[:half] + got_ref[:half]
    lower = own_ref[half:] + got_ref[half:]
    keep_ref[...] = jnp.where(bit == 0, upper, lower)
    send_ref[...] = jnp.where(bit == 0, lower, upper)


def tail_body(own_ref, got_ref, conv_ref, rest_ref, square_ref):
    piece = own_ref[...] + got_ref[...]
    share = piece.shape[0]
    for tap in range(9):
        conv_ref[tap] = piece[:, tap * K:(tap + 1) * K]
    start = 9 * K // LANES * LANES
    rest = jnp.concatenate([piece[:, start:start + LANES], jnp.zeros((LANES - share, LANES), f32)], axis=0)
    rest_ref[...] = rest.T[9 * K - start:9 * K - start + 3, 0:share]
    square_ref[...] = jnp.broadcast_to(jnp.sum(piece * piece).reshape(1, 1), square_ref.shape)


def final_body(sq_ref, got_ref, conv_ref, rest_ref, out_ref, bias_ref, head_ref, *, limit):
    factor = jnp.minimum(1.0, limit / jnp.sqrt(sq_ref[0:1, 0:1] + got_ref[0:1, 0:1] + 1e-06))
    out_ref[...] = conv_ref[...] * factor.reshape(1, 1, 1)
    bias_ref[...] = rest_ref[0:1] * factor
    head_ref[...] = rest_ref[1:3] * factor


def cerr_row(z0, z1, z2):
    z = z0 + z1 + z2
    return shift_down(z[:, 0:LANES], -1) + z[:, LANES:2 * LANES] + shift_down(z[:, 2 * LANES:], 1)


def cerr_own_body(mid_ref, edge_ref, w_ref, ce_ref, rest_ref):
    rows = mid_ref.shape[0] + 2
    cols = mid_ref.shape[1]
    valid = lane_valid(cols)
    row = lambda r: edge_ref[0] if r == 0 else (edge_ref[1] if r == rows - 1 else mid_ref[r - 1])
    for r in range(rows):
        parts = [dot(row(r + 1 - ty), w_ref[ty], NT) for ty in range(3) if 0 <= r + 1 - ty < rows]
        total = cerr_row(parts[0], parts[1], parts[2] if len(parts) == 3 else 0.0)
        if 0 < r < rows - 1:
            ce_ref[r - 1] = jnp.where(valid, total * (C ** -0.5), 0.0).astype(bf16)
        else:
            rest_ref[min(r, 1)] = total


def cerr_edge_body(par_ref, mid_ref, rest_ref, ha_ref, hb_ref, w_ref, ce_ref, ea_ref, eb_ref, h_ref):
    rows = mid_ref.shape[0] + 2
    cols = mid_ref.shape[1]
    par = par_ref[0]
    h_ref[1 - par] = ha_ref[...]
    h_ref[par] = hb_ref[...]
    valid = lane_valid(cols)
    lane = iota((cols, LANES), 1)
    for i in range(2):
        total = rest_ref[i] + cerr_row(dot(h_ref[i], w_ref[2 - 2 * i], NT), 0.0, 0.0)
        ce_ref[i] = jnp.where(valid, total * (C ** -0.5), 0.0).astype(bf16)
    to_low = jnp.zeros((cols, LANES), f32)
    to_high = jnp.zeros((cols, LANES), f32)
    low_at = high_at = 0
    for r in range(rows):
        total = (ce_ref[min(r, 1)] if r in (0, rows - 1) else mid_ref[r - 1]).astype(f32)
        count = 9 * (RADIUS - r)
        moved = pltpu.roll(total, low_at, 1) if low_at else total
        to_low = jnp.where((lane >= low_at) & (lane < low_at + count), moved, to_low)
        low_at += count
        count = 9 * (r + 1 + RADIUS - rows)
        start = K - count
        moved = pltpu.roll(total, (high_at - start) % LANES, 1)
        to_high = jnp.where((lane >= high_at) & (lane < high_at + count), moved, to_high)
        high_at += count
    up = to_low.astype(bf16)
    down = to_high.astype(bf16)

    @pl.when(par == 0)
    def _():
        ea_ref[...] = down
        eb_ref[...] = up

    @pl.when(par != 0)
    def _():
        ea_ref[...] = up
        eb_ref[...] = down


def row_grad(cerr, own_rows, first_ref, second_ref, low_ref, high_ref, fg_ref, part_ref, old_ref):
    rows, cols = first_ref.shape[0], first_ref.shape[1]
    parts = [None if old_ref is None else old_ref[q] for q in range(rows)]
    for i, r in enumerate(own_rows):
        bands = cerr[i].astype(f32)
        turned = first_ref[r].T
        acc = jnp.zeros((cols, C), f32)
        for dyi in range(WIN):
            q = r + dyi - RADIUS
            src = low_ref[q + RADIUS] if q < 0 else (high_ref[q - rows] if q >= rows else second_ref[q])
            spread = spread_of(bands, dyi)
            acc = acc + dot(spread, src)
            if 0 <= q < rows:
                gave = dot(turned, spread)
                parts[q] = gave if parts[q] is None else parts[q] + gave
        fg_ref[i] = acc.astype(bf16)
    for q in range(rows):
        part_ref[q] = parts[q]


def mid_grad_body(ce_ref, first_ref, second_ref, low_ref, high_ref, fg_ref, part_ref):
    row_grad(ce_ref, range(1, first_ref.shape[0] - 1), first_ref, second_ref, low_ref, high_ref, fg_ref, part_ref, None)


def edge_grad_body(ce_ref, old_ref, first_ref, second_ref, low_ref, high_ref, fg_ref, part_ref):
    row_grad(ce_ref, (0, first_ref.shape[0] - 1), first_ref, second_ref, low_ref, high_ref, fg_ref, part_ref, old_ref)


def halo_grad_body(par_ref, part_ref, ca_ref, cb_ref, low_ref, high_ref, sg_ref, c_ref):
    rows, cols = part_ref.shape[0], part_ref.shape[2]
    par = par_ref[0]
    c_ref[1 - par] = ca_ref[...].astype(f32)
    c_ref[par] = cb_ref[...].astype(f32)
    parts = [part_ref[r] for r in range(rows)]
    above = c_ref[0]
    below = c_ref[1]
    at = 0
    for a in range(rows):
        turned = low_ref[a].T
        for i, dy in enumerate(range(rows - a, RADIUS + 1)):
            q = a + dy - rows
            parts[q] = parts[q] + dot(turned, spread_of(above, at // 9 + i))
        at += 9 * (RADIUS + 1 - rows + a)
    at = 0
    for b in range(rows):
        turned = high_ref[b].T
        for i, dy in enumerate(range(-RADIUS, -b)):
            q = rows + b + dy
            parts[q] = parts[q] + dot(turned, spread_of(below, at // 9 + i))
        at += 9 * (RADIUS - b)
    for r in range(rows):
        sg_ref[r] = parts[r].T.astype(bf16)


def on_device(first_map, second_map, flow_target, valid_tiles, conv_weight, conv_bias, head_weight):
    rows, cols = first_map.shape[0], first_map.shape[1]
    hid = conv_weight.shape[2]
    count = lax.axis_size("region")
    index = lax.axis_index("region")
    par = (index % 2).reshape(1)
    forward = [(i, i + 1) for i in range(count - 1)]
    backward = [(b, a) for a, b in forward]
    inner = [(i, i ^ 1) for i in range(count)]
    outer = [(i, i + 1) for i in range(1, count - 1, 2)]
    outer = outer + [(b, a) for a, b in outer]

    def permute(x, pairs):
        return lax.ppermute(x, "region", pairs)

    def swap(x, step):
        return permute(x, [(i, i ^ (1 << step)) for i in range(count)])

    second_low = permute(second_map, forward)
    second_high = permute(second_map, backward)

    share = hid // count
    radix = [2] * (count.bit_length() - 1)
    turn = tuple(reversed(range(len(radix)))) + (len(radix),)

    def reorder(x):
        return jnp.transpose(x.reshape(tuple(radix) + (share,)), turn).reshape(hid)

    order = reorder(jnp.arange(hid))
    select = (jnp.arange(hid)[:, None] == order[None, :]).astype(bf16)
    weight = jnp.einsum("tkh,hg->tkg", conv_weight, select, preferred_element_type=bf16)
    weight = jnp.pad(weight, ((0, 0), (0, LANES - K), (0, 0))).reshape(3, 3 * LANES, hid)
    head = jnp.einsum("jh,hg->jg", head_weight, select, preferred_element_type=bf16)
    head = jnp.pad(head, ((0, 14), (0, 0)))
    bias = reorder(conv_bias).reshape(1, hid)
    tile_rows = jnp.repeat(valid_tiles, TILE, axis=0)
    own_tiles = lax.dynamic_slice_in_dim(tile_rows, index * rows, rows, 0)
    mask = jnp.repeat(own_tiles, TILE, axis=1).astype(f32)

    vector = lambda *s: pltpu.VMEM(s, bf16)
    (corr_own,) = call(corr_own_body, [((rows, cols, LANES), bf16)], (first_map, second_map))
    weight, head, bias, mask, corr_own, second_low, second_high = lax.optimization_barrier(
        (weight, head, bias, mask, corr_own, second_low, second_high)
    )
    corr, edge_a, edge_b = call(
        corr_halo_body,
        [((rows, cols, LANES), bf16), ((cols, LANES), bf16), ((cols, LANES), bf16)],
        (par, first_map, corr_own, second_low, second_high),
        scratch=[vector(rows, cols, LANES)],
        scalar=True,
    )
    halo_a = permute(edge_a, inner)
    halo_b = permute(edge_b, outer)
    taps, pre_edge, pe_mid, part_sums, head_part = call(
        conv_own_body,
        [((rows, cols, 3 * LANES), bf16), ((2, cols, hid), f32), ((rows - 2, cols, hid), bf16), ((hid, 9 * LANES), f32), ((16, hid), f32)],
        (corr, weight, bias, head, flow_target, mask),
        scratch=[vector(hid, (rows - 2) * cols)],
    )
    halo_a, halo_b, taps = lax.optimization_barrier((halo_a, halo_b, taps))
    pe_edge, pe_a, pe_b, keep, send = call(
        conv_edge_body,
        [((2, cols, hid), bf16), ((cols, hid), bf16), ((cols, hid), bf16), ((hid // 2, WIDTH), f32), ((hid // 2, WIDTH), f32)],
        (par, taps, pre_edge, part_sums, head_part, halo_a, halo_b, weight, head, flow_target, mask),
        scratch=[vector(2, cols, 3 * LANES), vector(2, hid, cols)],
        scalar=True,
    )
    got = swap(send, 0)
    pe_halo_a = permute(pe_a, inner)
    pe_halo_b = permute(pe_b, outer)

    def halve(step, keep, got):
        half = keep.shape[0] // 2
        bit = ((index >> step) & 1).reshape(1)
        return call(halve_body, [((half, WIDTH), f32)] * 2, (bit, keep, got), scalar=True)

    keep, send = halve(1, keep, got)
    got = swap(send, 1)
    ce_mid, ce_rest = call(
        cerr_own_body,
        [((rows - 2, cols, LANES), bf16), ((2, cols, LANES), f32)],
        (pe_mid, pe_edge, weight),
    )
    mid_grad, part = call(
        mid_grad_body,
        [((rows - 2, cols, C), bf16), ((rows, C, cols), f32)],
        (after(ce_mid, send), first_map, second_map, second_low, second_high),
    )
    got, part = lax.optimization_barrier((got, part))
    keep, send = halve(2, keep, got)
    got = swap(send, 2)
    first_tied = after(first_map, send)
    first_low = permute(first_tied, forward)
    first_high = permute(first_tied, backward)
    ce_edge, ce_a, ce_b = call(
        cerr_edge_body,
        [((2, cols, LANES), bf16), ((cols, LANES), bf16), ((cols, LANES), bf16)],
        (par, ce_mid, after(ce_rest, send), pe_halo_a, pe_halo_b, weight),
        scratch=[vector(2, cols, hid)],
        scalar=True,
    )
    ce_halo_a = permute(ce_a, inner)
    ce_halo_b = permute(ce_b, outer)
    got, ce_edge = lax.optimization_barrier((got, ce_edge))
    for step in range(3, len(radix)):
        keep, send = halve(step, keep, got)
        got = swap(send, step)
    edge_grad, part = call(
        edge_grad_body,
        [((2, cols, C), bf16), ((rows, C, cols), f32)],
        (after(ce_edge, send), part, first_map, second_map, second_low, second_high),
    )
    got, part = lax.optimization_barrier((got, part))
    conv_raw, rest_raw, square = call(
        tail_body,
        [((9, share, K), f32), ((3, share), f32), ((8, LANES), f32)],
        (keep, got),
    )
    (second_grad,) = call(
        halo_grad_body,
        [((rows, cols, C), bf16)],
        (par, part, ce_halo_a, ce_halo_b, first_low, first_high),
        scratch=[pltpu.VMEM((2, cols, LANES), f32)],
        scalar=True,
    )
    got = swap(square, 0)
    for step in range(1, len(radix)):
        square = square + got
        got = swap(square, step)
    param_count = 9 * K * hid + 3 * hid
    conv_piece, bias_piece, head_piece = call(
        functools.partial(final_body, limit=clip_fraction * param_count ** 0.5),
        [((9, share, K), f32), ((1, share), f32), ((2, share), f32)],
        (square, got, conv_raw, rest_raw),
    )
    first_grad = jnp.concatenate([edge_grad[:1], mid_grad, edge_grad[1:]], axis=0)
    return first_grad, second_grad, jnp.transpose(conv_piece, (0, 2, 1)), bias_piece.reshape(share), head_piece


def solution(mesh):
    return jax.shard_map(
        on_device,
        mesh=mesh,
        in_specs=(
            P("region", "group", None),
            P("region", "group", None),
            P(None, "region", "group"),
            P(None, "group"),
            P(),
            P(),
            P(),
        ),
        out_specs=(
            P("region", "group", None),
            P("region", "group", None),
            P("group", None, "region"),
            P(("group", "region")),
            P("group", "region"),
        ),
        check_vma=False,
    )
```

time: 111 us -> 101 us (0.910)
  starting transfers between devices: 41.9 us -> 35.7 us
  Pallas kernels: 39 us -> 34.4 us
  waiting for transfers between devices: 16.4 us -> 18.4 us
  other arithmetic: 2.02 us -> 0.88 us
    ppermute x18, starting transfers between devices: 41.9 us -> 35.7 us  [permute(): return lax.ppermute(x, 'region', pairs)]
    pallas_call x7 -> x14, Pallas kernels: 39 us -> 34.4 us  [call(): pl.pallas_call(body, out_shape=[jax.ShapeDtypeStruct(s, d) for s, d in ou...]
    unnamed x37 -> x40, local copies, waits for them, and re-layouts: 5.52 us -> 8.05 us
    ppermute x18, waiting for transfers between devices: 16.4 us -> 18.4 us  [permute(): return lax.ppermute(x, 'region', pairs)]
    add x8 -> x3, other arithmetic: 1.99 us -> 0.01 us  [on_device(): square = square + got]
    squeeze x4 -> x0, local copies, waits for them, and re-layouts: 1.15 us -> none  [on_device(): send = lax.dynamic_index_in_dim(halves, 1 - bit, 0, False)]
  transfers between devices with their start and end apart: 18 -> 18, of which waited for: 7 -> 7; matrix products, arithmetic and copies ran while one was open for 7% -> 3% of each run, Pallas kernels for 16% -> 22%
where the time goes in v2:
time: 101 us; the launch traced here: 100 us
  starting transfers between devices  35.7 us (35%)
  Pallas kernels  34.4 us (34%)
  waiting for transfers between devices  18.4 us (18%)
  local copies, waits for them, and re-layouts  9.23 us (9%)
    ppermute x18, starting transfers between devices, permute(): return lax.ppermute(x, 'region', pairs)  35.7 us
    pallas_call x14, Pallas kernels, call(): pl.pallas_call(body, out_shape=[jax.ShapeDtypeStruct(s, d) for s, d in ou...  34.4 us
    ppermute x18, waiting for transfers between devices, permute(): return lax.ppermute(x, 'region', pairs)  18.4 us
    unnamed x40, local copies, waits for them, and re-layouts  8.05 us
  transfers between devices with their start and end apart: 18, of which 7 were waited for; matrix products, arithmetic and copies ran while one was open for 3% of the time, Pallas kernels for 22%

profile of v2, /device:TPU:0, one launch (start us, length us, event | category | flops | bytes accessed | tf_op | source)
XLA Modules:
  0.0 100.0 jit_solution(746031839595383263)
XLA Ops:
  0.7 2.5 %collective-permute-start = (bf16[4,256,256]{2,1,0:T(8,128)(2,1)}, bf16[4,256,256]{2,1,0:T(8,128)(2,1)S(1)}, u32[]{:S(2)}, u32[]{:S(2)}) collective-permute-start(bf16[4,256,256]{2,1,0:T(8,128)(2,1)} %second_ref.3), channel_id=1, source_target_pairs={{0,1},{1,2},{2,3},{3,4},{4,5},{5,6},{6,7},{7,8},{8,9},{9,10},{10,1... | collective-permute-start | bytes 1572872 | tf_op jit(solution)/shard_map/ppermute | solution.py:367
  6.0 2.3 %shard_map.110.old_ref = bf16[4,256,128]{2,1,0:T(8,128)(2,1)S(1)} custom-call(bf16[4,256,256]{2,1,0:T(8,128)(2,1)S(1)} %copy-done.1, bf16[4,256,256]{2,1,0:T(8,128)(2,1)S(1)} %copy-done.2), custom_call_target="tpu_custom_call" | custom-call | tf_op jit(solution)/shard_map/pallas_call | solution.py:46
  9.3 3.8 %shard_map.111 = (bf16[4,256,128]{2,1,0:T(8,128)(2,1)S(1)}, bf16[256,128]{1,0:T(8,128)(2,1)S(1)}, bf16[256,128]{1,0:T(8,128)(2,1)S(1)}) custom-call(s32[1]{0:T(128)} %bitcast.2.par_ref, bf16[4,256,256]{2,1,0:T(8,128)(2,1)S(1)} %copy-done.1, bf16[4,256,128]{2,1,0:T(8,128)(2,1)S(1)} %shard_map.110.old_ref, ...), custom_call_target="tpu_custom_call" | custom-call | tf_op jit(solution)/shard_map/pallas_call | solution.py:46
  13.1 8.6 %collective-permute-start.2 = (bf16[256,128]{1,0:T(8,128)(2,1)S(1)}, bf16[256,128]{1,0:T(8,128)(2,1)S(1)}, u32[]{:S(2)}, u32[]{:S(2)}) collective-permute-start(bf16[256,128]{1,0:T(8,128)(2,1)S(1)} %get-tuple-element.62), channel_id=1, source_target_pairs={{0,1},{1,0},{2,3},{3,2},{4,5},{5,4},{6,7},{7,6},{8,9},{9,8},{10,11... | collective-permute-start | bytes 196616 | tf_op jit(solution)/shard_map/ppermute | solution.py:367
  22.4 2.6 %shard_map.112 = (bf16[4,256,384]{2,1,0:T(8,128)(2,1)S(1)}, f32[2,256,256]{2,1,0:T(8,128)S(1)}, bf16[2,256,256]{2,1,0:T(8,128)(2,1)S(1)}, f32[256,1152]{1,0:T(8,128)S(1)}, f32[16,256]{1,0:T(8,128)S(1)}) custom-call(bf16[4,256,128]{2,1,0:T(8,128)(2,1)S(1)} %get-tuple-element.64.corr_ref, bf16[3,384,256]{2,1,0:T(8,128)(2,1)S(1)} %bitcast.18, ...), custom_call_target="tpu_custom_call" | custom-call | tf_op jit(solution)/shard_map/pallas_call | solution.py:46
  25.0 2.5 %shard_map.113 = (bf16[2,256,256]{2,1,0:T(8,128)(2,1)S(1)}, bf16[256,256]{1,0:T(8,128)(2,1)S(1)}, bf16[256,256]{1,0:T(8,128)(2,1)S(1)}, f32[128,768]{1,0:T(8,128)S(1)}, f32[128,768]{1,0:T(8,128)}) custom-call(s32[1]{0:T(128)} %bitcast.2.par_ref, bf16[4,256,384]{2,1,0:T(8,128)(2,1)S(1)} %get-tuple-element.70.x_ref, ...), custom_call_target="tpu_custom_call" | custom-call | tf_op jit(solution)/shard_map/pallas_call | solution.py:46
  29.5 3.6 %collective-permute-start.4 = (f32[128,768]{1,0:T(8,128)}, f32[128,768]{1,0:T(8,128)}, u32[]{:S(2)}, u32[]{:S(2)}) collective-permute-start(f32[128,768]{1,0:T(8,128)} %get-tuple-element.77), channel_id=1, source_target_pairs={{0,1},{1,0},{2,3},{3,2},{4,5},{5,4},{6,7},{7,6},{8,9},{9,8},{10,11... | collective-permute-start | bytes 1179656 | tf_op jit(solution)/shard_map/ppermute | solution.py:367
  33.2 1.7 %collective-permute-done.4.got_ref = f32[128,768]{1,0:T(8,128)} collective-permute-done((f32[128,768]{1,0:T(8,128)}, f32[128,768]{1,0:T(8,128)}, u32[]{:S(2)}, u32[]{:S(2)}) %collective-permute-start.4) | collective-permute-done | bytes 393248 | tf_op jit(solution)/shard_map/ppermute | solution.py:367
  34.9 1.7 %shard_map.114 = (f32[64,768]{1,0:T(8,128)S(1)}, f32[64,768]{1,0:T(8,128)}) custom-call(s32[1]{0:T(128)} %bitcast.1.bit_ref, f32[128,768]{1,0:T(8,128)S(1)} %get-tuple-element.76.own_ref, f32[128,768]{1,0:T(8,128)} %collective-permute-done.4.got_ref), custom_call_target="tpu_custom_call" | custom-call | tf_op jit(solution)/shard_map/pallas_call | solution.py:46
  37.3 2.3 %collective-permute-start.5 = (f32[64,768]{1,0:T(8,128)}, f32[64,768]{1,0:T(8,128)}, u32[]{:S(2)}, u32[]{:S(2)}) collective-permute-start(f32[64,768]{1,0:T(8,128)} %get-tuple-element.79), channel_id=1, source_target_pairs={{0,2},{1,3},{2,0},{3,1},{4,6},{5,7},{6,4},{7,5},{8,10},{9,11},{10,... | collective-permute-start | bytes 589832 | tf_op jit(solution)/shard_map/ppermute | solution.py:367
  44.5 4.1 %shard_map.116 = (bf16[2,256,256]{2,1,0:T(8,128)(2,1)S(1)}, f32[4,256,256]{2,1,0:T(8,128)S(1)}) custom-call(bf16[2,256,128]{2,1,0:T(8,128)(2,1)S(1)} %get-tuple-element.83.ce_ref.mid_ref, bf16[4,256,256]{2,1,0:T(8,128)(2,1)S(1)} %copy-done.1, bf16[4,256,256]{2,1,0:T(8,128)(2,1)S(1)} %copy-done.2, bf16[4,256,256]{2,1,0:T(8,128)(2,1)S(1)} %collective-permute-done.low_ref, ...), custom_call_target="tpu_custom_call" | custom-call | tf_op jit(solution)/shard_map/pallas_call | solution.py:46
  49.5 1.6 %shard_map.117 = (f32[32,768]{1,0:T(8,128)S(1)}, f32[32,768]{1,0:T(8,128)}) custom-call(s32[1]{0:T(128)} %bitcast.bit_ref, f32[64,768]{1,0:T(8,128)S(1)} %copy-done.12, f32[64,768]{1,0:T(8,128)} %collective-permute-done.5.got_ref), custom_call_target="tpu_custom_call" | custom-call | tf_op jit(solution)/shard_map/pallas_call | solution.py:46
  51.8 3.8 %collective-permute-start.12 = (bf16[4,256,256]{2,1,0:T(8,128)(2,1)S(1)}, bf16[4,256,256]{2,1,0:T(8,128)(2,1)}, u32[]{:S(2)}, u32[]{:S(2)}) collective-permute-start(bf16[4,256,256]{2,1,0:T(8,128)(2,1)S(1)} %copy-done.1), channel_id=1, source_target_pairs={{0,1},{1,2},{2,3},{3,4},{4,5},{5,6},{6,7},{7,8},{8,9},{9,10},{10,1... | collective-permute-start | bytes 1572872 | tf_op jit(solution)/shard_map/ppermute | solution.py:367
  55.6 1.5 %collective-permute-start.13 = (bf16[4,256,256]{2,1,0:T(8,128)(2,1)S(1)}, bf16[4,256,256]{2,1,0:T(8,128)(2,1)}, u32[]{:S(2)}, u32[]{:S(2)}) collective-permute-start(bf16[4,256,256]{2,1,0:T(8,128)(2,1)S(1)} %copy-done.1), channel_id=1, source_target_pairs={{1,0},{2,1},{3,2},{4,3},{5,4},{6,5},{7,6},{8,7},{9,8},{10,9},{11,1... | collective-permute-start | bytes 1572872 | tf_op jit(solution)/shard_map/ppermute | solution.py:367
  57.0 3.7 %collective-permute-start.6 = (f32[32,768]{1,0:T(8,128)}, f32[32,768]{1,0:T(8,128)}, u32[]{:S(2)}, u32[]{:S(2)}) collective-permute-start(f32[32,768]{1,0:T(8,128)} %get-tuple-element.86), channel_id=1, source_target_pairs={{0,4},{1,5},{2,6},{3,7},{4,0},{5,1},{6,2},{7,3},{8,12},{9,13},{10,... | collective-permute-start | bytes 294920 | tf_op jit(solution)/shard_map/ppermute | solution.py:367
  61.8 1.4 %shard_map.118 = (bf16[2,256,128]{2,1,0:T(8,128)(2,1)S(1)}, bf16[256,128]{1,0:T(8,128)(2,1)S(1)}, bf16[256,128]{1,0:T(8,128)(2,1)S(1)}) custom-call(s32[1]{0:T(128)} %bitcast.2.par_ref, bf16[2,256,128]{2,1,0:T(8,128)(2,1)S(1)} %get-tuple-element.83.ce_ref.mid_ref, f32[2,256,128]{2,1,0:T(8,128)S(1)} %copy-done.10, ...), custom_call_target="tpu_custom_call" | custom-call | tf_op jit(solution)/shard_map/pallas_call | solution.py:46
  63.2 6.6 %collective-permute-done.6.got_ref = f32[32,768]{1,0:T(8,128)} collective-permute-done((f32[32,768]{1,0:T(8,128)}, f32[32,768]{1,0:T(8,128)}, u32[]{:S(2)}, u32[]{:S(2)}) %collective-permute-start.6) | collective-permute-done | bytes 98336 | tf_op jit(solution)/shard_map/ppermute | solution.py:367
  70.7 3.1 %collective-permute-start.9 = (f32[16,768]{1,0:T(8,128)S(1)}, f32[16,768]{1,0:T(8,128)S(1)}, u32[]{:S(2)}, u32[]{:S(2)}) collective-permute-start(f32[16,768]{1,0:T(8,128)S(1)} %get-tuple-element.95), channel_id=1, source_target_pairs={{0,8},{1,9},{2,10},{3,11},{4,12},{5,13},{6,14},{7,15},{8,0},{9,1},... | collective-permute-start | bytes 147464 | tf_op jit(solution)/shard_map/ppermute | solution.py:367
  73.9 7.1 %shard_map.120 = (bf16[2,256,256]{2,1,0:T(8,128)(2,1)S(1)}, f32[4,256,256]{2,1,0:T(8,128)S(1)}) custom-call(bf16[2,256,128]{2,1,0:T(8,128)(2,1)S(1)} %get-tuple-element.96.ce_ref, f32[4,256,256]{2,1,0:T(8,128)S(1)} %copy-done.4, bf16[4,256,256]{2,1,0:T(8,128)(2,1)S(1)} %copy-done.1, bf16[4,256,256]{2,1,0:T(8,128)(2,1)S(1)} %copy-done.2, ...), custom_call_target="tpu_custom_call" | custom-call | tf_op jit(solution)/shard_map/pallas_call | solution.py:46
  83.2 2.8 %collective-permute-done.15 = f32[8,128]{1,0:T(8,128)S(1)} collective-permute-done((f32[8,128]{1,0:T(8,128)S(1)}, f32[8,128]{1,0:T(8,128)S(1)}, u32[]{:S(2)}, u32[]{:S(2)}) %collective-permute-start.15) | collective-permute-done | bytes 4128 | tf_op jit(solution)/shard_map/ppermute | solution.py:367
  86.0 2.0 %collective-permute-start.16 = (f32[8,128]{1,0:T(8,128)S(1)}, f32[8,128]{1,0:T(8,128)S(1)}, u32[]{:S(2)}, u32[]{:S(2)}) collective-permute-start(f32[8,128]{1,0:T(8,128)S(1)} %add.50), channel_id=1, source_target_pairs={{0,4},{1,5},{2,6},{3,7},{4,0},{5,1},{6,2},{7,3},{8,12},{9,13},{10,... | collective-permute-start | bytes 12296 | tf_op jit(solution)/shard_map/ppermute | solution.py:367
  88.0 2.2 %collective-permute-done.16 = f32[8,128]{1,0:T(8,128)S(1)} collective-permute-done((f32[8,128]{1,0:T(8,128)S(1)}, f32[8,128]{1,0:T(8,128)S(1)}, u32[]{:S(2)}, u32[]{:S(2)}) %collective-permute-start.16) | collective-permute-done | bytes 4128 | tf_op jit(solution)/shard_map/ppermute | solution.py:367
  91.5 3.2 %collective-permute-done.17.got_ref = f32[8,128]{1,0:T(8,128)S(1)} collective-permute-done((f32[8,128]{1,0:T(8,128)S(1)}, f32[8,128]{1,0:T(8,128)S(1)}, u32[]{:S(2)}, u32[]{:S(2)}) %collective-permute-start.17) | collective-permute-done | bytes 4128 | tf_op jit(solution)/shard_map/ppermute | solution.py:367
  95.4 4.6 %shard_map.121 = bf16[4,256,256]{2,1,0:T(8,128)(2,1)} custom-call(s32[1]{0:T(128)} %bitcast.2.par_ref, f32[4,256,256]{2,1,0:T(8,128)S(1)} %get-tuple-element.101.part_ref, bf16[256,128]{1,0:T(8,128)(2,1)S(1)} %collective-permute-done.10.ca_ref, bf16[256,128]{1,0:T(8,128)(2,1)S(1)} %collective-permute-done.11.cb_ref, ...), custom_call_target="tpu_custom_call" | custom-call | tf_op jit(solution)/shard_map/pallas_call | solution.py:46
  (84 shorter events, 19.8 us)
Async XLA Ops:
  0.6 5.4 %copy-start.2 = (bf16[4,256,256]{2,1,0:T(8,128)(2,1)S(1)}, bf16[4,256,256]{2,1,0:T(8,128)(2,1)}, u32[]{:S(2)}) copy-start(bf16[4,256,256]{2,1,0:T(8,128)(2,1)} %second_ref.3) | copy-start | bytes 1572868
  0.7 5.2 %copy-start.19 = (bf16[2,256]{1,0:T(2,128)(2,1)S(1)}, bf16[2,256]{1,0:T(2,128)(2,1)}, u32[]{:S(2)}) copy-start(bf16[2,256]{1,0:T(2,128)(2,1)} %param.13) | copy-start | bytes 3076
  0.7 5.4 %copy-start.1 = (bf16[4,256,256]{2,1,0:T(8,128)(2,1)S(1)}, bf16[4,256,256]{2,1,0:T(8,128)(2,1)}, u32[]{:S(2)}) copy-start(bf16[4,256,256]{2,1,0:T(8,128)(2,1)} %first_ref.7) | copy-start | bytes 1572868
  0.7 7.8 %collective-permute-start = (bf16[4,256,256]{2,1,0:T(8,128)(2,1)}, bf16[4,256,256]{2,1,0:T(8,128)(2,1)S(1)}, u32[]{:S(2)}, u32[]{:S(2)}) collective-permute-start(bf16[4,256,256]{2,1,0:T(8,128)(2,1)} %second_ref.3), channel_id=1, source_target_pairs={{0,1},{1,2},{2,3},{3,4},{4,5},{5,6},{6,7},{7,8},{8,9},{9,10},{10,1... | collective-permute-start | bytes 1572872 | tf_op jit(solution)/shard_map/ppermute | solution.py:367
  3.2 6.1 %collective-permute-start.1 = (bf16[4,256,256]{2,1,0:T(8,128)(2,1)}, bf16[4,256,256]{2,1,0:T(8,128)(2,1)S(1)}, u32[]{:S(2)}, u32[]{:S(2)}) collective-permute-start(bf16[4,256,256]{2,1,0:T(8,128)(2,1)} %second_ref.3), channel_id=1, source_target_pairs={{1,0},{2,1},{3,2},{4,3},{5,4},{6,5},{7,6},{8,7},{9,8},{10,9},{11,1... | collective-permute-start | bytes 1572872 | tf_op jit(solution)/shard_map/ppermute | solution.py:367
  8.3 14.1 %copy-start.15 = (f32[2,4,256]{2,1,0:T(4,128)S(1)}, f32[2,4,256]{2,1,0:T(4,128)}, u32[]{:S(2)}) copy-start(f32[2,4,256]{2,1,0:T(4,128)} %target_ref.3) | copy-start | bytes 24580
  13.1 11.9 %collective-permute-start.2 = (bf16[256,128]{1,0:T(8,128)(2,1)S(1)}, bf16[256,128]{1,0:T(8,128)(2,1)S(1)}, u32[]{:S(2)}, u32[]{:S(2)}) collective-permute-start(bf16[256,128]{1,0:T(8,128)(2,1)S(1)} %get-tuple-element.62), channel_id=1, source_target_pairs={{0,1},{1,0},{2,3},{3,2},{4,5},{5,4},{6,7},{7,6},{8,9},{9,8},{10,11... | collective-permute-start | bytes 196616 | tf_op jit(solution)/shard_map/ppermute | solution.py:367
  21.7 3.3 %collective-permute-start.3 = (bf16[256,128]{1,0:T(8,128)(2,1)S(1)}, bf16[256,128]{1,0:T(8,128)(2,1)S(1)}, u32[]{:S(2)}, u32[]{:S(2)}) collective-permute-start(bf16[256,128]{1,0:T(8,128)(2,1)S(1)} %get-tuple-element.63), channel_id=1, source_target_pairs={{1,2},{3,4},{5,6},{7,8},{9,10},{11,12},{13,14},{2,1},{4,3},{6,5},{... | collective-permute-start | bytes 196616 | tf_op jit(solution)/shard_map/ppermute | solution.py:367
  29.5 5.3 %collective-permute-start.4 = (f32[128,768]{1,0:T(8,128)}, f32[128,768]{1,0:T(8,128)}, u32[]{:S(2)}, u32[]{:S(2)}) collective-permute-start(f32[128,768]{1,0:T(8,128)} %get-tuple-element.77), channel_id=1, source_target_pairs={{0,1},{1,0},{2,3},{3,2},{4,5},{5,4},{6,7},{7,6},{8,9},{9,8},{10,11... | collective-permute-start | bytes 1179656 | tf_op jit(solution)/shard_map/ppermute | solution.py:367
  37.3 12.2 %collective-permute-start.5 = (f32[64,768]{1,0:T(8,128)}, f32[64,768]{1,0:T(8,128)}, u32[]{:S(2)}, u32[]{:S(2)}) collective-permute-start(f32[64,768]{1,0:T(8,128)} %get-tuple-element.79), channel_id=1, source_target_pairs={{0,2},{1,3},{2,0},{3,1},{4,6},{5,7},{6,4},{7,5},{8,10},{9,11},{10,... | collective-permute-start | bytes 589832 | tf_op jit(solution)/shard_map/ppermute | solution.py:367
  39.6 21.1 %collective-permute-start.7 = (bf16[256,256]{1,0:T(8,128)(2,1)}, bf16[256,256]{1,0:T(8,128)(2,1)}, u32[]{:S(2)}, u32[]{:S(2)}) collective-permute-start(bf16[256,256]{1,0:T(8,128)(2,1)} %copy-done.17), channel_id=1, source_target_pairs={{0,1},{1,0},{2,3},{3,2},{4,5},{5,4},{6,7},{7,6},{8,9},{9,8},{10,11... | collective-permute-start | bytes 393224 | tf_op jit(solution)/shard_map/ppermute | solution.py:367
  39.7 21.0 %collective-permute-start.8 = (bf16[256,256]{1,0:T(8,128)(2,1)}, bf16[256,256]{1,0:T(8,128)(2,1)}, u32[]{:S(2)}, u32[]{:S(2)}) collective-permute-start(bf16[256,256]{1,0:T(8,128)(2,1)} %copy-done.16), channel_id=1, source_target_pairs={{1,2},{3,4},{5,6},{7,8},{9,10},{11,12},{13,14},{2,1},{4,3},{6,5},{... | collective-permute-start | bytes 393224 | tf_op jit(solution)/shard_map/ppermute | solution.py:367
  51.8 43.6 %collective-permute-start.12 = (bf16[4,256,256]{2,1,0:T(8,128)(2,1)S(1)}, bf16[4,256,256]{2,1,0:T(8,128)(2,1)}, u32[]{:S(2)}, u32[]{:S(2)}) collective-permute-start(bf16[4,256,256]{2,1,0:T(8,128)(2,1)S(1)} %copy-done.1), channel_id=1, source_target_pairs={{0,1},{1,2},{2,3},{3,4},{4,5},{5,6},{6,7},{7,8},{8,9},{9,10},{10,1... | collective-permute-start | bytes 1572872 | tf_op jit(solution)/shard_map/ppermute | solution.py:367
  55.6 39.8 %collective-permute-start.13 = (bf16[4,256,256]{2,1,0:T(8,128)(2,1)S(1)}, bf16[4,256,256]{2,1,0:T(8,128)(2,1)}, u32[]{:S(2)}, u32[]{:S(2)}) collective-permute-start(bf16[4,256,256]{2,1,0:T(8,128)(2,1)S(1)} %copy-done.1), channel_id=1, source_target_pairs={{1,0},{2,1},{3,2},{4,3},{5,4},{6,5},{7,6},{8,7},{9,8},{10,9},{11,1... | collective-permute-start | bytes 1572872 | tf_op jit(solution)/shard_map/ppermute | solution.py:367
  57.0 12.8 %collective-permute-start.6 = (f32[32,768]{1,0:T(8,128)}, f32[32,768]{1,0:T(8,128)}, u32[]{:S(2)}, u32[]{:S(2)}) collective-permute-start(f32[32,768]{1,0:T(8,128)} %get-tuple-element.86), channel_id=1, source_target_pairs={{0,4},{1,5},{2,6},{3,7},{4,0},{5,1},{6,2},{7,3},{8,12},{9,13},{10,... | collective-permute-start | bytes 294920 | tf_op jit(solution)/shard_map/ppermute | solution.py:367
  60.7 13.2 %copy-start.4 = (f32[4,256,256]{2,1,0:T(8,128)S(1)}, f32[4,256,256]{2,1,0:T(8,128)}, u32[]{:S(2)}) copy-start(f32[4,256,256]{2,1,0:T(8,128)} %copy-done.3) | copy-start | bytes 3145732
  61.8 8.1 %copy-start.14 = (f32[32,768]{1,0:T(8,128)S(1)}, f32[32,768]{1,0:T(8,128)}, u32[]{:S(2)}) copy-start(f32[32,768]{1,0:T(8,128)} %copy-done.13) | copy-start | bytes 294916
  70.7 10.3 %collective-permute-start.9 = (f32[16,768]{1,0:T(8,128)S(1)}, f32[16,768]{1,0:T(8,128)S(1)}, u32[]{:S(2)}, u32[]{:S(2)}) collective-permute-start(f32[16,768]{1,0:T(8,128)S(1)} %get-tuple-element.95), channel_id=1, source_target_pairs={{0,8},{1,9},{2,10},{3,11},{4,12},{5,13},{6,14},{7,15},{8,0},{9,1},... | collective-permute-start | bytes 147464 | tf_op jit(solution)/shard_map/ppermute | solution.py:367
  81.2 1.2 %collective-permute-start.14 = (f32[8,128]{1,0:T(8,128)S(1)}, f32[8,128]{1,0:T(8,128)S(1)}, u32[]{:S(2)}, u32[]{:S(2)}) collective-permute-start(f32[8,128]{1,0:T(8,128)S(1)} %get-tuple-element.107), channel_id=1, source_target_pairs={{0,1},{1,0},{2,3},{3,2},{4,5},{5,4},{6,7},{7,6},{8,9},{9,8},{10,11... | collective-permute-start | bytes 12296 | tf_op jit(solution)/shard_map/ppermute | solution.py:367
  82.4 3.6 %collective-permute-start.15 = (f32[8,128]{1,0:T(8,128)S(1)}, f32[8,128]{1,0:T(8,128)S(1)}, u32[]{:S(2)}, u32[]{:S(2)}) collective-permute-start(f32[8,128]{1,0:T(8,128)S(1)} %add.49), channel_id=1, source_target_pairs={{0,2},{1,3},{2,0},{3,1},{4,6},{5,7},{6,4},{7,5},{8,10},{9,11},{10,... | collective-permute-start | bytes 12296 | tf_op jit(solution)/shard_map/ppermute | solution.py:367
  82.4 13.0 %collective-permute-start.10 = (bf16[256,128]{1,0:T(8,128)(2,1)S(1)}, bf16[256,128]{1,0:T(8,128)(2,1)S(1)}, u32[]{:S(2)}, u32[]{:S(2)}) collective-permute-start(bf16[256,128]{1,0:T(8,128)(2,1)S(1)} %get-tuple-element.102), channel_id=1, source_target_pairs={{0,1},{1,0},{2,3},{3,2},{4,5},{5,4},{6,7},{7,6},{8,9},{9,8},{10,11... | collective-permute-start | bytes 196616 | tf_op jit(solution)/shard_map/ppermute | solution.py:367
  82.6 12.8 %collective-permute-start.11 = (bf16[256,128]{1,0:T(8,128)(2,1)S(1)}, bf16[256,128]{1,0:T(8,128)(2,1)S(1)}, u32[]{:S(2)}, u32[]{:S(2)}) collective-permute-start(bf16[256,128]{1,0:T(8,128)(2,1)S(1)} %get-tuple-element.103), channel_id=1, source_target_pairs={{1,2},{3,4},{5,6},{7,8},{9,10},{11,12},{13,14},{2,1},{4,3},{6,5},{... | collective-permute-start | bytes 196616 | tf_op jit(solution)/shard_map/ppermute | solution.py:367
  86.0 4.2 %collective-permute-start.16 = (f32[8,128]{1,0:T(8,128)S(1)}, f32[8,128]{1,0:T(8,128)S(1)}, u32[]{:S(2)}, u32[]{:S(2)}) collective-permute-start(f32[8,128]{1,0:T(8,128)S(1)} %add.50), channel_id=1, source_target_pairs={{0,4},{1,5},{2,6},{3,7},{4,0},{5,1},{6,2},{7,3},{8,12},{9,13},{10,... | collective-permute-start | bytes 12296 | tf_op jit(solution)/shard_map/ppermute | solution.py:367
  90.2 4.5 %collective-permute-start.17 = (f32[8,128]{1,0:T(8,128)S(1)}, f32[8,128]{1,0:T(8,128)S(1)}, u32[]{:S(2)}, u32[]{:S(2)}) collective-permute-start(f32[8,128]{1,0:T(8,128)S(1)} %add.51.sq_ref), channel_id=1, source_target_pairs={{0,8},{1,9},{2,10},{3,11},{4,12},{5,13},{6,14},{7,15},{8,0},{9,1},... | collective-permute-start | bytes 12296 | tf_op jit(solution)/shard_map/ppermute | solution.py:367
  (14 other events, 23.0 us)

commit v3 on v2

--- a/solution.py
+++ b/solution.py
@@ -39,7 +39,7 @@
 VMEM = pl.BlockSpec(memory_space=pltpu.VMEM)
 
 
-def call(body, outs, args, scratch=(), scalar=False):
+def call(body, outs, args, scratch=(), scalar=False, alias=None):
     specs = [VMEM] * len(args)
     if scalar:
         specs[0] = SMEM
@@ -49,6 +49,7 @@
         in_specs=specs,
         out_specs=[VMEM] * len(outs),
         scratch_shapes=list(scratch),
+        input_output_aliases=alias or {},
         compiler_params=pltpu.CompilerParams(vmem_limit_bytes=VMEM_LIMIT),
     )(*args)
 
@@ -123,7 +124,7 @@
 
 def corr_halo_body(par_ref, first_ref, old_ref, low_ref, high_ref, corr_ref, ea_ref, eb_ref, mid_ref):
     rows = first_ref.shape[0]
-    par = par_ref[0]
+    par = par_ref[0] & 1
     corr_rows(first_ref, low_ref, -low_ref.shape[0], old_ref, lambda r, v: mid_ref.__setitem__(r, v))
     corr_rows(first_ref, high_ref, rows, mid_ref, lambda r, v: corr_ref.__setitem__(r, v))
     ea_ref[...] = corr_ref[(1 - par) * (rows - 1)]
@@ -180,7 +181,7 @@
                    pe_ref, pa_ref, pb_ref, keep_ref, send_ref, h_ref, pt_ref):
     rows, cols = x_ref.shape[0], x_ref.shape[1]
     hid = w_ref.shape[2]
-    par = par_ref[0]
+    par = par_ref[0] & 1
     put_taps(h_ref, 1 - par, ha_ref[...])
     put_taps(h_ref, par, hb_ref[...])
     head = head_ref[...]
@@ -212,13 +213,17 @@
     send_ref[...] = jnp.where(par == 0, lower, upper)
 
 
-def halve_body(bit_ref, own_ref, got_ref, keep_ref, send_ref):
+def halve_body(index_ref, own_ref, got_ref, keep_ref, send_ref, *, step):
     half = keep_ref.shape[0]
-    bit = bit_ref[0]
+    bit = (index_ref[0] >> step) & 1
     upper = own_ref[:half] + got_ref[:half]
     lower = own_ref[half:] + got_ref[half:]
     keep_ref[...] = jnp.where(bit == 0, upper, lower)
     send_ref[...] = jnp.where(bit == 0, lower, upper)
+
+
+def add_body(own_ref, got_ref, out_ref):
+    out_ref[...] = own_ref[...] + got_ref[...]
 
 
 def tail_body(own_ref, got_ref, conv_ref, rest_ref, square_ref):
@@ -261,7 +266,7 @@
 def cerr_edge_body(par_ref, mid_ref, rest_ref, ha_ref, hb_ref, w_ref, ce_ref, ea_ref, eb_ref, h_ref):
     rows = mid_ref.shape[0] + 2
     cols = mid_ref.shape[1]
-    par = par_ref[0]
+    par = par_ref[0] & 1
     h_ref[1 - par] = ha_ref[...]
     h_ref[par] = hb_ref[...]
     valid = lane_valid(cols)
@@ -297,58 +302,54 @@
         eb_ref[...] = down
 
 
-def row_grad(cerr, own_rows, first_ref, second_ref, low_ref, high_ref, fg_ref, part_ref, old_ref):
+def row_grad_body(ce_ref, first_ref, second_ref, low_ref, high_ref, *refs, r, at, done):
+    fg_ref, part_ref = refs[-2:]
+    old_ref = refs[0] if len(refs) > 2 else None
     rows, cols = first_ref.shape[0], first_ref.shape[1]
-    parts = [None if old_ref is None else old_ref[q] for q in range(rows)]
-    for i, r in enumerate(own_rows):
-        bands = cerr[i].astype(f32)
-        turned = first_ref[r].T
-        acc = jnp.zeros((cols, C), f32)
-        for dyi in range(WIN):
-            q = r + dyi - RADIUS
-            src = low_ref[q + RADIUS] if q < 0 else (high_ref[q - rows] if q >= rows else second_ref[q])
-            spread = spread_of(bands, dyi)
-            acc = acc + dot(spread, src)
-            if 0 <= q < rows:
-                gave = dot(turned, spread)
-                parts[q] = gave if parts[q] is None else parts[q] + gave
-        fg_ref[i] = acc.astype(bf16)
+    bands = ce_ref[at].astype(f32)
+    turned = first_ref[r].T
+    acc = jnp.zeros((cols, C), f32)
+    for dyi in range(WIN):
+        q = r + dyi - RADIUS
+        src = low_ref[q + RADIUS] if q < 0 else (high_ref[q - rows] if q >= rows else second_ref[q])
+        spread = spread_of(bands, dyi)
+        acc = acc + dot(spread, src)
+        if 0 <= q < rows:
+            gave = dot(turned, spread)
+            part_ref[q] = gave if old_ref is None else old_ref[q] + gave
+    fg_ref[r if done else 0] = acc.astype(bf16)
+    for other, row_ref in zip(done, refs[1:]):
+        fg_ref[other] = row_ref[0]
+
+
+def halo_part(bands, rows_ref, dys_of, old_ref):
+    rows = old_ref.shape[0]
+    parts = [old_ref[q] for q in range(rows)]
+    slot = 0
+    for r in range(rows):
+        turned = rows_ref[r].T
+        for q in dys_of(r):
+            parts[q] = parts[q] + dot(turned, spread_of(bands, slot))
+            slot += 1
+    return parts
+
+
+def halo_above_body(index_ref, ca_ref, cb_ref, low_ref, old_ref, part_ref):
+    par = index_ref[0] & 1
+    rows = part_ref.shape[0]
+    bands = jnp.where(par == 0, cb_ref[...].astype(f32), ca_ref[...].astype(f32))
+    parts = halo_part(bands, low_ref, lambda a: range(0, a + RADIUS + 1 - rows), old_ref)
     for q in range(rows):
         part_ref[q] = parts[q]
 
 
-def mid_grad_body(ce_ref, first_ref, second_ref, low_ref, high_ref, fg_ref, part_ref):
-    row_grad(ce_ref, range(1, first_ref.shape[0] - 1), first_ref, second_ref, low_ref, high_ref, fg_ref, part_ref, None)
-
-
-def edge_grad_body(ce_ref, old_ref, first_ref, second_ref, low_ref, high_ref, fg_ref, part_ref):
-    row_grad(ce_ref, (0, first_ref.shape[0] - 1), first_ref, second_ref, low_ref, high_ref, fg_ref, part_ref, old_ref)
-
-
-def halo_grad_body(par_ref, part_ref, ca_ref, cb_ref, low_ref, high_ref, sg_ref, c_ref):
-    rows, cols = part_ref.shape[0], part_ref.shape[2]
-    par = par_ref[0]
-    c_ref[1 - par] = ca_ref[...].astype(f32)
-    c_ref[par] = cb_ref[...].astype(f32)
-    parts = [part_ref[r] for r in range(rows)]
-    above = c_ref[0]
-    below = c_ref[1]
-    at = 0
-    for a in range(rows):
-        turned = low_ref[a].T
-        for i, dy in enumerate(range(rows - a, RADIUS + 1)):
-            q = a + dy - rows
-            parts[q] = parts[q] + dot(turned, spread_of(above, at // 9 + i))
-        at += 9 * (RADIUS + 1 - rows + a)
-    at = 0
-    for b in range(rows):
-        turned = high_ref[b].T
-        for i, dy in enumerate(range(-RADIUS, -b)):
-            q = rows + b + dy
-            parts[q] = parts[q] + dot(turned, spread_of(below, at // 9 + i))
-        at += 9 * (RADIUS - b)
-    for r in range(rows):
-        sg_ref[r] = parts[r].T.astype(bf16)
+def halo_below_body(index_ref, ca_ref, cb_ref, high_ref, part_ref, sg_ref):
+    par = index_ref[0] & 1
+    rows = part_ref.shape[0]
+    bands = jnp.where(par == 0, ca_ref[...].astype(f32), cb_ref[...].astype(f32))
+    parts = halo_part(bands, high_ref, lambda b: range(rows + b - RADIUS, rows), part_ref)
+    for q in range(rows):
+        sg_ref[q] = parts[q].T.astype(bf16)
 
 
 def on_device(first_map, second_map, flow_target, valid_tiles, conv_weight, conv_bias, head_weight):
@@ -356,7 +357,7 @@
     hid = conv_weight.shape[2]
     count = lax.axis_size("region")
     index = lax.axis_index("region")
-    par = (index % 2).reshape(1)
+    par = index.reshape(1)
     forward = [(i, i + 1) for i in range(count - 1)]
     backward = [(b, a) for a, b in forward]
     inner = [(i, i ^ 1) for i in range(count)]
@@ -424,27 +425,35 @@
 
     def halve(step, keep, got):
         half = keep.shape[0] // 2
-        bit = ((index >> step) & 1).reshape(1)
-        return call(halve_body, [((half, WIDTH), f32)] * 2, (bit, keep, got), scalar=True)
-
+        return call(functools.partial(halve_body, step=step), [((half, WIDTH), f32)] * 2, (par, keep, got), scalar=True)
+
+    def row_grad(r, at, cerr, part, done=()):
+        args = (cerr, first_map, second_map, second_low, second_high)
+        if part is not None:
+            args = args + (part,) + tuple(row for _, row in done)
+        return call(
+            functools.partial(row_grad_body, r=r, at=at, done=[other for other, _ in done]),
+            [((rows if done else 1, cols, C), bf16), ((rows, C, cols), f32)],
+            args,
+            alias=None if part is None else {5: 1},
+        )
+
+    steps = len(radix)
     keep, send = halve(1, keep, got)
     got = swap(send, 1)
     ce_mid, ce_rest = call(
         cerr_own_body,
         [((rows - 2, cols, LANES), bf16), ((2, cols, LANES), f32)],
-        (pe_mid, pe_edge, weight),
-    )
-    mid_grad, part = call(
-        mid_grad_body,
-        [((rows - 2, cols, C), bf16), ((rows, C, cols), f32)],
-        (after(ce_mid, send), first_map, second_map, second_low, second_high),
-    )
+        (after(pe_mid, send), pe_edge, weight),
+    )
+    part = None
+    done = []
+    for r in range(1, rows - 1):
+        row, part = row_grad(r, r - 1, ce_mid, part)
+        done.append((r, row))
     got, part = lax.optimization_barrier((got, part))
     keep, send = halve(2, keep, got)
     got = swap(send, 2)
-    first_tied = after(first_map, send)
-    first_low = permute(first_tied, forward)
-    first_high = permute(first_tied, backward)
     ce_edge, ce_a, ce_b = call(
         cerr_edge_body,
         [((2, cols, LANES), bf16), ((cols, LANES), bf16), ((cols, LANES), bf16)],
@@ -454,31 +463,48 @@
     )
     ce_halo_a = permute(ce_a, inner)
     ce_halo_b = permute(ce_b, outer)
-    got, ce_edge = lax.optimization_barrier((got, ce_edge))
-    for step in range(3, len(radix)):
+    first_tied = after(first_map, ce_a)
+    first_low = permute(first_tied, forward)
+    first_high = permute(first_tied, backward)
+    row, part = row_grad(0, 0, ce_edge, part)
+    done.append((0, row))
+    got, part = lax.optimization_barrier((got, part))
+    for step in range(3, steps):
         keep, send = halve(step, keep, got)
         got = swap(send, step)
-    edge_grad, part = call(
-        edge_grad_body,
-        [((2, cols, C), bf16), ((rows, C, cols), f32)],
-        (after(ce_edge, send), part, first_map, second_map, second_low, second_high),
-    )
-    got, part = lax.optimization_barrier((got, part))
+    first_grad, part = row_grad(rows - 1, 1, after(ce_edge, send), part, done)
+    got, part, ce_halo_a, ce_halo_b = lax.optimization_barrier((got, part, ce_halo_a, ce_halo_b))
     conv_raw, rest_raw, square = call(
         tail_body,
         [((9, share, K), f32), ((3, share), f32), ((8, LANES), f32)],
         (keep, got),
     )
+
+    def add(x, y):
+        return call(add_body, [((8, LANES), f32)], (x, y))[0]
+
+    got = swap(square, 0)
+    square = add(square, got)
+    got = swap(square, 1)
+    (part,) = call(
+        halo_above_body,
+        [((rows, C, cols), f32)],
+        (par, after(ce_halo_a, square), ce_halo_b, first_low, part),
+        scalar=True,
+        alias={4: 0},
+    )
+    got, part = lax.optimization_barrier((got, part))
+    square = add(square, got)
+    got = swap(square, 2)
     (second_grad,) = call(
-        halo_grad_body,
+        halo_below_body,
         [((rows, cols, C), bf16)],
-        (par, part, ce_halo_a, ce_halo_b, first_low, first_high),
-        scratch=[pltpu.VMEM((2, cols, LANES), f32)],
+        (par, after(ce_halo_a, square), ce_halo_b, first_high, part),
         scalar=True,
     )
-    got = swap(square, 0)
-    for step in range(1, len(radix)):
-        square = square + got
+    got, second_grad = lax.optimization_barrier((got, second_grad))
+    for step in range(3, steps):
+        square = add(square, got)
         got = swap(square, step)
     param_count = 9 * K * hid + 3 * hid
     conv_piece, bias_piece, head_piece = call(
@@ -486,7 +512,6 @@
         [((9, share, K), f32), ((1, share), f32), ((2, share), f32)],
         (square, got, conv_raw, rest_raw),
     )
-    first_grad = jnp.concatenate([edge_grad[:1], mid_grad, edge_grad[1:]], axis=0)
     return first_grad, second_grad, jnp.transpose(conv_piece, (0, 2, 1)), bias_piece.reshape(share), head_piece
 
 

time: 101 us -> 79.6 us (0.79)
  Pallas kernels: 34.4 us -> 21.9 us
  local copies, waits for them, and re-layouts: 9.23 us -> 3.96 us
  waiting for transfers between devices: 18.4 us -> 16 us
    pallas_call x14 -> x20, Pallas kernels: 34.4 us -> 21.9 us  [call(): pl.pallas_call(body, out_shape=[jax.ShapeDtypeStruct(s, d) for s, d in ou...]
    unnamed x40 -> x14, local copies, waits for them, and re-layouts: 8.05 us -> 2.12 us
    ppermute x18, waiting for transfers between devices: 18.4 us -> 16 us  [permute(): return lax.ppermute(x, 'region', pairs)]
  transfers between devices with their start and end apart: 18 -> 18, of which waited for: 7 -> 8; matrix products, arithmetic and copies ran while one was open for 3% -> 3% of each run, Pallas kernels for 22% -> 19%
where the time goes in v3:
time: 79.6 us; the launch traced here: 79.2 us
  starting transfers between devices  35.9 us (45%)
  Pallas kernels  21.9 us (28%)
  waiting for transfers between devices  16 us (20%)
  local copies, waits for them, and re-layouts  3.96 us (5%)
  between operations  0.96 us (1%)
    ppermute x18, starting transfers between devices, permute(): return lax.ppermute(x, 'region', pairs)  35.9 us
    pallas_call x20, Pallas kernels, call(): pl.pallas_call(body, out_shape=[jax.ShapeDtypeStruct(s, d) for s, d in ou...  21.9 us
    ppermute x18, waiting for transfers between devices, permute(): return lax.ppermute(x, 'region', pairs)  16 us
    unnamed x14, local copies, waits for them, and re-layouts  2.12 us
  transfers between devices with their start and end apart: 18, of which 8 were waited for; matrix products, arithmetic and copies ran while one was open for 3% of the time, Pallas kernels for 19%

profile of v3, /device:TPU:0, one launch (start us, length us, event | category | flops | bytes accessed | tf_op | source)
XLA Modules:
  0.0 79.2 jit_solution(6019333856976840170)
XLA Ops:
  0.7 1.4 %collective-permute-start.1 = (bf16[4,256,256]{2,1,0:T(8,128)(2,1)}, bf16[4,256,256]{2,1,0:T(8,128)(2,1)S(1)}, u32[]{:S(2)}, u32[]{:S(2)}) collective-permute-start(bf16[4,256,256]{2,1,0:T(8,128)(2,1)} %second_ref.7), channel_id=1, source_target_pairs={{1,0},{2,1},{3,2},{4,3},{5,4},{6,5},{7,6},{8,7},{9,8},{10,9},{11,1... | collective-permute-start | bytes 1572872 | tf_op jit(solution)/shard_map/ppermute | solution.py:368
  2.1 3.1 %collective-permute-start = (bf16[4,256,256]{2,1,0:T(8,128)(2,1)}, bf16[4,256,256]{2,1,0:T(8,128)(2,1)S(1)}, u32[]{:S(2)}, u32[]{:S(2)}) collective-permute-start(bf16[4,256,256]{2,1,0:T(8,128)(2,1)} %second_ref.7), channel_id=1, source_target_pairs={{0,1},{1,2},{2,3},{3,4},{4,5},{5,6},{6,7},{7,8},{8,9},{9,10},{10,1... | collective-permute-start | bytes 1572872 | tf_op jit(solution)/shard_map/ppermute | solution.py:368
  9.1 2.3 %shard_map.110.old_ref = bf16[4,256,128]{2,1,0:T(8,128)(2,1)S(1)} custom-call(bf16[4,256,256]{2,1,0:T(8,128)(2,1)S(1)} %copy-done.1, bf16[4,256,256]{2,1,0:T(8,128)(2,1)S(1)} %copy-done.3), custom_call_target="tpu_custom_call" | custom-call | tf_op jit(solution)/shard_map/pallas_call | solution.py:46
  11.9 3.8 %shard_map.111 = (bf16[4,256,128]{2,1,0:T(8,128)(2,1)S(1)}, bf16[256,128]{1,0:T(8,128)(2,1)S(1)}, bf16[256,128]{1,0:T(8,128)(2,1)S(1)}) custom-call(s32[1]{0:T(128)} %bitcast.par_ref.index_ref, bf16[4,256,256]{2,1,0:T(8,128)(2,1)S(1)} %copy-done.1, bf16[4,256,128]{2,1,0:T(8,128)(2,1)S(1)} %shard_map.110.old_ref, ...), custom_call_target="tpu_custom_call" | custom-call | tf_op jit(solution)/shard_map/pallas_call | solution.py:46
  15.7 6.9 %collective-permute-start.2 = (bf16[256,128]{1,0:T(8,128)(2,1)S(1)}, bf16[256,128]{1,0:T(8,128)(2,1)S(1)}, u32[]{:S(2)}, u32[]{:S(2)}) collective-permute-start(bf16[256,128]{1,0:T(8,128)(2,1)S(1)} %get-tuple-element.80), channel_id=1, source_target_pairs={{0,1},{1,0},{2,3},{3,2},{4,5},{5,4},{6,7},{7,6},{8,9},{9,8},{10,11... | collective-permute-start | bytes 196616 | tf_op jit(solution)/shard_map/ppermute | solution.py:368
  23.3 2.6 %shard_map.112 = (bf16[4,256,384]{2,1,0:T(8,128)(2,1)S(1)}, f32[2,256,256]{2,1,0:T(8,128)S(1)}, bf16[2,256,256]{2,1,0:T(8,128)(2,1)S(1)}, f32[256,1152]{1,0:T(8,128)S(1)}, f32[16,256]{1,0:T(8,128)S(1)}) custom-call(bf16[4,256,128]{2,1,0:T(8,128)(2,1)S(1)} %get-tuple-element.74.corr_ref, bf16[3,384,256]{2,1,0:T(8,128)(2,1)S(1)} %bitcast.15, ...), custom_call_target="tpu_custom_call" | custom-call | tf_op jit(solution)/shard_map/pallas_call | solution.py:46
  25.9 1.8 %shard_map.113 = (bf16[2,256,256]{2,1,0:T(8,128)(2,1)S(1)}, bf16[256,256]{1,0:T(8,128)(2,1)S(1)}, bf16[256,256]{1,0:T(8,128)(2,1)S(1)}, f32[128,768]{1,0:T(8,128)S(1)}, f32[128,768]{1,0:T(8,128)S(1)}) custom-call(s32[1]{0:T(128)} %bitcast.par_ref.index_ref, bf16[4,256,384]{2,1,0:T(8,128)(2,1)S(1)} %get-tuple-element.83.x_ref, ...), custom_call_target="tpu_custom_call" | custom-call | tf_op jit(solution)/shard_map/pallas_call | solution.py:46
  27.7 3.7 %collective-permute-start.4 = (f32[128,768]{1,0:T(8,128)S(1)}, f32[128,768]{1,0:T(8,128)S(1)}, u32[]{:S(2)}, u32[]{:S(2)}) collective-permute-start(f32[128,768]{1,0:T(8,128)S(1)} %get-tuple-element.90), channel_id=1, source_target_pairs={{0,1},{1,0},{2,3},{3,2},{4,5},{5,4},{6,7},{7,6},{8,9},{9,8},{10,11... | collective-permute-start | bytes 1179656 | tf_op jit(solution)/shard_map/ppermute | solution.py:368
  31.4 1.3 %collective-permute-done.4.got_ref = f32[128,768]{1,0:T(8,128)S(1)} collective-permute-done((f32[128,768]{1,0:T(8,128)S(1)}, f32[128,768]{1,0:T(8,128)S(1)}, u32[]{:S(2)}, u32[]{:S(2)}) %collective-permute-start.4) | collective-permute-done | bytes 393248 | tf_op jit(solution)/shard_map/ppermute | solution.py:368
  32.8 2.4 %collective-permute-start.5 = (f32[64,768]{1,0:T(8,128)S(1)}, f32[64,768]{1,0:T(8,128)S(1)}, u32[]{:S(2)}, u32[]{:S(2)}) collective-permute-start(f32[64,768]{1,0:T(8,128)S(1)} %get-tuple-element.91), channel_id=1, source_target_pairs={{0,2},{1,3},{2,0},{3,1},{4,6},{5,7},{6,4},{7,5},{8,10},{9,11},{10,... | collective-permute-start | bytes 589832 | tf_op jit(solution)/shard_map/ppermute | solution.py:368
  38.0 1.2 %shard_map.117 = (bf16[1,256,256]{2,1,0:T(8,128)(2,1)S(1)}, f32[4,256,256]{2,1,0:T(8,128)S(1)}) custom-call(bf16[2,256,128]{2,1,0:T(8,128)(2,1)S(1)} %get-tuple-element.94.ce_ref.mid_ref, bf16[4,256,256]{2,1,0:T(8,128)(2,1)S(1)} %copy-done.2, bf16[4,256,256]{2,1,0:T(8,128)(2,1)S(1)} %copy-done.4, ...), custom_call_target="tpu_custom_call", output_to_operand_aliasing={{1}: (5, {})} | custom-call | tf_op jit(solution)/shard_map/pallas_call | solution.py:46
  39.2 2.6 %collective-permute-done.5.got_ref = f32[64,768]{1,0:T(8,128)S(1)} collective-permute-done((f32[64,768]{1,0:T(8,128)S(1)}, f32[64,768]{1,0:T(8,128)S(1)}, u32[]{:S(2)}, u32[]{:S(2)}) %collective-permute-start.5) | collective-permute-done | bytes 196640 | tf_op jit(solution)/shard_map/ppermute | solution.py:368
  42.4 2.8 %collective-permute-start.14 = (bf16[4,256,256]{2,1,0:T(8,128)(2,1)S(1)}, bf16[4,256,256]{2,1,0:T(8,128)(2,1)S(1)}, u32[]{:S(2)}, u32[]{:S(2)}) collective-permute-start(bf16[4,256,256]{2,1,0:T(8,128)(2,1)S(1)} %copy-done.2), channel_id=1, source_target_pairs={{0,1},{1,2},{2,3},{3,4},{4,5},{5,6},{6,7},{7,8},{8,9},{9,10},{10,1... | collective-permute-start | bytes 1572872 | tf_op jit(solution)/shard_map/ppermute | solution.py:368
  45.2 1.5 %collective-permute-start.16 = (bf16[4,256,256]{2,1,0:T(8,128)(2,1)S(1)}, bf16[4,256,256]{2,1,0:T(8,128)(2,1)S(1)}, u32[]{:S(2)}, u32[]{:S(2)}) collective-permute-start(bf16[4,256,256]{2,1,0:T(8,128)(2,1)S(1)} %copy-done.2), channel_id=1, source_target_pairs={{1,0},{2,1},{3,2},{4,3},{5,4},{6,5},{7,6},{8,7},{9,8},{10,9},{11,1... | collective-permute-start | bytes 1572872 | tf_op jit(solution)/shard_map/ppermute | solution.py:368
  46.7 4.6 %collective-permute-start.8 = (f32[32,768]{1,0:T(8,128)S(1)}, f32[32,768]{1,0:T(8,128)S(1)}, u32[]{:S(2)}, u32[]{:S(2)}) collective-permute-start(f32[32,768]{1,0:T(8,128)S(1)} %get-tuple-element.100), channel_id=1, source_target_pairs={{0,4},{1,5},{2,6},{3,7},{4,0},{5,1},{6,2},{7,3},{8,12},{9,13},{10,... | collective-permute-start | bytes 294920 | tf_op jit(solution)/shard_map/ppermute | solution.py:368
  52.0 3.1 %collective-permute-start.10 = (bf16[256,128]{1,0:T(8,128)(2,1)S(1)}, bf16[256,128]{1,0:T(8,128)(2,1)S(1)}, u32[]{:S(2)}, u32[]{:S(2)}) collective-permute-start(bf16[256,128]{1,0:T(8,128)(2,1)S(1)} %get-tuple-element.118), channel_id=1, source_target_pairs={{0,1},{1,0},{2,3},{3,2},{4,5},{5,4},{6,7},{7,6},{8,9},{9,8},{10,11... | collective-permute-start | bytes 196616 | tf_op jit(solution)/shard_map/ppermute | solution.py:368
  56.3 4.0 %collective-permute-done.8.got_ref = f32[32,768]{1,0:T(8,128)S(1)} collective-permute-done((f32[32,768]{1,0:T(8,128)S(1)}, f32[32,768]{1,0:T(8,128)S(1)}, u32[]{:S(2)}, u32[]{:S(2)}) %collective-permute-start.8) | collective-permute-done | bytes 98336 | tf_op jit(solution)/shard_map/ppermute | solution.py:368
  60.3 2.2 %collective-permute-start.9 = (f32[16,768]{1,0:T(8,128)S(1)}, f32[16,768]{1,0:T(8,128)S(1)}, u32[]{:S(2)}, u32[]{:S(2)}) collective-permute-start(f32[16,768]{1,0:T(8,128)S(1)} %get-tuple-element.109), channel_id=1, source_target_pairs={{0,8},{1,9},{2,10},{3,11},{4,12},{5,13},{6,14},{7,15},{8,0},{9,1},... | collective-permute-start | bytes 147464 | tf_op jit(solution)/shard_map/ppermute | solution.py:368
  62.5 2.3 %shard_map.122 = (bf16[4,256,256]{2,1,0:T(8,128)(2,1)}, f32[4,256,256]{2,1,0:T(8,128)S(1)}) custom-call(bf16[2,256,128]{2,1,0:T(8,128)(2,1)S(1)} %get-tuple-element.110.ce_ref, bf16[4,256,256]{2,1,0:T(8,128)(2,1)S(1)} %copy-done.2, bf16[4,256,256]{2,1,0:T(8,128)(2,1)S(1)} %copy-done.4, ...), custom_call_target="tpu_custom_call", output_to_operand_aliasing={{1}: (5, {})} | custom-call | tf_op jit(solution)/shard_map/pallas_call | solution.py:46
  68.0 2.4 %collective-permute-done.13.got_ref = f32[8,128]{1,0:T(8,128)S(1)} collective-permute-done((f32[8,128]{1,0:T(8,128)S(1)}, f32[8,128]{1,0:T(8,128)S(1)}, u32[]{:S(2)}, u32[]{:S(2)}) %collective-permute-start.13) | collective-permute-done | bytes 4128 | tf_op jit(solution)/shard_map/ppermute | solution.py:368
  70.4 2.3 %shard_map.127 = bf16[4,256,256]{2,1,0:T(8,128)(2,1)} custom-call(s32[1]{0:T(128)} %bitcast.par_ref.index_ref, bf16[256,128]{1,0:T(8,128)(2,1)S(1)} %collective-permute-done.10.ca_ref, bf16[256,128]{1,0:T(8,128)(2,1)S(1)} %collective-permute-done.11.cb_ref, bf16[4,256,256]{2,1,0:T(8,128)(2,1)S(1)} %collective-permute-done.16.high_ref, ...), custom_call_target="tpu_custom_call" | custom-call | tf_op jit(solution)/shard_map/pallas_call | solution.py:46
  72.7 1.3 %collective-permute-done.15.got_ref = f32[8,128]{1,0:T(8,128)S(1)} collective-permute-done((f32[8,128]{1,0:T(8,128)S(1)}, f32[8,128]{1,0:T(8,128)S(1)}, u32[]{:S(2)}, u32[]{:S(2)}) %collective-permute-start.15) | collective-permute-done | bytes 4128 | tf_op jit(solution)/shard_map/ppermute | solution.py:368
  74.0 2.1 %collective-permute-start.17 = (f32[8,128]{1,0:T(8,128)S(1)}, f32[8,128]{1,0:T(8,128)S(1)}, u32[]{:S(2)}, u32[]{:S(2)}) collective-permute-start(f32[8,128]{1,0:T(8,128)S(1)} %shard_map.128.sq_ref), channel_id=1, source_target_pairs={{0,8},{1,9},{2,10},{3,11},{4,12},{5,13},{6,14},{7,15},{8,0},{9,1},... | collective-permute-start | bytes 12296 | tf_op jit(solution)/shard_map/ppermute | solution.py:368
  76.1 2.4 %collective-permute-done.17.got_ref = f32[8,128]{1,0:T(8,128)S(1)} collective-permute-done((f32[8,128]{1,0:T(8,128)S(1)}, f32[8,128]{1,0:T(8,128)S(1)}, u32[]{:S(2)}, u32[]{:S(2)}) %collective-permute-start.17) | collective-permute-done | bytes 4128 | tf_op jit(solution)/shard_map/ppermute | solution.py:368
  (59 shorter events, 14.1 us)
Async XLA Ops:
  0.6 10.9 %copy-start = (bf16[9,81,256]{2,1,0:T(8,128)(2,1)S(1)}, bf16[9,81,256]{2,1,0:T(8,128)(2,1)}, u32[]{:S(2)}) copy-start(bf16[9,81,256]{2,1,0:T(8,128)(2,1)} %param.11) | copy-start | bytes 1119748
  0.6 10.7 %copy-start.6 = (bf16[2,256]{1,0:T(2,128)(2,1)S(1)}, bf16[2,256]{1,0:T(2,128)(2,1)}, u32[]{:S(2)}) copy-start(bf16[2,256]{1,0:T(2,128)(2,1)} %param.13) | copy-start | bytes 3076
  0.7 11.2 %collective-permute-start.1 = (bf16[4,256,256]{2,1,0:T(8,128)(2,1)}, bf16[4,256,256]{2,1,0:T(8,128)(2,1)S(1)}, u32[]{:S(2)}, u32[]{:S(2)}) collective-permute-start(bf16[4,256,256]{2,1,0:T(8,128)(2,1)} %second_ref.7), channel_id=1, source_target_pairs={{1,0},{2,1},{3,2},{4,3},{5,4},{6,5},{7,6},{8,7},{9,8},{10,9},{11,1... | collective-permute-start | bytes 1572872 | tf_op jit(solution)/shard_map/ppermute | solution.py:368
  2.1 9.8 %collective-permute-start = (bf16[4,256,256]{2,1,0:T(8,128)(2,1)}, bf16[4,256,256]{2,1,0:T(8,128)(2,1)S(1)}, u32[]{:S(2)}, u32[]{:S(2)}) collective-permute-start(bf16[4,256,256]{2,1,0:T(8,128)(2,1)} %second_ref.7), channel_id=1, source_target_pairs={{0,1},{1,2},{2,3},{3,4},{4,5},{5,6},{6,7},{7,8},{8,9},{9,10},{10,1... | collective-permute-start | bytes 1572872 | tf_op jit(solution)/shard_map/ppermute | solution.py:368
  7.0 1.0 %copy-start.1 = (bf16[4,256,256]{2,1,0:T(8,128)(2,1)S(1)}, bf16[4,256,256]{2,1,0:T(8,128)(2,1)}, u32[]{:S(2)}) copy-start(bf16[4,256,256]{2,1,0:T(8,128)(2,1)} %first_ref.11) | copy-start | bytes 1572868
  11.8 11.5 %copy-start.5 = (f32[2,4,256]{2,1,0:T(4,128)S(1)}, f32[2,4,256]{2,1,0:T(4,128)}, u32[]{:S(2)}) copy-start(f32[2,4,256]{2,1,0:T(4,128)} %target_ref.3) | copy-start | bytes 24580
  15.7 10.2 %collective-permute-start.2 = (bf16[256,128]{1,0:T(8,128)(2,1)S(1)}, bf16[256,128]{1,0:T(8,128)(2,1)S(1)}, u32[]{:S(2)}, u32[]{:S(2)}) collective-permute-start(bf16[256,128]{1,0:T(8,128)(2,1)S(1)} %get-tuple-element.80), channel_id=1, source_target_pairs={{0,1},{1,0},{2,3},{3,2},{4,5},{5,4},{6,7},{7,6},{8,9},{9,8},{10,11... | collective-permute-start | bytes 196616 | tf_op jit(solution)/shard_map/ppermute | solution.py:368
  22.6 3.3 %collective-permute-start.3 = (bf16[256,128]{1,0:T(8,128)(2,1)S(1)}, bf16[256,128]{1,0:T(8,128)(2,1)S(1)}, u32[]{:S(2)}, u32[]{:S(2)}) collective-permute-start(bf16[256,128]{1,0:T(8,128)(2,1)S(1)} %get-tuple-element.81), channel_id=1, source_target_pairs={{1,2},{3,4},{5,6},{7,8},{9,10},{11,12},{13,14},{2,1},{4,3},{6,5},{... | collective-permute-start | bytes 196616 | tf_op jit(solution)/shard_map/ppermute | solution.py:368
  27.7 9.1 %copy-start.2 = (bf16[4,256,256]{2,1,0:T(8,128)(2,1)S(1)}, bf16[4,256,256]{2,1,0:T(8,128)(2,1)}, u32[]{:S(2)}) copy-start(bf16[4,256,256]{2,1,0:T(8,128)(2,1)} %first_ref.11) | copy-start | bytes 1572868
  27.7 9.1 %copy-start.4 = (bf16[4,256,256]{2,1,0:T(8,128)(2,1)S(1)}, bf16[4,256,256]{2,1,0:T(8,128)(2,1)}, u32[]{:S(2)}) copy-start(bf16[4,256,256]{2,1,0:T(8,128)(2,1)} %second_ref.7) | copy-start | bytes 1572868
  27.7 5.1 %collective-permute-start.4 = (f32[128,768]{1,0:T(8,128)S(1)}, f32[128,768]{1,0:T(8,128)S(1)}, u32[]{:S(2)}, u32[]{:S(2)}) collective-permute-start(f32[128,768]{1,0:T(8,128)S(1)} %get-tuple-element.90), channel_id=1, source_target_pairs={{0,1},{1,0},{2,3},{3,2},{4,5},{5,4},{6,7},{7,6},{8,9},{9,8},{10,11... | collective-permute-start | bytes 1179656 | tf_op jit(solution)/shard_map/ppermute | solution.py:368
  32.8 9.0 %collective-permute-start.5 = (f32[64,768]{1,0:T(8,128)S(1)}, f32[64,768]{1,0:T(8,128)S(1)}, u32[]{:S(2)}, u32[]{:S(2)}) collective-permute-start(f32[64,768]{1,0:T(8,128)S(1)} %get-tuple-element.91), channel_id=1, source_target_pairs={{0,2},{1,3},{2,0},{3,1},{4,6},{5,7},{6,4},{7,5},{8,10},{9,11},{10,... | collective-permute-start | bytes 589832 | tf_op jit(solution)/shard_map/ppermute | solution.py:368
  35.2 6.7 %collective-permute-start.6 = (bf16[256,256]{1,0:T(8,128)(2,1)S(1)}, bf16[256,256]{1,0:T(8,128)(2,1)S(1)}, u32[]{:S(2)}, u32[]{:S(2)}) collective-permute-start(bf16[256,256]{1,0:T(8,128)(2,1)S(1)} %get-tuple-element.102), channel_id=1, source_target_pairs={{0,1},{1,0},{2,3},{3,2},{4,5},{5,4},{6,7},{7,6},{8,9},{9,8},{10,11... | collective-permute-start | bytes 393224 | tf_op jit(solution)/shard_map/ppermute | solution.py:368
  35.3 6.6 %collective-permute-start.7 = (bf16[256,256]{1,0:T(8,128)(2,1)S(1)}, bf16[256,256]{1,0:T(8,128)(2,1)S(1)}, u32[]{:S(2)}, u32[]{:S(2)}) collective-permute-start(bf16[256,256]{1,0:T(8,128)(2,1)S(1)} %get-tuple-element.103), channel_id=1, source_target_pairs={{1,2},{3,4},{5,6},{7,8},{9,10},{11,12},{13,14},{2,1},{4,3},{6,5},{... | collective-permute-start | bytes 393224 | tf_op jit(solution)/shard_map/ppermute | solution.py:368
  42.4 24.4 %collective-permute-start.14 = (bf16[4,256,256]{2,1,0:T(8,128)(2,1)S(1)}, bf16[4,256,256]{2,1,0:T(8,128)(2,1)S(1)}, u32[]{:S(2)}, u32[]{:S(2)}) collective-permute-start(bf16[4,256,256]{2,1,0:T(8,128)(2,1)S(1)} %copy-done.2), channel_id=1, source_target_pairs={{0,1},{1,2},{2,3},{3,4},{4,5},{5,6},{6,7},{7,8},{8,9},{9,10},{10,1... | collective-permute-start | bytes 1572872 | tf_op jit(solution)/shard_map/ppermute | solution.py:368
  45.2 25.1 %collective-permute-start.16 = (bf16[4,256,256]{2,1,0:T(8,128)(2,1)S(1)}, bf16[4,256,256]{2,1,0:T(8,128)(2,1)S(1)}, u32[]{:S(2)}, u32[]{:S(2)}) collective-permute-start(bf16[4,256,256]{2,1,0:T(8,128)(2,1)S(1)} %copy-done.2), channel_id=1, source_target_pairs={{1,0},{2,1},{3,2},{4,3},{5,4},{6,5},{7,6},{8,7},{9,8},{10,9},{11,1... | collective-permute-start | bytes 1572872 | tf_op jit(solution)/shard_map/ppermute | solution.py:368
  46.7 13.6 %collective-permute-start.8 = (f32[32,768]{1,0:T(8,128)S(1)}, f32[32,768]{1,0:T(8,128)S(1)}, u32[]{:S(2)}, u32[]{:S(2)}) collective-permute-start(f32[32,768]{1,0:T(8,128)S(1)} %get-tuple-element.100), channel_id=1, source_target_pairs={{0,4},{1,5},{2,6},{3,7},{4,0},{5,1},{6,2},{7,3},{8,12},{9,13},{10,... | collective-permute-start | bytes 294920 | tf_op jit(solution)/shard_map/ppermute | solution.py:368
  51.3 13.4 %collective-permute-start.11 = (bf16[256,128]{1,0:T(8,128)(2,1)S(1)}, bf16[256,128]{1,0:T(8,128)(2,1)S(1)}, u32[]{:S(2)}, u32[]{:S(2)}) collective-permute-start(bf16[256,128]{1,0:T(8,128)(2,1)S(1)} %get-tuple-element.119), channel_id=1, source_target_pairs={{1,2},{3,4},{5,6},{7,8},{9,10},{11,12},{13,14},{2,1},{4,3},{6,5},{... | collective-permute-start | bytes 196616 | tf_op jit(solution)/shard_map/ppermute | solution.py:368
  52.0 12.7 %collective-permute-start.10 = (bf16[256,128]{1,0:T(8,128)(2,1)S(1)}, bf16[256,128]{1,0:T(8,128)(2,1)S(1)}, u32[]{:S(2)}, u32[]{:S(2)}) collective-permute-start(bf16[256,128]{1,0:T(8,128)(2,1)S(1)} %get-tuple-element.118), channel_id=1, source_target_pairs={{0,1},{1,0},{2,3},{3,2},{4,5},{5,4},{6,7},{7,6},{8,9},{9,8},{10,11... | collective-permute-start | bytes 196616 | tf_op jit(solution)/shard_map/ppermute | solution.py:368
  60.3 5.1 %collective-permute-start.9 = (f32[16,768]{1,0:T(8,128)S(1)}, f32[16,768]{1,0:T(8,128)S(1)}, u32[]{:S(2)}, u32[]{:S(2)}) collective-permute-start(f32[16,768]{1,0:T(8,128)S(1)} %get-tuple-element.109), channel_id=1, source_target_pairs={{0,8},{1,9},{2,10},{3,11},{4,12},{5,13},{6,14},{7,15},{8,0},{9,1},... | collective-permute-start | bytes 147464 | tf_op jit(solution)/shard_map/ppermute | solution.py:368
  65.5 1.2 %collective-permute-start.12 = (f32[8,128]{1,0:T(8,128)S(1)}, f32[8,128]{1,0:T(8,128)S(1)}, u32[]{:S(2)}, u32[]{:S(2)}) collective-permute-start(f32[8,128]{1,0:T(8,128)S(1)} %get-tuple-element.121.own_ref), channel_id=1, source_target_pairs={{0,1},{1,0},{2,3},{3,2},{4,5},{5,4},{6,7},{7,6},{8,9},{9,8},{10,11... | collective-permute-start | bytes 12296 | tf_op jit(solution)/shard_map/ppermute | solution.py:368
  66.8 3.6 %collective-permute-start.13 = (f32[8,128]{1,0:T(8,128)S(1)}, f32[8,128]{1,0:T(8,128)S(1)}, u32[]{:S(2)}, u32[]{:S(2)}) collective-permute-start(f32[8,128]{1,0:T(8,128)S(1)} %shard_map.124.own_ref), channel_id=1, source_target_pairs={{0,2},{1,3},{2,0},{3,1},{4,6},{5,7},{6,4},{7,5},{8,10},{9,11},{10,... | collective-permute-start | bytes 12296 | tf_op jit(solution)/shard_map/ppermute | solution.py:368
  70.4 3.6 %collective-permute-start.15 = (f32[8,128]{1,0:T(8,128)S(1)}, f32[8,128]{1,0:T(8,128)S(1)}, u32[]{:S(2)}, u32[]{:S(2)}) collective-permute-start(f32[8,128]{1,0:T(8,128)S(1)} %shard_map.126.own_ref), channel_id=1, source_target_pairs={{0,4},{1,5},{2,6},{3,7},{4,0},{5,1},{6,2},{7,3},{8,12},{9,13},{10,... | collective-permute-start | bytes 12296 | tf_op jit(solution)/shard_map/ppermute | solution.py:368
  74.0 4.5 %collective-permute-start.17 = (f32[8,128]{1,0:T(8,128)S(1)}, f32[8,128]{1,0:T(8,128)S(1)}, u32[]{:S(2)}, u32[]{:S(2)}) collective-permute-start(f32[8,128]{1,0:T(8,128)S(1)} %shard_map.128.sq_ref), channel_id=1, source_target_pairs={{0,8},{1,9},{2,10},{3,11},{4,12},{5,13},{6,14},{7,15},{8,0},{9,1},... | collective-permute-start | bytes 12296 | tf_op jit(solution)/shard_map/ppermute | solution.py:368
  (1 other events, 1.0 us)

commit v4 on v3

--- a/solution.py
+++ b/solution.py
@@ -93,21 +93,20 @@
     return (col >= 0) & (col < rows) & (lane < K)
 
 
-def corr_rows(first_ref, second_ref, start, before, put):
-    rows, cols = first_ref.shape[0], first_ref.shape[1]
+def corr_rows(turned_ref, second_ref, start, before, put):
+    rows, cols = turned_ref.shape[0], turned_ref.shape[1]
     count = second_ref.shape[0]
     lane = iota((cols, LANES), 1)
     valid = lane_valid(cols)
-    mirror = (iota((cols, cols), 0) + iota((cols, cols), 1) == cols - 1).astype(bf16)
+    mirror = mirror_of(cols)
     for r in range(rows):
         dys = [q - r + RADIUS for q in range(start, start + count) if abs(q - r) <= RADIUS]
         if not dys:
             put(r, before[r])
             continue
-        turned = dot(mirror, first_ref[r]).astype(bf16)
         acc = jnp.zeros((cols, LANES), f32)
         for dyi in dys:
-            band = band_of(dot(turned, second_ref[r + dyi - RADIUS - start], NT), dyi)
+            band = band_of(dot(turned_ref[r], second_ref[r + dyi - RADIUS - start], NT), dyi)
             acc = jnp.where((lane >= 9 * dyi) & (lane < 9 * dyi + 9), band, acc)
         acc = jnp.where(valid, dot(mirror, (acc * (C ** -0.5)).astype(bf16)), 0.0)
         if before is None:
@@ -118,17 +117,38 @@
         put(r, acc.astype(bf16))
 
 
-def corr_own_body(first_ref, own_ref, corr_ref):
-    corr_rows(first_ref, own_ref, 0, None, lambda r, v: corr_ref.__setitem__(r, v))
-
-
-def corr_halo_body(par_ref, first_ref, old_ref, low_ref, high_ref, corr_ref, ea_ref, eb_ref, mid_ref):
-    rows = first_ref.shape[0]
-    par = par_ref[0] & 1
-    corr_rows(first_ref, low_ref, -low_ref.shape[0], old_ref, lambda r, v: mid_ref.__setitem__(r, v))
-    corr_rows(first_ref, high_ref, rows, mid_ref, lambda r, v: corr_ref.__setitem__(r, v))
-    ea_ref[...] = corr_ref[(1 - par) * (rows - 1)]
-    eb_ref[...] = corr_ref[par * (rows - 1)]
+def mirror_of(cols):
+    return (iota((cols, cols), 0) + iota((cols, cols), 1) == cols - 1).astype(bf16)
+
+
+def by_side(below, body):
+    pl.when(below)(lambda: body(True))
+    pl.when(jnp.logical_not(below))(lambda: body(False))
+
+
+def corr_near_body(index_ref, first_ref, own_ref, inner_ref, corr_ref, turned_ref, mid_ref):
+    rows, cols = first_ref.shape[0], first_ref.shape[1]
+    mirror = mirror_of(cols)
+    for r in range(rows):
+        turned_ref[r] = dot(mirror, first_ref[r]).astype(bf16)
+    corr_rows(turned_ref, own_ref, 0, None, lambda r, v: mid_ref.__setitem__(r, v))
+
+    def side(below):
+        corr_rows(turned_ref, inner_ref, rows if below else -rows, mid_ref, lambda r, v: corr_ref.__setitem__(r, v))
+
+    by_side(index_ref[0] & 1 == 0, side)
+
+
+def corr_outer_body(index_ref, turned_ref, old_ref, outer_ref, corr_ref, ea_ref, eb_ref):
+    rows = turned_ref.shape[0]
+    par = index_ref[0] & 1
+
+    def side(below):
+        corr_rows(turned_ref, outer_ref, rows if below else -rows, old_ref, lambda r, v: corr_ref.__setitem__(r, v))
+        ea_ref[...] = corr_ref[0 if below else rows - 1]
+        eb_ref[...] = corr_ref[rows - 1 if below else 0]
+
+    by_side(par == 1, side)
 
 
 def shift_down(x, steps):
@@ -226,15 +246,16 @@
     out_ref[...] = own_ref[...] + got_ref[...]
 
 
-def tail_body(own_ref, got_ref, conv_ref, rest_ref, square_ref):
-    piece = own_ref[...] + got_ref[...]
-    share = piece.shape[0]
+def tail_body(index_ref, own_ref, got_ref, conv_ref, rest_ref, square_ref, *, step):
+    both = own_ref[...] + got_ref[...]
+    share = conv_ref.shape[1]
+    piece = jnp.where((index_ref[0] >> step) & 1 == 0, both[:share], both[share:])
     for tap in range(9):
         conv_ref[tap] = piece[:, tap * K:(tap + 1) * K]
     start = 9 * K // LANES * LANES
     rest = jnp.concatenate([piece[:, start:start + LANES], jnp.zeros((LANES - share, LANES), f32)], axis=0)
     rest_ref[...] = rest.T[9 * K - start:9 * K - start + 3, 0:share]
-    square_ref[...] = jnp.broadcast_to(jnp.sum(piece * piece).reshape(1, 1), square_ref.shape)
+    square_ref[...] = jnp.broadcast_to(jnp.sum(both * both).reshape(1, 1), square_ref.shape)
 
 
 def final_body(sq_ref, got_ref, conv_ref, rest_ref, out_ref, bias_ref, head_ref, *, limit):
@@ -302,16 +323,22 @@
         eb_ref[...] = down
 
 
-def row_grad_body(ce_ref, first_ref, second_ref, low_ref, high_ref, *refs, r, at, done):
+def row_grad_body(index_ref, ce_ref, first_ref, second_ref, inner_ref, outer_ref, *refs, r, at, done):
     fg_ref, part_ref = refs[-2:]
     old_ref = refs[0] if len(refs) > 2 else None
     rows, cols = first_ref.shape[0], first_ref.shape[1]
+    even = index_ref[0] & 1 == 0
     bands = ce_ref[at].astype(f32)
     turned = first_ref[r].T
     acc = jnp.zeros((cols, C), f32)
     for dyi in range(WIN):
         q = r + dyi - RADIUS
-        src = low_ref[q + RADIUS] if q < 0 else (high_ref[q - rows] if q >= rows else second_ref[q])
+        if q < 0:
+            src = jnp.where(even, outer_ref[q + rows], inner_ref[q + rows])
+        elif q >= rows:
+            src = jnp.where(even, inner_ref[q - rows], outer_ref[q - rows])
+        else:
+            src = second_ref[q]
         spread = spread_of(bands, dyi)
         acc = acc + dot(spread, src)
         if 0 <= q < rows:
@@ -322,34 +349,33 @@
         fg_ref[other] = row_ref[0]
 
 
-def halo_part(bands, rows_ref, dys_of, old_ref):
+def halo_parts(bands_ref, rows_ref, below, old_ref):
     rows = old_ref.shape[0]
+    bands = bands_ref[...].astype(f32)
     parts = [old_ref[q] for q in range(rows)]
     slot = 0
     for r in range(rows):
         turned = rows_ref[r].T
-        for q in dys_of(r):
+        for q in range(rows + r - RADIUS, rows) if below else range(0, r + RADIUS + 1 - rows):
             parts[q] = parts[q] + dot(turned, spread_of(bands, slot))
             slot += 1
     return parts
 
 
-def halo_above_body(index_ref, ca_ref, cb_ref, low_ref, old_ref, part_ref):
-    par = index_ref[0] & 1
-    rows = part_ref.shape[0]
-    bands = jnp.where(par == 0, cb_ref[...].astype(f32), ca_ref[...].astype(f32))
-    parts = halo_part(bands, low_ref, lambda a: range(0, a + RADIUS + 1 - rows), old_ref)
-    for q in range(rows):
-        part_ref[q] = parts[q]
-
-
-def halo_below_body(index_ref, ca_ref, cb_ref, high_ref, part_ref, sg_ref):
-    par = index_ref[0] & 1
-    rows = part_ref.shape[0]
-    bands = jnp.where(par == 0, ca_ref[...].astype(f32), cb_ref[...].astype(f32))
-    parts = halo_part(bands, high_ref, lambda b: range(rows + b - RADIUS, rows), part_ref)
-    for q in range(rows):
-        sg_ref[q] = parts[q].T.astype(bf16)
+def halo_inner_body(index_ref, bands_ref, rows_ref, old_ref, part_ref):
+    def side(below):
+        for q, part in enumerate(halo_parts(bands_ref, rows_ref, below, old_ref)):
+            part_ref[q] = part
+
+    by_side(index_ref[0] & 1 == 0, side)
+
+
+def halo_outer_body(index_ref, bands_ref, rows_ref, old_ref, sg_ref):
+    def side(below):
+        for q, part in enumerate(halo_parts(bands_ref, rows_ref, below, old_ref)):
+            sg_ref[q] = part.T.astype(bf16)
+
+    by_side(index_ref[0] & 1 == 1, side)
 
 
 def on_device(first_map, second_map, flow_target, valid_tiles, conv_weight, conv_bias, head_weight):
@@ -358,8 +384,6 @@
     count = lax.axis_size("region")
     index = lax.axis_index("region")
     par = index.reshape(1)
-    forward = [(i, i + 1) for i in range(count - 1)]
-    backward = [(b, a) for a, b in forward]
     inner = [(i, i ^ 1) for i in range(count)]
     outer = [(i, i + 1) for i in range(1, count - 1, 2)]
     outer = outer + [(b, a) for a, b in outer]
@@ -370,8 +394,9 @@
     def swap(x, step):
         return permute(x, [(i, i ^ (1 << step)) for i in range(count)])
 
-    second_low = permute(second_map, forward)
-    second_high = permute(second_map, backward)
+    second_outer = permute(second_map, outer)
+    second_inner = permute(second_map, inner)
+    first_inner = permute(first_map, inner)
 
     share = hid // count
     radix = [2] * (count.bit_length() - 1)
@@ -392,19 +417,24 @@
     mask = jnp.repeat(own_tiles, TILE, axis=1).astype(f32)
 
     vector = lambda *s: pltpu.VMEM(s, bf16)
-    (corr_own,) = call(corr_own_body, [((rows, cols, LANES), bf16)], (first_map, second_map))
-    weight, head, bias, mask, corr_own, second_low, second_high = lax.optimization_barrier(
-        (weight, head, bias, mask, corr_own, second_low, second_high)
+    corr_near, turned = call(
+        corr_near_body,
+        [((rows, cols, LANES), bf16), ((rows, cols, C), bf16)],
+        (par, first_map, second_map, second_inner),
+        scratch=[vector(rows, cols, LANES)],
+        scalar=True,
+    )
+    weight, head, bias, mask, corr_near, second_outer, first_inner = lax.optimization_barrier(
+        (weight, head, bias, mask, corr_near, second_outer, first_inner)
     )
     corr, edge_a, edge_b = call(
-        corr_halo_body,
+        corr_outer_body,
         [((rows, cols, LANES), bf16), ((cols, LANES), bf16), ((cols, LANES), bf16)],
-        (par, first_map, corr_own, second_low, second_high),
-        scratch=[vector(rows, cols, LANES)],
-        scalar=True,
-    )
+        (par, turned, corr_near, second_outer),
+        scalar=True,
+    )
+    halo_b = permute(edge_b, outer)
     halo_a = permute(edge_a, inner)
-    halo_b = permute(edge_b, outer)
     taps, pre_edge, pe_mid, part_sums, head_part = call(
         conv_own_body,
         [((rows, cols, 3 * LANES), bf16), ((2, cols, hid), f32), ((rows - 2, cols, hid), bf16), ((hid, 9 * LANES), f32), ((16, hid), f32)],
@@ -423,19 +453,23 @@
     pe_halo_a = permute(pe_a, inner)
     pe_halo_b = permute(pe_b, outer)
 
+    def add(x, y):
+        return call(add_body, [(x.shape, f32)], (x, y))[0]
+
     def halve(step, keep, got):
         half = keep.shape[0] // 2
         return call(functools.partial(halve_body, step=step), [((half, WIDTH), f32)] * 2, (par, keep, got), scalar=True)
 
     def row_grad(r, at, cerr, part, done=()):
-        args = (cerr, first_map, second_map, second_low, second_high)
+        args = (par, cerr, first_map, second_map, second_inner, second_outer)
         if part is not None:
             args = args + (part,) + tuple(row for _, row in done)
         return call(
             functools.partial(row_grad_body, r=r, at=at, done=[other for other, _ in done]),
             [((rows if done else 1, cols, C), bf16), ((rows, C, cols), f32)],
             args,
-            alias=None if part is None else {5: 1},
+            scalar=True,
+            alias=None if part is None else {6: 1},
         )
 
     steps = len(radix)
@@ -461,49 +495,46 @@
         scratch=[vector(2, cols, hid)],
         scalar=True,
     )
-    ce_halo_a = permute(ce_a, inner)
-    ce_halo_b = permute(ce_b, outer)
-    first_tied = after(first_map, ce_a)
-    first_low = permute(first_tied, forward)
-    first_high = permute(first_tied, backward)
+    ce_outer = permute(ce_b, outer)
+    ce_inner = permute(ce_a, inner)
+    first_outer = permute(after(first_map, ce_a), outer)
     row, part = row_grad(0, 0, ce_edge, part)
     done.append((0, row))
     got, part = lax.optimization_barrier((got, part))
-    for step in range(3, steps):
+    for step in range(3, steps - 1):
         keep, send = halve(step, keep, got)
         got = swap(send, step)
-    first_grad, part = row_grad(rows - 1, 1, after(ce_edge, send), part, done)
-    got, part, ce_halo_a, ce_halo_b = lax.optimization_barrier((got, part, ce_halo_a, ce_halo_b))
+    piece = add(keep, got)
+    got = swap(piece, steps - 1)
+    first_grad, part = row_grad(rows - 1, 1, after(ce_edge, piece), part, done)
+    got, part, ce_inner, ce_outer = lax.optimization_barrier((got, part, ce_inner, ce_outer))
     conv_raw, rest_raw, square = call(
-        tail_body,
+        functools.partial(tail_body, step=steps - 1),
         [((9, share, K), f32), ((3, share), f32), ((8, LANES), f32)],
-        (keep, got),
-    )
-
-    def add(x, y):
-        return call(add_body, [((8, LANES), f32)], (x, y))[0]
-
+        (par, piece, got),
+        scalar=True,
+    )
     got = swap(square, 0)
     square = add(square, got)
     got = swap(square, 1)
     (part,) = call(
-        halo_above_body,
+        halo_inner_body,
         [((rows, C, cols), f32)],
-        (par, after(ce_halo_a, square), ce_halo_b, first_low, part),
-        scalar=True,
-        alias={4: 0},
+        (par, after(ce_inner, square), first_inner, part),
+        scalar=True,
+        alias={3: 0},
     )
     got, part = lax.optimization_barrier((got, part))
     square = add(square, got)
     got = swap(square, 2)
     (second_grad,) = call(
-        halo_below_body,
+        halo_outer_body,
         [((rows, cols, C), bf16)],
-        (par, after(ce_halo_a, square), ce_halo_b, first_high, part),
+        (par, after(ce_outer, square), first_outer, part),
         scalar=True,
     )
     got, second_grad = lax.optimization_barrier((got, second_grad))
-    for step in range(3, steps):
+    for step in range(3, steps - 1):
         square = add(square, got)
         got = swap(square, step)
     param_count = 9 * K * hid + 3 * hid

time: 79.6 us -> 71.1 us (0.89)
  starting transfers between devices: 35.9 us -> 31.7 us
  waiting for transfers between devices: 16 us -> 13.3 us
  local copies, waits for them, and re-layouts: 3.96 us -> 1.86 us
    ppermute x18 -> x17, starting transfers between devices: 35.9 us -> 31.7 us  [permute(): return lax.ppermute(x, 'region', pairs)]
    ppermute x18 -> x17, waiting for transfers between devices: 16 us -> 13.3 us  [permute(): return lax.ppermute(x, 'region', pairs)]
    unnamed x14 -> x8, local copies, waits for them, and re-layouts: 2.12 us -> 0.02 us
    pallas_call x20 -> x19, Pallas kernels: 21.9 us -> 21.9 us  [call(): pl.pallas_call(body, out_shape=[jax.ShapeDtypeStruct(s, d) for s, d in ou...]
  transfers between devices with their start and end apart: 18 -> 17, of which waited for: 8 -> 5; matrix products, arithmetic and copies ran while one was open for 3% -> 4% of each run, Pallas kernels for 19% -> 24%
where the time goes in v4:
time: 71.1 us; the launch traced here: 70.9 us
  starting transfers between devices  31.7 us (45%)
  Pallas kernels  21.9 us (31%)
  waiting for transfers between devices  13.3 us (19%)
  local copies, waits for them, and re-layouts  1.86 us (3%)
  matrix products  1.12 us (2%)
  between operations  0.92 us (1%)
    ppermute x17, starting transfers between devices, permute(): return lax.ppermute(x, 'region', pairs)  31.7 us
    pallas_call x19, Pallas kernels, call(): pl.pallas_call(body, out_shape=[jax.ShapeDtypeStruct(s, d) for s, d in ou...  21.9 us
    ppermute x17, waiting for transfers between devices, permute(): return lax.ppermute(x, 'region', pairs)  13.3 us
  transfers between devices with their start and end apart: 17, of which 5 were waited for; matrix products, arithmetic and copies ran while one was open for 4% of the time, Pallas kernels for 24%

profile of v4, /device:TPU:0, one launch (start us, length us, event | category | flops | bytes accessed | tf_op | source)
XLA Modules:
  0.0 70.9 jit_solution(13704839566336880738)
XLA Ops:
  1.5 4.4 %collective-permute-start = (bf16[4,256,256]{2,1,0:T(8,128)(2,1)}, bf16[4,256,256]{2,1,0:T(8,128)(2,1)S(1)}, u32[]{:S(2)}, u32[]{:S(2)}) collective-permute-start(bf16[4,256,256]{2,1,0:T(8,128)(2,1)} %second_ref.7), channel_id=1, source_target_pairs={{0,1},{1,0},{2,3},{3,2},{4,5},{5,4},{6,7},{7,6},{8,9},{9,8},{10,11... | collective-permute-start | bytes 1572872 | tf_op jit(solution)/shard_map/ppermute | solution.py:392
  7.8 0.8 %convolution_bitcast_fusion.1 = bf16[2,256]{1,0:T(2,128)(2,1)S(1)} fusion(bf16[2,256]{1,0:T(2,128)(2,1)} %param.13, s32[256]{0:T(256)S(1)} %reshape.145), kind=kOutput, calls=%fused_computation.1 | convolution fusion | flops 327680 | bytes 3072 | tf_op jit(solution)/shard_map/jh,hg->jg/dot_general | solution.py:412
  9.0 4.0 %shard_map.110 = (bf16[4,256,128]{2,1,0:T(8,128)(2,1)S(1)}, bf16[4,256,256]{2,1,0:T(8,128)(2,1)S(1)}) custom-call(s32[1]{0:T(128)} %bitcast.index_ref.par_ref, bf16[4,256,256]{2,1,0:T(8,128)(2,1)S(1)} %copy-done.2, bf16[4,256,256]{2,1,0:T(8,128)(2,1)S(1)} %copy-done.1, bf16[4,256,256]{2,1,0:T(8,128)(2,1)S(1)} %collective-permute-done.inner_ref), custom_call_target="tpu_custom_call" | custom-call | tf_op jit(solution)/shard_map/pallas_call | solution.py:46
  13.1 1.7 %shard_map.111 = (bf16[4,256,128]{2,1,0:T(8,128)(2,1)S(1)}, bf16[256,128]{1,0:T(8,128)(2,1)S(1)}, bf16[256,128]{1,0:T(8,128)(2,1)S(1)}) custom-call(s32[1]{0:T(128)} %bitcast.index_ref.par_ref, bf16[4,256,256]{2,1,0:T(8,128)(2,1)S(1)} %get-tuple-element.71.turned_ref, bf16[4,256,128]{2,1,0:T(8,128)(2,1)S(1)} %get-tuple-element.73.old_ref, ...), custom_call_target="tpu_custom_call" | custom-call | tf_op jit(solution)/shard_map/pallas_call | solution.py:46
  14.8 5.0 %collective-permute-start.3 = (bf16[256,128]{1,0:T(8,128)(2,1)S(1)}, bf16[256,128]{1,0:T(8,128)(2,1)S(1)}, u32[]{:S(2)}, u32[]{:S(2)}) collective-permute-start(bf16[256,128]{1,0:T(8,128)(2,1)S(1)} %get-tuple-element.81), channel_id=1, source_target_pairs={{0,1},{1,0},{2,3},{3,2},{4,5},{5,4},{6,7},{7,6},{8,9},{9,8},{10,11... | collective-permute-start | bytes 196616 | tf_op jit(solution)/shard_map/ppermute | solution.py:392
  20.4 2.6 %shard_map.112 = (bf16[4,256,384]{2,1,0:T(8,128)(2,1)S(1)}, f32[2,256,256]{2,1,0:T(8,128)S(1)}, bf16[2,256,256]{2,1,0:T(8,128)(2,1)S(1)}, f32[256,1152]{1,0:T(8,128)S(1)}, f32[16,256]{1,0:T(8,128)S(1)}) custom-call(bf16[4,256,128]{2,1,0:T(8,128)(2,1)S(1)} %get-tuple-element.75.corr_ref, bf16[3,384,256]{2,1,0:T(8,128)(2,1)S(1)} %bitcast.15, ...), custom_call_target="tpu_custom_call" | custom-call | tf_op jit(solution)/shard_map/pallas_call | solution.py:46
  23.0 1.8 %shard_map.113 = (bf16[2,256,256]{2,1,0:T(8,128)(2,1)S(1)}, bf16[256,256]{1,0:T(8,128)(2,1)S(1)}, bf16[256,256]{1,0:T(8,128)(2,1)S(1)}, f32[128,768]{1,0:T(8,128)S(1)}, f32[128,768]{1,0:T(8,128)S(1)}) custom-call(s32[1]{0:T(128)} %bitcast.index_ref.par_ref, bf16[4,256,384]{2,1,0:T(8,128)(2,1)S(1)} %get-tuple-element.84.x_ref, ...), custom_call_target="tpu_custom_call" | custom-call | tf_op jit(solution)/shard_map/pallas_call | solution.py:46
  24.8 3.6 %collective-permute-start.5 = (f32[128,768]{1,0:T(8,128)S(1)}, f32[128,768]{1,0:T(8,128)S(1)}, u32[]{:S(2)}, u32[]{:S(2)}) collective-permute-start(f32[128,768]{1,0:T(8,128)S(1)} %get-tuple-element.91), channel_id=1, source_target_pairs={{0,1},{1,0},{2,3},{3,2},{4,5},{5,4},{6,7},{7,6},{8,9},{9,8},{10,11... | collective-permute-start | bytes 1179656 | tf_op jit(solution)/shard_map/ppermute | solution.py:392
  28.4 1.3 %collective-permute-done.5.got_ref = f32[128,768]{1,0:T(8,128)S(1)} collective-permute-done((f32[128,768]{1,0:T(8,128)S(1)}, f32[128,768]{1,0:T(8,128)S(1)}, u32[]{:S(2)}, u32[]{:S(2)}) %collective-permute-start.5) | collective-permute-done | bytes 393248 | tf_op jit(solution)/shard_map/ppermute | solution.py:392
  29.8 2.4 %collective-permute-start.6 = (f32[64,768]{1,0:T(8,128)S(1)}, f32[64,768]{1,0:T(8,128)S(1)}, u32[]{:S(2)}, u32[]{:S(2)}) collective-permute-start(f32[64,768]{1,0:T(8,128)S(1)} %get-tuple-element.92), channel_id=1, source_target_pairs={{0,2},{1,3},{2,0},{3,1},{4,6},{5,7},{6,4},{7,5},{8,10},{9,11},{10,... | collective-permute-start | bytes 589832 | tf_op jit(solution)/shard_map/ppermute | solution.py:392
  32.2 0.8 %collective-permute-start.8 = (bf16[256,256]{1,0:T(8,128)(2,1)S(1)}, bf16[256,256]{1,0:T(8,128)(2,1)S(1)}, u32[]{:S(2)}, u32[]{:S(2)}) collective-permute-start(bf16[256,256]{1,0:T(8,128)(2,1)S(1)} %get-tuple-element.104), channel_id=1, source_target_pairs={{1,2},{3,4},{5,6},{7,8},{9,10},{11,12},{13,14},{2,1},{4,3},{6,5},{... | collective-permute-start | bytes 393224 | tf_op jit(solution)/shard_map/ppermute | solution.py:392
  33.1 0.9 %shard_map.115 = (bf16[2,256,128]{2,1,0:T(8,128)(2,1)S(1)}, f32[2,256,128]{2,1,0:T(8,128)S(1)}) custom-call(bf16[2,256,256]{2,1,0:T(8,128)(2,1)S(1)} %get-tuple-element.93.mid_ref, bf16[2,256,256]{2,1,0:T(8,128)(2,1)S(1)} %get-tuple-element.94.edge_ref, bf16[3,384,256]{2,1,0:T(8,128)(2,1)S(1)} %bitcast.17), custom_call_target="tpu_custom_call" | custom-call | tf_op jit(solution)/shard_map/pallas_call | solution.py:46
  33.9 1.2 %shard_map.116 = (bf16[1,256,256]{2,1,0:T(8,128)(2,1)S(1)}, f32[4,256,256]{2,1,0:T(8,128)S(1)}) custom-call(s32[1]{0:T(128)} %bitcast.index_ref.par_ref, bf16[2,256,128]{2,1,0:T(8,128)(2,1)S(1)} %get-tuple-element.95.ce_ref.mid_ref, bf16[4,256,256]{2,1,0:T(8,128)(2,1)S(1)} %copy-done.2, bf16[4,256,256]{2,1,0:T(8,128)(2,1)S(1)} %copy-done.1, ...), custom_call_target="tpu_custom_call" | custom-call | tf_op jit(solution)/shard_map/pallas_call | solution.py:46
  35.1 1.2 %shard_map.117 = (bf16[1,256,256]{2,1,0:T(8,128)(2,1)S(1)}, f32[4,256,256]{2,1,0:T(8,128)S(1)}) custom-call(s32[1]{0:T(128)} %bitcast.index_ref.par_ref, bf16[2,256,128]{2,1,0:T(8,128)(2,1)S(1)} %get-tuple-element.95.ce_ref.mid_ref, bf16[4,256,256]{2,1,0:T(8,128)(2,1)S(1)} %copy-done.2, ...), custom_call_target="tpu_custom_call", output_to_operand_aliasing={{1}: (6, {})} | custom-call | tf_op jit(solution)/shard_map/pallas_call | solution.py:46
  36.3 2.5 %collective-permute-done.6.got_ref = f32[64,768]{1,0:T(8,128)S(1)} collective-permute-done((f32[64,768]{1,0:T(8,128)S(1)}, f32[64,768]{1,0:T(8,128)S(1)}, u32[]{:S(2)}, u32[]{:S(2)}) %collective-permute-start.6) | collective-permute-done | bytes 196640 | tf_op jit(solution)/shard_map/ppermute | solution.py:392
  40.0 4.3 %collective-permute-start.9 = (f32[32,768]{1,0:T(8,128)S(1)}, f32[32,768]{1,0:T(8,128)S(1)}, u32[]{:S(2)}, u32[]{:S(2)}) collective-permute-start(f32[32,768]{1,0:T(8,128)S(1)} %get-tuple-element.101), channel_id=1, source_target_pairs={{0,4},{1,5},{2,6},{3,7},{4,0},{5,1},{6,2},{7,3},{8,12},{9,13},{10,... | collective-permute-start | bytes 294920 | tf_op jit(solution)/shard_map/ppermute | solution.py:392
  44.3 1.2 %shard_map.120 = (bf16[1,256,256]{2,1,0:T(8,128)(2,1)S(1)}, f32[4,256,256]{2,1,0:T(8,128)S(1)}) custom-call(s32[1]{0:T(128)} %bitcast.index_ref.par_ref, bf16[2,256,128]{2,1,0:T(8,128)(2,1)S(1)} %get-tuple-element.110.ce_ref, bf16[4,256,256]{2,1,0:T(8,128)(2,1)S(1)} %copy-done.2, ...), custom_call_target="tpu_custom_call", output_to_operand_aliasing={{1}: (6, {})} | custom-call | tf_op jit(solution)/shard_map/pallas_call | solution.py:46
  45.5 8.4 %collective-permute-done.9.got_ref = f32[32,768]{1,0:T(8,128)S(1)} collective-permute-done((f32[32,768]{1,0:T(8,128)S(1)}, f32[32,768]{1,0:T(8,128)S(1)}, u32[]{:S(2)}, u32[]{:S(2)}) %collective-permute-start.9) | collective-permute-done | bytes 98336 | tf_op jit(solution)/shard_map/ppermute | solution.py:392
  53.9 2.9 %collective-permute-start.10 = (f32[32,768]{1,0:T(8,128)S(1)}, f32[32,768]{1,0:T(8,128)S(1)}, u32[]{:S(2)}, u32[]{:S(2)}) collective-permute-start(f32[32,768]{1,0:T(8,128)S(1)} %shard_map.121.own_ref), channel_id=1, source_target_pairs={{0,8},{1,9},{2,10},{3,11},{4,12},{5,13},{6,14},{7,15},{8,0},{9,1},... | collective-permute-start | bytes 294920 | tf_op jit(solution)/shard_map/ppermute | solution.py:392
  57.5 2.3 %shard_map.122 = (bf16[4,256,256]{2,1,0:T(8,128)(2,1)}, f32[4,256,256]{2,1,0:T(8,128)S(1)}) custom-call(s32[1]{0:T(128)} %bitcast.index_ref.par_ref, bf16[2,256,128]{2,1,0:T(8,128)(2,1)S(1)} %get-tuple-element.110.ce_ref, bf16[4,256,256]{2,1,0:T(8,128)(2,1)S(1)} %copy-done.2, bf16[4,256,256]{2,1,0:T(8,128)(2,1)S(1)} %copy-done.1, ...), custom_call_target="tpu_custom_call", output_to_operand_aliasing={{1}: (6, {})} | custom-call | tf_op jit(solution)/shard_map/pallas_call | solution.py:46
  61.3 2.2 %collective-permute-start.14 = (f32[8,128]{1,0:T(8,128)S(1)}, f32[8,128]{1,0:T(8,128)S(1)}, u32[]{:S(2)}, u32[]{:S(2)}) collective-permute-start(f32[8,128]{1,0:T(8,128)S(1)} %shard_map.124.own_ref), channel_id=1, source_target_pairs={{0,2},{1,3},{2,0},{3,1},{4,6},{5,7},{6,4},{7,5},{8,10},{9,11},{10,... | collective-permute-start | bytes 12296 | tf_op jit(solution)/shard_map/ppermute | solution.py:392
  63.5 1.4 %shard_map.125.old_ref = f32[4,256,256]{2,1,0:T(8,128)S(1)} custom-call(s32[1]{0:T(128)} %bitcast.index_ref.par_ref, bf16[256,128]{1,0:T(8,128)(2,1)S(1)} %collective-permute-done.11.bands_ref, bf16[4,256,256]{2,1,0:T(8,128)(2,1)S(1)} %collective-permute-done.2.rows_ref, f32[4,256,256]{2,1,0:T(8,128)S(1)} %get-tuple-element.124.old_ref), custom_call_target="tpu_custom_call", output_to_operand_aliasing={{}: (3, {})} | custom-call | tf_op jit(solution)/shard_map/pallas_call | solution.py:46
  65.1 2.7 %collective-permute-start.15 = (f32[8,128]{1,0:T(8,128)S(1)}, f32[8,128]{1,0:T(8,128)S(1)}, u32[]{:S(2)}, u32[]{:S(2)}) collective-permute-start(f32[8,128]{1,0:T(8,128)S(1)} %shard_map.126.sq_ref), channel_id=1, source_target_pairs={{0,4},{1,5},{2,6},{3,7},{4,0},{5,1},{6,2},{7,3},{8,12},{9,13},{10,... | collective-permute-start | bytes 12296 | tf_op jit(solution)/shard_map/ppermute | solution.py:392
  67.8 2.3 %shard_map.127 = bf16[4,256,256]{2,1,0:T(8,128)(2,1)} custom-call(s32[1]{0:T(128)} %bitcast.index_ref.par_ref, bf16[256,128]{1,0:T(8,128)(2,1)S(1)} %collective-permute-done.12.bands_ref, bf16[4,256,256]{2,1,0:T(8,128)(2,1)S(1)} %collective-permute-done.16.rows_ref, f32[4,256,256]{2,1,0:T(8,128)S(1)} %shard_map.125.old_ref), custom_call_target="tpu_custom_call" | custom-call | tf_op jit(solution)/shard_map/pallas_call | solution.py:46
  (50 shorter events, 8.2 us)
Async XLA Ops:
  0.6 8.0 %copy-start = (bf16[9,81,256]{2,1,0:T(8,128)(2,1)S(1)}, bf16[9,81,256]{2,1,0:T(8,128)(2,1)}, u32[]{:S(2)}) copy-start(bf16[9,81,256]{2,1,0:T(8,128)(2,1)} %param.11) | copy-start | bytes 1119748
  0.6 8.3 %copy-start.1 = (bf16[4,256,256]{2,1,0:T(8,128)(2,1)S(1)}, bf16[4,256,256]{2,1,0:T(8,128)(2,1)}, u32[]{:S(2)}) copy-start(bf16[4,256,256]{2,1,0:T(8,128)(2,1)} %second_ref.7) | copy-start | bytes 1572868
  0.7 8.3 %copy-start.2 = (bf16[4,256,256]{2,1,0:T(8,128)(2,1)S(1)}, bf16[4,256,256]{2,1,0:T(8,128)(2,1)}, u32[]{:S(2)}) copy-start(bf16[4,256,256]{2,1,0:T(8,128)(2,1)} %first_ref.9) | copy-start | bytes 1572868
  0.7 12.4 %collective-permute-start.1 = (bf16[4,256,256]{2,1,0:T(8,128)(2,1)}, bf16[4,256,256]{2,1,0:T(8,128)(2,1)S(1)}, u32[]{:S(2)}, u32[]{:S(2)}) collective-permute-start(bf16[4,256,256]{2,1,0:T(8,128)(2,1)} %second_ref.7), channel_id=1, source_target_pairs={{1,2},{3,4},{5,6},{7,8},{9,10},{11,12},{13,14},{2,1},{4,3},{6,5},{... | collective-permute-start | bytes 1572872 | tf_op jit(solution)/shard_map/ppermute | solution.py:392
  1.5 7.5 %collective-permute-start = (bf16[4,256,256]{2,1,0:T(8,128)(2,1)}, bf16[4,256,256]{2,1,0:T(8,128)(2,1)S(1)}, u32[]{:S(2)}, u32[]{:S(2)}) collective-permute-start(bf16[4,256,256]{2,1,0:T(8,128)(2,1)} %second_ref.7), channel_id=1, source_target_pairs={{0,1},{1,0},{2,3},{3,2},{4,5},{5,4},{6,7},{7,6},{8,9},{9,8},{10,11... | collective-permute-start | bytes 1572872 | tf_op jit(solution)/shard_map/ppermute | solution.py:392
  5.9 7.2 %collective-permute-start.2 = (bf16[4,256,256]{2,1,0:T(8,128)(2,1)}, bf16[4,256,256]{2,1,0:T(8,128)(2,1)S(1)}, u32[]{:S(2)}, u32[]{:S(2)}) collective-permute-start(bf16[4,256,256]{2,1,0:T(8,128)(2,1)} %first_ref.9), channel_id=1, source_target_pairs={{0,1},{1,0},{2,3},{3,2},{4,5},{5,4},{6,7},{7,6},{8,9},{9,8},{10,11... | collective-permute-start | bytes 1572872 | tf_op jit(solution)/shard_map/ppermute | solution.py:392
  9.0 11.4 %copy-start.3 = (f32[2,4,256]{2,1,0:T(4,128)S(1)}, f32[2,4,256]{2,1,0:T(4,128)}, u32[]{:S(2)}) copy-start(f32[2,4,256]{2,1,0:T(4,128)} %target_ref.3) | copy-start | bytes 24580
  14.8 8.2 %collective-permute-start.3 = (bf16[256,128]{1,0:T(8,128)(2,1)S(1)}, bf16[256,128]{1,0:T(8,128)(2,1)S(1)}, u32[]{:S(2)}, u32[]{:S(2)}) collective-permute-start(bf16[256,128]{1,0:T(8,128)(2,1)S(1)} %get-tuple-element.81), channel_id=1, source_target_pairs={{0,1},{1,0},{2,3},{3,2},{4,5},{5,4},{6,7},{7,6},{8,9},{9,8},{10,11... | collective-permute-start | bytes 196616 | tf_op jit(solution)/shard_map/ppermute | solution.py:392
  19.7 3.3 %collective-permute-start.4 = (bf16[256,128]{1,0:T(8,128)(2,1)S(1)}, bf16[256,128]{1,0:T(8,128)(2,1)S(1)}, u32[]{:S(2)}, u32[]{:S(2)}) collective-permute-start(bf16[256,128]{1,0:T(8,128)(2,1)S(1)} %get-tuple-element.82), channel_id=1, source_target_pairs={{1,2},{3,4},{5,6},{7,8},{9,10},{11,12},{13,14},{2,1},{4,3},{6,5},{... | collective-permute-start | bytes 196616 | tf_op jit(solution)/shard_map/ppermute | solution.py:392
  24.8 4.9 %collective-permute-start.5 = (f32[128,768]{1,0:T(8,128)S(1)}, f32[128,768]{1,0:T(8,128)S(1)}, u32[]{:S(2)}, u32[]{:S(2)}) collective-permute-start(f32[128,768]{1,0:T(8,128)S(1)} %get-tuple-element.91), channel_id=1, source_target_pairs={{0,1},{1,0},{2,3},{3,2},{4,5},{5,4},{6,7},{7,6},{8,9},{9,8},{10,11... | collective-permute-start | bytes 1179656 | tf_op jit(solution)/shard_map/ppermute | solution.py:392
  29.8 9.0 %collective-permute-start.6 = (f32[64,768]{1,0:T(8,128)S(1)}, f32[64,768]{1,0:T(8,128)S(1)}, u32[]{:S(2)}, u32[]{:S(2)}) collective-permute-start(f32[64,768]{1,0:T(8,128)S(1)} %get-tuple-element.92), channel_id=1, source_target_pairs={{0,2},{1,3},{2,0},{3,1},{4,6},{5,7},{6,4},{7,5},{8,10},{9,11},{10,... | collective-permute-start | bytes 589832 | tf_op jit(solution)/shard_map/ppermute | solution.py:392
  32.2 6.7 %collective-permute-start.7 = (bf16[256,256]{1,0:T(8,128)(2,1)S(1)}, bf16[256,256]{1,0:T(8,128)(2,1)S(1)}, u32[]{:S(2)}, u32[]{:S(2)}) collective-permute-start(bf16[256,256]{1,0:T(8,128)(2,1)S(1)} %get-tuple-element.103), channel_id=1, source_target_pairs={{0,1},{1,0},{2,3},{3,2},{4,5},{5,4},{6,7},{7,6},{8,9},{9,8},{10,11... | collective-permute-start | bytes 393224 | tf_op jit(solution)/shard_map/ppermute | solution.py:392
  32.2 6.6 %collective-permute-start.8 = (bf16[256,256]{1,0:T(8,128)(2,1)S(1)}, bf16[256,256]{1,0:T(8,128)(2,1)S(1)}, u32[]{:S(2)}, u32[]{:S(2)}) collective-permute-start(bf16[256,256]{1,0:T(8,128)(2,1)S(1)} %get-tuple-element.104), channel_id=1, source_target_pairs={{1,2},{3,4},{5,6},{7,8},{9,10},{11,12},{13,14},{2,1},{4,3},{6,5},{... | collective-permute-start | bytes 393224 | tf_op jit(solution)/shard_map/ppermute | solution.py:392
  39.3 28.5 %collective-permute-start.16 = (bf16[4,256,256]{2,1,0:T(8,128)(2,1)S(1)}, bf16[4,256,256]{2,1,0:T(8,128)(2,1)S(1)}, u32[]{:S(2)}, u32[]{:S(2)}) collective-permute-start(bf16[4,256,256]{2,1,0:T(8,128)(2,1)S(1)} %copy-done.2), channel_id=1, source_target_pairs={{1,2},{3,4},{5,6},{7,8},{9,10},{11,12},{13,14},{2,1},{4,3},{6,5},{... | collective-permute-start | bytes 1572872 | tf_op jit(solution)/shard_map/ppermute | solution.py:392
  40.0 13.9 %collective-permute-start.9 = (f32[32,768]{1,0:T(8,128)S(1)}, f32[32,768]{1,0:T(8,128)S(1)}, u32[]{:S(2)}, u32[]{:S(2)}) collective-permute-start(f32[32,768]{1,0:T(8,128)S(1)} %get-tuple-element.101), channel_id=1, source_target_pairs={{0,4},{1,5},{2,6},{3,7},{4,0},{5,1},{6,2},{7,3},{8,12},{9,13},{10,... | collective-permute-start | bytes 294920 | tf_op jit(solution)/shard_map/ppermute | solution.py:392
  53.9 5.9 %collective-permute-start.10 = (f32[32,768]{1,0:T(8,128)S(1)}, f32[32,768]{1,0:T(8,128)S(1)}, u32[]{:S(2)}, u32[]{:S(2)}) collective-permute-start(f32[32,768]{1,0:T(8,128)S(1)} %shard_map.121.own_ref), channel_id=1, source_target_pairs={{0,8},{1,9},{2,10},{3,11},{4,12},{5,13},{6,14},{7,15},{8,0},{9,1},... | collective-permute-start | bytes 294920 | tf_op jit(solution)/shard_map/ppermute | solution.py:392
  56.8 3.0 %collective-permute-start.12 = (bf16[256,128]{1,0:T(8,128)(2,1)S(1)}, bf16[256,128]{1,0:T(8,128)(2,1)S(1)}, u32[]{:S(2)}, u32[]{:S(2)}) collective-permute-start(bf16[256,128]{1,0:T(8,128)(2,1)S(1)} %get-tuple-element.118), channel_id=1, source_target_pairs={{1,2},{3,4},{5,6},{7,8},{9,10},{11,12},{13,14},{2,1},{4,3},{6,5},{... | collective-permute-start | bytes 196616 | tf_op jit(solution)/shard_map/ppermute | solution.py:392
  57.4 2.3 %collective-permute-start.11 = (bf16[256,128]{1,0:T(8,128)(2,1)S(1)}, bf16[256,128]{1,0:T(8,128)(2,1)S(1)}, u32[]{:S(2)}, u32[]{:S(2)}) collective-permute-start(bf16[256,128]{1,0:T(8,128)(2,1)S(1)} %get-tuple-element.117), channel_id=1, source_target_pairs={{0,1},{1,0},{2,3},{3,2},{4,5},{5,4},{6,7},{7,6},{8,9},{9,8},{10,11... | collective-permute-start | bytes 196616 | tf_op jit(solution)/shard_map/ppermute | solution.py:392
  60.0 1.4 %collective-permute-start.13 = (f32[8,128]{1,0:T(8,128)S(1)}, f32[8,128]{1,0:T(8,128)S(1)}, u32[]{:S(2)}, u32[]{:S(2)}) collective-permute-start(f32[8,128]{1,0:T(8,128)S(1)} %get-tuple-element.120.own_ref), channel_id=1, source_target_pairs={{0,1},{1,0},{2,3},{3,2},{4,5},{5,4},{6,7},{7,6},{8,9},{9,8},{10,11... | collective-permute-start | bytes 12296 | tf_op jit(solution)/shard_map/ppermute | solution.py:392
  61.3 3.8 %collective-permute-start.14 = (f32[8,128]{1,0:T(8,128)S(1)}, f32[8,128]{1,0:T(8,128)S(1)}, u32[]{:S(2)}, u32[]{:S(2)}) collective-permute-start(f32[8,128]{1,0:T(8,128)S(1)} %shard_map.124.own_ref), channel_id=1, source_target_pairs={{0,2},{1,3},{2,0},{3,1},{4,6},{5,7},{6,4},{7,5},{8,10},{9,11},{10,... | collective-permute-start | bytes 12296 | tf_op jit(solution)/shard_map/ppermute | solution.py:392
  65.1 5.0 %collective-permute-start.15 = (f32[8,128]{1,0:T(8,128)S(1)}, f32[8,128]{1,0:T(8,128)S(1)}, u32[]{:S(2)}, u32[]{:S(2)}) collective-permute-start(f32[8,128]{1,0:T(8,128)S(1)} %shard_map.126.sq_ref), channel_id=1, source_target_pairs={{0,4},{1,5},{2,6},{3,7},{4,0},{5,1},{6,2},{7,3},{8,12},{9,13},{10,... | collective-permute-start | bytes 12296 | tf_op jit(solution)/shard_map/ppermute | solution.py:392

commit v5 on v4

--- a/solution.py
+++ b/solution.py
@@ -236,10 +236,16 @@
 def halve_body(index_ref, own_ref, got_ref, keep_ref, send_ref, *, step):
     half = keep_ref.shape[0]
     bit = (index_ref[0] >> step) & 1
-    upper = own_ref[:half] + got_ref[:half]
-    lower = own_ref[half:] + got_ref[half:]
+    upper = own_ref[:half] + got_ref[:half].astype(f32)
+    lower = own_ref[half:] + got_ref[half:].astype(f32)
     keep_ref[...] = jnp.where(bit == 0, upper, lower)
-    send_ref[...] = jnp.where(bit == 0, lower, upper)
+    send_ref[...] = jnp.where(bit == 0, lower, upper).astype(send_ref.dtype)
+
+
+def piece_body(own_ref, got_ref, piece_ref, send_ref):
+    piece = own_ref[...] + got_ref[...].astype(f32)
+    piece_ref[...] = piece
+    send_ref[...] = piece.astype(bf16)
 
 
 def add_body(own_ref, got_ref, out_ref):
@@ -247,7 +253,7 @@
 
 
 def tail_body(index_ref, own_ref, got_ref, conv_ref, rest_ref, square_ref, *, step):
-    both = own_ref[...] + got_ref[...]
+    both = own_ref[...] + got_ref[...].astype(f32)
     share = conv_ref.shape[1]
     piece = jnp.where((index_ref[0] >> step) & 1 == 0, both[:share], both[share:])
     for tap in range(9):
@@ -458,7 +464,7 @@
 
     def halve(step, keep, got):
         half = keep.shape[0] // 2
-        return call(functools.partial(halve_body, step=step), [((half, WIDTH), f32)] * 2, (par, keep, got), scalar=True)
+        return call(functools.partial(halve_body, step=step), [((half, WIDTH), f32), ((half, WIDTH), bf16)], (par, keep, got), scalar=True)
 
     def row_grad(r, at, cerr, part, done=()):
         args = (par, cerr, first_map, second_map, second_inner, second_outer)
@@ -498,15 +504,16 @@
     ce_outer = permute(ce_b, outer)
     ce_inner = permute(ce_a, inner)
     first_outer = permute(after(first_map, ce_a), outer)
-    row, part = row_grad(0, 0, ce_edge, part)
-    done.append((0, row))
-    got, part = lax.optimization_barrier((got, part))
+    got, ce_edge, part = lax.optimization_barrier((got, ce_edge, part))
     for step in range(3, steps - 1):
         keep, send = halve(step, keep, got)
         got = swap(send, step)
-    piece = add(keep, got)
-    got = swap(piece, steps - 1)
-    first_grad, part = row_grad(rows - 1, 1, after(ce_edge, piece), part, done)
+    piece, send = call(piece_body, [(keep.shape, f32), (keep.shape, bf16)], (keep, got))
+    got = swap(send, steps - 1)
+    ce_edge = after(ce_edge, piece)
+    row, part = row_grad(0, 0, ce_edge, part)
+    done.append((0, row))
+    first_grad, part = row_grad(rows - 1, 1, ce_edge, part, done)
     got, part, ce_inner, ce_outer = lax.optimization_barrier((got, part, ce_inner, ce_outer))
     conv_raw, rest_raw, square = call(
         functools.partial(tail_body, step=steps - 1),

time: 71.1 us -> 68.3 us (0.961)
  starting transfers between devices: 31.7 us -> 29.8 us
  waiting for transfers between devices: 13.3 us -> 12.3 us
    ppermute x17, starting transfers between devices: 31.7 us -> 29.8 us  [permute(): return lax.ppermute(x, 'region', pairs)]
    ppermute x17, waiting for transfers between devices: 13.3 us -> 12.3 us  [permute(): return lax.ppermute(x, 'region', pairs)]
  transfers between devices with their start and end apart: 17 -> 17, of which waited for: 5 -> 6; matrix products, arithmetic and copies ran while one was open for 4% -> 4% of each run, Pallas kernels for 24% -> 25%
where the time goes in v5:
time: 68.3 us; the launch traced here: 68 us
  starting transfers between devices  29.8 us (44%)
  Pallas kernels  21.9 us (32%)
  waiting for transfers between devices  12.3 us (18%)
  local copies, waits for them, and re-layouts  1.86 us (3%)
  matrix products  1.12 us (2%)
  between operations  0.92 us (1%)
    ppermute x17, starting transfers between devices, permute(): return lax.ppermute(x, 'region', pairs)  29.8 us
    pallas_call x19, Pallas kernels, call(): pl.pallas_call(body, out_shape=[jax.ShapeDtypeStruct(s, d) for s, d in ou...  21.9 us
    ppermute x17, waiting for transfers between devices, permute(): return lax.ppermute(x, 'region', pairs)  12.3 us
  transfers between devices with their start and end apart: 17, of which 6 were waited for; matrix products, arithmetic and copies ran while one was open for 4% of the time, Pallas kernels for 25%

profile of v5, /device:TPU:0, one launch (start us, length us, event | category | flops | bytes accessed | tf_op | source)
XLA Modules:
  0.0 68.0 jit_solution(14139111491269799939)
XLA Ops:
  1.5 4.4 %collective-permute-start = (bf16[4,256,256]{2,1,0:T(8,128)(2,1)}, bf16[4,256,256]{2,1,0:T(8,128)(2,1)S(1)}, u32[]{:S(2)}, u32[]{:S(2)}) collective-permute-start(bf16[4,256,256]{2,1,0:T(8,128)(2,1)} %second_ref.7), channel_id=1, source_target_pairs={{0,1},{1,0},{2,3},{3,2},{4,5},{5,4},{6,7},{7,6},{8,9},{9,8},{10,11... | collective-permute-start | bytes 1572872 | tf_op jit(solution)/shard_map/ppermute | solution.py:398
  7.8 0.8 %convolution_bitcast_fusion.1 = bf16[2,256]{1,0:T(2,128)(2,1)S(1)} fusion(bf16[2,256]{1,0:T(2,128)(2,1)} %param.13, s32[256]{0:T(256)S(1)} %reshape.145), kind=kOutput, calls=%fused_computation.1 | convolution fusion | flops 327680 | bytes 3072 | tf_op jit(solution)/shard_map/jh,hg->jg/dot_general | solution.py:418
  9.0 4.0 %shard_map.110 = (bf16[4,256,128]{2,1,0:T(8,128)(2,1)S(1)}, bf16[4,256,256]{2,1,0:T(8,128)(2,1)S(1)}) custom-call(s32[1]{0:T(128)} %bitcast.index_ref.par_ref, bf16[4,256,256]{2,1,0:T(8,128)(2,1)S(1)} %copy-done.2, bf16[4,256,256]{2,1,0:T(8,128)(2,1)S(1)} %copy-done.1, bf16[4,256,256]{2,1,0:T(8,128)(2,1)S(1)} %collective-permute-done.inner_ref), custom_call_target="tpu_custom_call" | custom-call | tf_op jit(solution)/shard_map/pallas_call | solution.py:46
  13.1 1.7 %shard_map.111 = (bf16[4,256,128]{2,1,0:T(8,128)(2,1)S(1)}, bf16[256,128]{1,0:T(8,128)(2,1)S(1)}, bf16[256,128]{1,0:T(8,128)(2,1)S(1)}) custom-call(s32[1]{0:T(128)} %bitcast.index_ref.par_ref, bf16[4,256,256]{2,1,0:T(8,128)(2,1)S(1)} %get-tuple-element.74.turned_ref, bf16[4,256,128]{2,1,0:T(8,128)(2,1)S(1)} %get-tuple-element.76.old_ref, ...), custom_call_target="tpu_custom_call" | custom-call | tf_op jit(solution)/shard_map/pallas_call | solution.py:46
  14.8 5.0 %collective-permute-start.3 = (bf16[256,128]{1,0:T(8,128)(2,1)S(1)}, bf16[256,128]{1,0:T(8,128)(2,1)S(1)}, u32[]{:S(2)}, u32[]{:S(2)}) collective-permute-start(bf16[256,128]{1,0:T(8,128)(2,1)S(1)} %get-tuple-element.78), channel_id=1, source_target_pairs={{0,1},{1,0},{2,3},{3,2},{4,5},{5,4},{6,7},{7,6},{8,9},{9,8},{10,11... | collective-permute-start | bytes 196616 | tf_op jit(solution)/shard_map/ppermute | solution.py:398
  20.4 2.6 %shard_map.112 = (bf16[4,256,384]{2,1,0:T(8,128)(2,1)S(1)}, f32[2,256,256]{2,1,0:T(8,128)S(1)}, bf16[2,256,256]{2,1,0:T(8,128)(2,1)S(1)}, f32[256,1152]{1,0:T(8,128)S(1)}, f32[16,256]{1,0:T(8,128)S(1)}) custom-call(bf16[4,256,128]{2,1,0:T(8,128)(2,1)S(1)} %get-tuple-element.80.corr_ref, bf16[3,384,256]{2,1,0:T(8,128)(2,1)S(1)} %bitcast.15, ...), custom_call_target="tpu_custom_call" | custom-call | tf_op jit(solution)/shard_map/pallas_call | solution.py:46
  23.0 1.8 %shard_map.113 = (bf16[2,256,256]{2,1,0:T(8,128)(2,1)S(1)}, bf16[256,256]{1,0:T(8,128)(2,1)S(1)}, bf16[256,256]{1,0:T(8,128)(2,1)S(1)}, f32[128,768]{1,0:T(8,128)S(1)}, f32[128,768]{1,0:T(8,128)S(1)}) custom-call(s32[1]{0:T(128)} %bitcast.index_ref.par_ref, bf16[4,256,384]{2,1,0:T(8,128)(2,1)S(1)} %get-tuple-element.86.x_ref, ...), custom_call_target="tpu_custom_call" | custom-call | tf_op jit(solution)/shard_map/pallas_call | solution.py:46
  24.8 3.6 %collective-permute-start.5 = (f32[128,768]{1,0:T(8,128)S(1)}, f32[128,768]{1,0:T(8,128)S(1)}, u32[]{:S(2)}, u32[]{:S(2)}) collective-permute-start(f32[128,768]{1,0:T(8,128)S(1)} %get-tuple-element.93), channel_id=1, source_target_pairs={{0,1},{1,0},{2,3},{3,2},{4,5},{5,4},{6,7},{7,6},{8,9},{9,8},{10,11... | collective-permute-start | bytes 1179656 | tf_op jit(solution)/shard_map/ppermute | solution.py:398
  29.8 3.2 %collective-permute-start.6 = (bf16[64,768]{1,0:T(8,128)(2,1)S(1)}, bf16[64,768]{1,0:T(8,128)(2,1)S(1)}, u32[]{:S(2)}, u32[]{:S(2)}) collective-permute-start(bf16[64,768]{1,0:T(8,128)(2,1)S(1)} %get-tuple-element.95), channel_id=1, source_target_pairs={{0,2},{1,3},{2,0},{3,1},{4,6},{5,7},{6,4},{7,5},{8,10},{9,11},{10,... | collective-permute-start | bytes 294920 | tf_op jit(solution)/shard_map/ppermute | solution.py:398
  33.0 0.9 %shard_map.115 = (bf16[2,256,128]{2,1,0:T(8,128)(2,1)S(1)}, f32[2,256,128]{2,1,0:T(8,128)S(1)}) custom-call(bf16[2,256,256]{2,1,0:T(8,128)(2,1)S(1)} %get-tuple-element.97.mid_ref, bf16[2,256,256]{2,1,0:T(8,128)(2,1)S(1)} %get-tuple-element.98.edge_ref, bf16[3,384,256]{2,1,0:T(8,128)(2,1)S(1)} %bitcast.17), custom_call_target="tpu_custom_call" | custom-call | tf_op jit(solution)/shard_map/pallas_call | solution.py:46
  33.9 1.2 %shard_map.116 = (bf16[1,256,256]{2,1,0:T(8,128)(2,1)S(1)}, f32[4,256,256]{2,1,0:T(8,128)S(1)}) custom-call(s32[1]{0:T(128)} %bitcast.index_ref.par_ref, bf16[2,256,128]{2,1,0:T(8,128)(2,1)S(1)} %get-tuple-element.99.ce_ref.mid_ref, bf16[4,256,256]{2,1,0:T(8,128)(2,1)S(1)} %copy-done.2, bf16[4,256,256]{2,1,0:T(8,128)(2,1)S(1)} %copy-done.1, ...), custom_call_target="tpu_custom_call" | custom-call | tf_op jit(solution)/shard_map/pallas_call | solution.py:46
  35.0 1.2 %shard_map.117 = (bf16[1,256,256]{2,1,0:T(8,128)(2,1)S(1)}, f32[4,256,256]{2,1,0:T(8,128)S(1)}) custom-call(s32[1]{0:T(128)} %bitcast.index_ref.par_ref, bf16[2,256,128]{2,1,0:T(8,128)(2,1)S(1)} %get-tuple-element.99.ce_ref.mid_ref, bf16[4,256,256]{2,1,0:T(8,128)(2,1)S(1)} %copy-done.2, ...), custom_call_target="tpu_custom_call", output_to_operand_aliasing={{1}: (6, {})} | custom-call | tf_op jit(solution)/shard_map/pallas_call | solution.py:46
  36.2 1.3 %collective-permute-done.6.got_ref = bf16[64,768]{1,0:T(8,128)(2,1)S(1)} collective-permute-done((bf16[64,768]{1,0:T(8,128)(2,1)S(1)}, bf16[64,768]{1,0:T(8,128)(2,1)S(1)}, u32[]{:S(2)}, u32[]{:S(2)}) %collective-permute-start.6) | collective-permute-done | bytes 98336 | tf_op jit(solution)/shard_map/ppermute | solution.py:398
  38.8 5.1 %collective-permute-start.7 = (bf16[32,768]{1,0:T(8,128)(2,1)S(1)}, bf16[32,768]{1,0:T(8,128)(2,1)S(1)}, u32[]{:S(2)}, u32[]{:S(2)}) collective-permute-start(bf16[32,768]{1,0:T(8,128)(2,1)S(1)} %get-tuple-element.103), channel_id=1, source_target_pairs={{0,4},{1,5},{2,6},{3,7},{4,0},{5,1},{6,2},{7,3},{8,12},{9,13},{10,... | collective-permute-start | bytes 147464 | tf_op jit(solution)/shard_map/ppermute | solution.py:398
  44.6 2.0 %collective-permute-start.11 = (bf16[256,128]{1,0:T(8,128)(2,1)S(1)}, bf16[256,128]{1,0:T(8,128)(2,1)S(1)}, u32[]{:S(2)}, u32[]{:S(2)}) collective-permute-start(bf16[256,128]{1,0:T(8,128)(2,1)S(1)} %get-tuple-element.123), channel_id=1, source_target_pairs={{0,1},{1,0},{2,3},{3,2},{4,5},{5,4},{6,7},{7,6},{8,9},{9,8},{10,11... | collective-permute-start | bytes 196616 | tf_op jit(solution)/shard_map/ppermute | solution.py:398
  46.6 6.0 %collective-permute-done.7.got_ref = bf16[32,768]{1,0:T(8,128)(2,1)S(1)} collective-permute-done((bf16[32,768]{1,0:T(8,128)(2,1)S(1)}, bf16[32,768]{1,0:T(8,128)(2,1)S(1)}, u32[]{:S(2)}, u32[]{:S(2)}) %collective-permute-start.7) | collective-permute-done | bytes 49184 | tf_op jit(solution)/shard_map/ppermute | solution.py:398
  52.5 2.7 %collective-permute-start.10 = (bf16[32,768]{1,0:T(8,128)(2,1)S(1)}, bf16[32,768]{1,0:T(8,128)(2,1)S(1)}, u32[]{:S(2)}, u32[]{:S(2)}) collective-permute-start(bf16[32,768]{1,0:T(8,128)(2,1)S(1)} %get-tuple-element.121), channel_id=1, source_target_pairs={{0,8},{1,9},{2,10},{3,11},{4,12},{5,13},{6,14},{7,15},{8,0},{9,1},... | collective-permute-start | bytes 147464 | tf_op jit(solution)/shard_map/ppermute | solution.py:398
  55.3 1.2 %shard_map.121 = (bf16[1,256,256]{2,1,0:T(8,128)(2,1)S(1)}, f32[4,256,256]{2,1,0:T(8,128)S(1)}) custom-call(s32[1]{0:T(128)} %bitcast.index_ref.par_ref, bf16[2,256,128]{2,1,0:T(8,128)(2,1)S(1)} %get-tuple-element.114.ce_ref, bf16[4,256,256]{2,1,0:T(8,128)(2,1)S(1)} %copy-done.2, ...), custom_call_target="tpu_custom_call", output_to_operand_aliasing={{1}: (6, {})} | custom-call | tf_op jit(solution)/shard_map/pallas_call | solution.py:46
  56.4 2.3 %shard_map.122 = (bf16[4,256,256]{2,1,0:T(8,128)(2,1)}, f32[4,256,256]{2,1,0:T(8,128)S(1)}) custom-call(s32[1]{0:T(128)} %bitcast.index_ref.par_ref, bf16[2,256,128]{2,1,0:T(8,128)(2,1)S(1)} %get-tuple-element.114.ce_ref, bf16[4,256,256]{2,1,0:T(8,128)(2,1)S(1)} %copy-done.2, bf16[4,256,256]{2,1,0:T(8,128)(2,1)S(1)} %copy-done.1, ...), custom_call_target="tpu_custom_call", output_to_operand_aliasing={{1}: (6, {})} | custom-call | tf_op jit(solution)/shard_map/pallas_call | solution.py:46
  58.9 1.2 %collective-permute-done.13.got_ref = f32[8,128]{1,0:T(8,128)S(1)} collective-permute-done((f32[8,128]{1,0:T(8,128)S(1)}, f32[8,128]{1,0:T(8,128)S(1)}, u32[]{:S(2)}, u32[]{:S(2)}) %collective-permute-start.13) | collective-permute-done | bytes 4128 | tf_op jit(solution)/shard_map/ppermute | solution.py:398
  60.1 1.4 %shard_map.125.old_ref = f32[4,256,256]{2,1,0:T(8,128)S(1)} custom-call(s32[1]{0:T(128)} %bitcast.index_ref.par_ref, bf16[256,128]{1,0:T(8,128)(2,1)S(1)} %collective-permute-done.11.bands_ref, bf16[4,256,256]{2,1,0:T(8,128)(2,1)S(1)} %collective-permute-done.2.rows_ref, f32[4,256,256]{2,1,0:T(8,128)S(1)} %get-tuple-element.130.old_ref), custom_call_target="tpu_custom_call", output_to_operand_aliasing={{}: (3, {})} | custom-call | tf_op jit(solution)/shard_map/pallas_call | solution.py:46
  61.5 2.2 %collective-permute-done.14.got_ref = f32[8,128]{1,0:T(8,128)S(1)} collective-permute-done((f32[8,128]{1,0:T(8,128)S(1)}, f32[8,128]{1,0:T(8,128)S(1)}, u32[]{:S(2)}, u32[]{:S(2)}) %collective-permute-start.14) | collective-permute-done | bytes 4128 | tf_op jit(solution)/shard_map/ppermute | solution.py:398
  63.7 2.4 %shard_map.127 = bf16[4,256,256]{2,1,0:T(8,128)(2,1)} custom-call(s32[1]{0:T(128)} %bitcast.index_ref.par_ref, bf16[256,128]{1,0:T(8,128)(2,1)S(1)} %collective-permute-done.12.bands_ref, bf16[4,256,256]{2,1,0:T(8,128)(2,1)S(1)} %collective-permute-done.16.rows_ref, f32[4,256,256]{2,1,0:T(8,128)S(1)} %shard_map.125.old_ref), custom_call_target="tpu_custom_call" | custom-call | tf_op jit(solution)/shard_map/pallas_call | solution.py:46
  66.1 1.2 %collective-permute-done.15.got_ref = f32[8,128]{1,0:T(8,128)S(1)} collective-permute-done((f32[8,128]{1,0:T(8,128)S(1)}, f32[8,128]{1,0:T(8,128)S(1)}, u32[]{:S(2)}, u32[]{:S(2)}) %collective-permute-start.15) | collective-permute-done | bytes 4128 | tf_op jit(solution)/shard_map/ppermute | solution.py:398
  (50 shorter events, 7.9 us)
Async XLA Ops:
  0.6 8.0 %copy-start = (bf16[9,81,256]{2,1,0:T(8,128)(2,1)S(1)}, bf16[9,81,256]{2,1,0:T(8,128)(2,1)}, u32[]{:S(2)}) copy-start(bf16[9,81,256]{2,1,0:T(8,128)(2,1)} %param.11) | copy-start | bytes 1119748
  0.6 8.3 %copy-start.1 = (bf16[4,256,256]{2,1,0:T(8,128)(2,1)S(1)}, bf16[4,256,256]{2,1,0:T(8,128)(2,1)}, u32[]{:S(2)}) copy-start(bf16[4,256,256]{2,1,0:T(8,128)(2,1)} %second_ref.7) | copy-start | bytes 1572868
  0.7 8.3 %copy-start.2 = (bf16[4,256,256]{2,1,0:T(8,128)(2,1)S(1)}, bf16[4,256,256]{2,1,0:T(8,128)(2,1)}, u32[]{:S(2)}) copy-start(bf16[4,256,256]{2,1,0:T(8,128)(2,1)} %first_ref.9) | copy-start | bytes 1572868
  0.7 12.4 %collective-permute-start.1 = (bf16[4,256,256]{2,1,0:T(8,128)(2,1)}, bf16[4,256,256]{2,1,0:T(8,128)(2,1)S(1)}, u32[]{:S(2)}, u32[]{:S(2)}) collective-permute-start(bf16[4,256,256]{2,1,0:T(8,128)(2,1)} %second_ref.7), channel_id=1, source_target_pairs={{1,2},{3,4},{5,6},{7,8},{9,10},{11,12},{13,14},{2,1},{4,3},{6,5},{... | collective-permute-start | bytes 1572872 | tf_op jit(solution)/shard_map/ppermute | solution.py:398
  1.5 7.5 %collective-permute-start = (bf16[4,256,256]{2,1,0:T(8,128)(2,1)}, bf16[4,256,256]{2,1,0:T(8,128)(2,1)S(1)}, u32[]{:S(2)}, u32[]{:S(2)}) collective-permute-start(bf16[4,256,256]{2,1,0:T(8,128)(2,1)} %second_ref.7), channel_id=1, source_target_pairs={{0,1},{1,0},{2,3},{3,2},{4,5},{5,4},{6,7},{7,6},{8,9},{9,8},{10,11... | collective-permute-start | bytes 1572872 | tf_op jit(solution)/shard_map/ppermute | solution.py:398
  5.9 7.2 %collective-permute-start.2 = (bf16[4,256,256]{2,1,0:T(8,128)(2,1)}, bf16[4,256,256]{2,1,0:T(8,128)(2,1)S(1)}, u32[]{:S(2)}, u32[]{:S(2)}) collective-permute-start(bf16[4,256,256]{2,1,0:T(8,128)(2,1)} %first_ref.9), channel_id=1, source_target_pairs={{0,1},{1,0},{2,3},{3,2},{4,5},{5,4},{6,7},{7,6},{8,9},{9,8},{10,11... | collective-permute-start | bytes 1572872 | tf_op jit(solution)/shard_map/ppermute | solution.py:398
  9.0 11.4 %copy-start.3 = (f32[2,4,256]{2,1,0:T(4,128)S(1)}, f32[2,4,256]{2,1,0:T(4,128)}, u32[]{:S(2)}) copy-start(f32[2,4,256]{2,1,0:T(4,128)} %target_ref.3) | copy-start | bytes 24580
  14.8 8.2 %collective-permute-start.3 = (bf16[256,128]{1,0:T(8,128)(2,1)S(1)}, bf16[256,128]{1,0:T(8,128)(2,1)S(1)}, u32[]{:S(2)}, u32[]{:S(2)}) collective-permute-start(bf16[256,128]{1,0:T(8,128)(2,1)S(1)} %get-tuple-element.78), channel_id=1, source_target_pairs={{0,1},{1,0},{2,3},{3,2},{4,5},{5,4},{6,7},{7,6},{8,9},{9,8},{10,11... | collective-permute-start | bytes 196616 | tf_op jit(solution)/shard_map/ppermute | solution.py:398
  19.7 3.3 %collective-permute-start.4 = (bf16[256,128]{1,0:T(8,128)(2,1)S(1)}, bf16[256,128]{1,0:T(8,128)(2,1)S(1)}, u32[]{:S(2)}, u32[]{:S(2)}) collective-permute-start(bf16[256,128]{1,0:T(8,128)(2,1)S(1)} %get-tuple-element.79), channel_id=1, source_target_pairs={{1,2},{3,4},{5,6},{7,8},{9,10},{11,12},{13,14},{2,1},{4,3},{6,5},{... | collective-permute-start | bytes 196616 | tf_op jit(solution)/shard_map/ppermute | solution.py:398
  24.8 4.9 %collective-permute-start.5 = (f32[128,768]{1,0:T(8,128)S(1)}, f32[128,768]{1,0:T(8,128)S(1)}, u32[]{:S(2)}, u32[]{:S(2)}) collective-permute-start(f32[128,768]{1,0:T(8,128)S(1)} %get-tuple-element.93), channel_id=1, source_target_pairs={{0,1},{1,0},{2,3},{3,2},{4,5},{5,4},{6,7},{7,6},{8,9},{9,8},{10,11... | collective-permute-start | bytes 1179656 | tf_op jit(solution)/shard_map/ppermute | solution.py:398
  28.4 9.2 %collective-permute-start.8 = (bf16[256,256]{1,0:T(8,128)(2,1)S(1)}, bf16[256,256]{1,0:T(8,128)(2,1)S(1)}, u32[]{:S(2)}, u32[]{:S(2)}) collective-permute-start(bf16[256,256]{1,0:T(8,128)(2,1)S(1)} %get-tuple-element.106), channel_id=1, source_target_pairs={{0,1},{1,0},{2,3},{3,2},{4,5},{5,4},{6,7},{7,6},{8,9},{9,8},{10,11... | collective-permute-start | bytes 393224 | tf_op jit(solution)/shard_map/ppermute | solution.py:398
  28.5 9.1 %collective-permute-start.9 = (bf16[256,256]{1,0:T(8,128)(2,1)S(1)}, bf16[256,256]{1,0:T(8,128)(2,1)S(1)}, u32[]{:S(2)}, u32[]{:S(2)}) collective-permute-start(bf16[256,256]{1,0:T(8,128)(2,1)S(1)} %get-tuple-element.107), channel_id=1, source_target_pairs={{1,2},{3,4},{5,6},{7,8},{9,10},{11,12},{13,14},{2,1},{4,3},{6,5},{... | collective-permute-start | bytes 393224 | tf_op jit(solution)/shard_map/ppermute | solution.py:398
  29.8 7.8 %collective-permute-start.6 = (bf16[64,768]{1,0:T(8,128)(2,1)S(1)}, bf16[64,768]{1,0:T(8,128)(2,1)S(1)}, u32[]{:S(2)}, u32[]{:S(2)}) collective-permute-start(bf16[64,768]{1,0:T(8,128)(2,1)S(1)} %get-tuple-element.95), channel_id=1, source_target_pairs={{0,2},{1,3},{2,0},{3,1},{4,6},{5,7},{6,4},{7,5},{8,10},{9,11},{10,... | collective-permute-start | bytes 294920 | tf_op jit(solution)/shard_map/ppermute | solution.py:398
  38.1 25.6 %collective-permute-start.16 = (bf16[4,256,256]{2,1,0:T(8,128)(2,1)S(1)}, bf16[4,256,256]{2,1,0:T(8,128)(2,1)S(1)}, u32[]{:S(2)}, u32[]{:S(2)}) collective-permute-start(bf16[4,256,256]{2,1,0:T(8,128)(2,1)S(1)} %copy-done.2), channel_id=1, source_target_pairs={{1,2},{3,4},{5,6},{7,8},{9,10},{11,12},{13,14},{2,1},{4,3},{6,5},{... | collective-permute-start | bytes 1572872 | tf_op jit(solution)/shard_map/ppermute | solution.py:398
  38.8 13.7 %collective-permute-start.7 = (bf16[32,768]{1,0:T(8,128)(2,1)S(1)}, bf16[32,768]{1,0:T(8,128)(2,1)S(1)}, u32[]{:S(2)}, u32[]{:S(2)}) collective-permute-start(bf16[32,768]{1,0:T(8,128)(2,1)S(1)} %get-tuple-element.103), channel_id=1, source_target_pairs={{0,4},{1,5},{2,6},{3,7},{4,0},{5,1},{6,2},{7,3},{8,12},{9,13},{10,... | collective-permute-start | bytes 147464 | tf_op jit(solution)/shard_map/ppermute | solution.py:398
  43.9 14.7 %collective-permute-start.12 = (bf16[256,128]{1,0:T(8,128)(2,1)S(1)}, bf16[256,128]{1,0:T(8,128)(2,1)S(1)}, u32[]{:S(2)}, u32[]{:S(2)}) collective-permute-start(bf16[256,128]{1,0:T(8,128)(2,1)S(1)} %get-tuple-element.124), channel_id=1, source_target_pairs={{1,2},{3,4},{5,6},{7,8},{9,10},{11,12},{13,14},{2,1},{4,3},{6,5},{... | collective-permute-start | bytes 196616 | tf_op jit(solution)/shard_map/ppermute | solution.py:398
  44.6 14.1 %collective-permute-start.11 = (bf16[256,128]{1,0:T(8,128)(2,1)S(1)}, bf16[256,128]{1,0:T(8,128)(2,1)S(1)}, u32[]{:S(2)}, u32[]{:S(2)}) collective-permute-start(bf16[256,128]{1,0:T(8,128)(2,1)S(1)} %get-tuple-element.123), channel_id=1, source_target_pairs={{0,1},{1,0},{2,3},{3,2},{4,5},{5,4},{6,7},{7,6},{8,9},{9,8},{10,11... | collective-permute-start | bytes 196616 | tf_op jit(solution)/shard_map/ppermute | solution.py:398
  52.5 6.1 %collective-permute-start.10 = (bf16[32,768]{1,0:T(8,128)(2,1)S(1)}, bf16[32,768]{1,0:T(8,128)(2,1)S(1)}, u32[]{:S(2)}, u32[]{:S(2)}) collective-permute-start(bf16[32,768]{1,0:T(8,128)(2,1)S(1)} %get-tuple-element.121), channel_id=1, source_target_pairs={{0,8},{1,9},{2,10},{3,11},{4,12},{5,13},{6,14},{7,15},{8,0},{9,1},... | collective-permute-start | bytes 147464 | tf_op jit(solution)/shard_map/ppermute | solution.py:398
  58.8 1.2 %collective-permute-start.13 = (f32[8,128]{1,0:T(8,128)S(1)}, f32[8,128]{1,0:T(8,128)S(1)}, u32[]{:S(2)}, u32[]{:S(2)}) collective-permute-start(f32[8,128]{1,0:T(8,128)S(1)} %get-tuple-element.126.own_ref), channel_id=1, source_target_pairs={{0,1},{1,0},{2,3},{3,2},{4,5},{5,4},{6,7},{7,6},{8,9},{9,8},{10,11... | collective-permute-start | bytes 12296 | tf_op jit(solution)/shard_map/ppermute | solution.py:398
  60.1 3.6 %collective-permute-start.14 = (f32[8,128]{1,0:T(8,128)S(1)}, f32[8,128]{1,0:T(8,128)S(1)}, u32[]{:S(2)}, u32[]{:S(2)}) collective-permute-start(f32[8,128]{1,0:T(8,128)S(1)} %shard_map.124.own_ref), channel_id=1, source_target_pairs={{0,2},{1,3},{2,0},{3,1},{4,6},{5,7},{6,4},{7,5},{8,10},{9,11},{10,... | collective-permute-start | bytes 12296 | tf_op jit(solution)/shard_map/ppermute | solution.py:398
  63.7 3.6 %collective-permute-start.15 = (f32[8,128]{1,0:T(8,128)S(1)}, f32[8,128]{1,0:T(8,128)S(1)}, u32[]{:S(2)}, u32[]{:S(2)}) collective-permute-start(f32[8,128]{1,0:T(8,128)S(1)} %shard_map.126.sq_ref), channel_id=1, source_target_pairs={{0,4},{1,5},{2,6},{3,7},{4,0},{5,1},{6,2},{7,3},{8,12},{9,13},{10,... | collective-permute-start | bytes 12296 | tf_op jit(solution)/shard_map/ppermute | solution.py:398

commit v6 on v5

--- a/solution.py
+++ b/solution.py
@@ -39,7 +39,7 @@
 VMEM = pl.BlockSpec(memory_space=pltpu.VMEM)
 
 
-def call(body, outs, args, scratch=(), scalar=False, alias=None):
+def call(body, outs, args, scratch=(), scalar=False, alias=None, first_any=False):
     specs = [VMEM] * len(args)
     if scalar:
         specs[0] = SMEM
@@ -47,7 +47,7 @@
         body,
         out_shape=[jax.ShapeDtypeStruct(s, d) for s, d in outs],
         in_specs=specs,
-        out_specs=[VMEM] * len(outs),
+        out_specs=[pl.BlockSpec(memory_space=pl.ANY) if first_any and i == 0 else VMEM for i in range(len(outs))],
         scratch_shapes=list(scratch),
         input_output_aliases=alias or {},
         compiler_params=pltpu.CompilerParams(vmem_limit_bytes=VMEM_LIMIT),
@@ -330,6 +330,15 @@
 
 
 def row_grad_body(index_ref, ce_ref, first_ref, second_ref, inner_ref, outer_ref, *refs, r, at, done):
+    copies = []
+    if done:
+        *refs, own_ref, sems = refs
+        copies = [
+            pltpu.make_async_copy(row_ref.at[0], refs[-2].at[other], sems.at[i])
+            for i, (other, row_ref) in enumerate(zip(done, refs[1:]))
+        ]
+        for copy in copies:
+            copy.start()
     fg_ref, part_ref = refs[-2:]
     old_ref = refs[0] if len(refs) > 2 else None
     rows, cols = first_ref.shape[0], first_ref.shape[1]
@@ -350,9 +359,14 @@
         if 0 <= q < rows:
             gave = dot(turned, spread)
             part_ref[q] = gave if old_ref is None else old_ref[q] + gave
-    fg_ref[r if done else 0] = acc.astype(bf16)
-    for other, row_ref in zip(done, refs[1:]):
-        fg_ref[other] = row_ref[0]
+    if not done:
+        fg_ref[0] = acc.astype(bf16)
+        return
+    own_ref[...] = acc.astype(bf16)
+    copies.append(pltpu.make_async_copy(own_ref, fg_ref.at[r], sems.at[len(done)]))
+    copies[-1].start()
+    for copy in copies:
+        copy.wait()
 
 
 def halo_parts(bands_ref, rows_ref, below, old_ref):
@@ -376,10 +390,28 @@
     by_side(index_ref[0] & 1 == 0, side)
 
 
-def halo_outer_body(index_ref, bands_ref, rows_ref, old_ref, sg_ref):
+def halo_outer_body(index_ref, bands_ref, rows_ref, old_ref, sg_ref, out_ref, sems):
+    rows = old_ref.shape[0]
+    bands = bands_ref[...].astype(f32)
+
     def side(below):
-        for q, part in enumerate(halo_parts(bands_ref, rows_ref, below, old_ref)):
-            sg_ref[q] = part.T.astype(bf16)
+        parts = [old_ref[q] for q in range(rows)]
+        copies = []
+        for r in range(rows) if below else reversed(range(rows)):
+            turned = rows_ref[r].T
+            if below:
+                slot = sum(RADIUS - i for i in range(r))
+                ends = range(rows + r - RADIUS, rows)
+            else:
+                slot = sum(i + RADIUS + 1 - rows for i in range(r))
+                ends = range(0, r + RADIUS + 1 - rows)
+            for i, q in enumerate(ends):
+                parts[q] = parts[q] + dot(turned, spread_of(bands, slot + i))
+            out_ref[r] = parts[r].T.astype(bf16)
+            copies.append(pltpu.make_async_copy(out_ref.at[r], sg_ref.at[r], sems.at[r]))
+            copies[-1].start()
+        for copy in copies:
+            copy.wait()
 
     by_side(index_ref[0] & 1 == 1, side)
 
@@ -474,8 +506,10 @@
             functools.partial(row_grad_body, r=r, at=at, done=[other for other, _ in done]),
             [((rows if done else 1, cols, C), bf16), ((rows, C, cols), f32)],
             args,
+            scratch=[vector(cols, C), pltpu.SemaphoreType.DMA((rows,))] if done else (),
             scalar=True,
             alias=None if part is None else {6: 1},
+            first_any=bool(done),
         )
 
     steps = len(radix)
@@ -513,8 +547,7 @@
     ce_edge = after(ce_edge, piece)
     row, part = row_grad(0, 0, ce_edge, part)
     done.append((0, row))
-    first_grad, part = row_grad(rows - 1, 1, ce_edge, part, done)
-    got, part, ce_inner, ce_outer = lax.optimization_barrier((got, part, ce_inner, ce_outer))
+    got, part = lax.optimization_barrier((got, part))
     conv_raw, rest_raw, square = call(
         functools.partial(tail_body, step=steps - 1),
         [((9, share, K), f32), ((3, share), f32), ((8, LANES), f32)],
@@ -524,6 +557,7 @@
     got = swap(square, 0)
     square = add(square, got)
     got = swap(square, 1)
+    first_grad, part = row_grad(rows - 1, 1, after(ce_edge, square), part, done)
     (part,) = call(
         halo_inner_body,
         [((rows, C, cols), f32)],
@@ -538,7 +572,9 @@
         halo_outer_body,
         [((rows, cols, C), bf16)],
         (par, after(ce_outer, square), first_outer, part),
+        scratch=[vector(rows, cols, C), pltpu.SemaphoreType.DMA((rows,))],
         scalar=True,
+        first_any=True,
     )
     got, second_grad = lax.optimization_barrier((got, second_grad))
     for step in range(3, steps - 1):

time: 68.3 us -> 67 us (0.981)
  waiting for transfers between devices: 12.3 us -> 11.4 us
    ppermute x17, waiting for transfers between devices: 12.3 us -> 11.4 us  [permute(): return lax.ppermute(x, 'region', pairs)]
  transfers between devices with their start and end apart: 17 -> 17, of which waited for: 6 -> 6; matrix products, arithmetic and copies ran while one was open for 4% -> 4% of each run, Pallas kernels for 25% -> 26%
where the time goes in v6:
time: 67 us; the launch traced here: 66.7 us
  starting transfers between devices  29.5 us (44%)
  Pallas kernels  21.9 us (33%)
  waiting for transfers between devices  11.4 us (17%)
  local copies, waits for them, and re-layouts  1.86 us (3%)
  matrix products  1.12 us (2%)
  between operations  0.93 us (1%)
    ppermute x17, starting transfers between devices, permute(): return lax.ppermute(x, 'region', pairs)  29.5 us
    pallas_call x19, Pallas kernels, call(): pl.pallas_call(body, out_shape=[jax.ShapeDtypeStruct(s, d) for s, d in ou...  21.9 us
    ppermute x17, waiting for transfers between devices, permute(): return lax.ppermute(x, 'region', pairs)  11.4 us
  transfers between devices with their start and end apart: 17, of which 6 were waited for; matrix products, arithmetic and copies ran while one was open for 4% of the time, Pallas kernels for 26%

profile of v6, /device:TPU:0, one launch (start us, length us, event | category | flops | bytes accessed | tf_op | source)
XLA Modules:
  0.0 66.7 jit_solution(869688634795932442)
XLA Ops:
  1.5 4.4 %collective-permute-start = (bf16[4,256,256]{2,1,0:T(8,128)(2,1)}, bf16[4,256,256]{2,1,0:T(8,128)(2,1)S(1)}, u32[]{:S(2)}, u32[]{:S(2)}) collective-permute-start(bf16[4,256,256]{2,1,0:T(8,128)(2,1)} %second_ref.7), channel_id=1, source_target_pairs={{0,1},{1,0},{2,3},{3,2},{4,5},{5,4},{6,7},{7,6},{8,9},{9,8},{10,11... | collective-permute-start | bytes 1572872 | tf_op jit(solution)/shard_map/ppermute | solution.py:430
  7.8 0.8 %convolution_bitcast_fusion.1 = bf16[2,256]{1,0:T(2,128)(2,1)S(1)} fusion(bf16[2,256]{1,0:T(2,128)(2,1)} %param.13, s32[256]{0:T(256)S(1)} %reshape.145), kind=kOutput, calls=%fused_computation.1 | convolution fusion | flops 327680 | bytes 3072 | tf_op jit(solution)/shard_map/jh,hg->jg/dot_general | solution.py:450
  9.0 4.0 %shard_map.110 = (bf16[4,256,128]{2,1,0:T(8,128)(2,1)S(1)}, bf16[4,256,256]{2,1,0:T(8,128)(2,1)S(1)}) custom-call(s32[1]{0:T(128)} %bitcast.index_ref.par_ref, bf16[4,256,256]{2,1,0:T(8,128)(2,1)S(1)} %copy-done.2, bf16[4,256,256]{2,1,0:T(8,128)(2,1)S(1)} %copy-done.1, bf16[4,256,256]{2,1,0:T(8,128)(2,1)S(1)} %collective-permute-done.inner_ref), custom_call_target="tpu_custom_call" | custom-call | tf_op jit(solution)/shard_map/pallas_call | solution.py:46
  13.1 1.7 %shard_map.111 = (bf16[4,256,128]{2,1,0:T(8,128)(2,1)S(1)}, bf16[256,128]{1,0:T(8,128)(2,1)S(1)}, bf16[256,128]{1,0:T(8,128)(2,1)S(1)}) custom-call(s32[1]{0:T(128)} %bitcast.index_ref.par_ref, bf16[4,256,256]{2,1,0:T(8,128)(2,1)S(1)} %get-tuple-element.73.turned_ref, bf16[4,256,128]{2,1,0:T(8,128)(2,1)S(1)} %get-tuple-element.75.old_ref, ...), custom_call_target="tpu_custom_call" | custom-call | tf_op jit(solution)/shard_map/pallas_call | solution.py:46
  14.8 5.0 %collective-permute-start.3 = (bf16[256,128]{1,0:T(8,128)(2,1)S(1)}, bf16[256,128]{1,0:T(8,128)(2,1)S(1)}, u32[]{:S(2)}, u32[]{:S(2)}) collective-permute-start(bf16[256,128]{1,0:T(8,128)(2,1)S(1)} %get-tuple-element.77), channel_id=1, source_target_pairs={{0,1},{1,0},{2,3},{3,2},{4,5},{5,4},{6,7},{7,6},{8,9},{9,8},{10,11... | collective-permute-start | bytes 196616 | tf_op jit(solution)/shard_map/ppermute | solution.py:430
  20.4 2.6 %shard_map.112 = (bf16[4,256,384]{2,1,0:T(8,128)(2,1)S(1)}, f32[2,256,256]{2,1,0:T(8,128)S(1)}, bf16[2,256,256]{2,1,0:T(8,128)(2,1)S(1)}, f32[256,1152]{1,0:T(8,128)S(1)}, f32[16,256]{1,0:T(8,128)S(1)}) custom-call(bf16[4,256,128]{2,1,0:T(8,128)(2,1)S(1)} %get-tuple-element.79.corr_ref, bf16[3,384,256]{2,1,0:T(8,128)(2,1)S(1)} %bitcast.15, ...), custom_call_target="tpu_custom_call" | custom-call | tf_op jit(solution)/shard_map/pallas_call | solution.py:46
  23.0 1.8 %shard_map.113 = (bf16[2,256,256]{2,1,0:T(8,128)(2,1)S(1)}, bf16[256,256]{1,0:T(8,128)(2,1)S(1)}, bf16[256,256]{1,0:T(8,128)(2,1)S(1)}, f32[128,768]{1,0:T(8,128)S(1)}, f32[128,768]{1,0:T(8,128)S(1)}) custom-call(s32[1]{0:T(128)} %bitcast.index_ref.par_ref, bf16[4,256,384]{2,1,0:T(8,128)(2,1)S(1)} %get-tuple-element.85.x_ref, ...), custom_call_target="tpu_custom_call" | custom-call | tf_op jit(solution)/shard_map/pallas_call | solution.py:46
  24.8 3.6 %collective-permute-start.5 = (f32[128,768]{1,0:T(8,128)S(1)}, f32[128,768]{1,0:T(8,128)S(1)}, u32[]{:S(2)}, u32[]{:S(2)}) collective-permute-start(f32[128,768]{1,0:T(8,128)S(1)} %get-tuple-element.92), channel_id=1, source_target_pairs={{0,1},{1,0},{2,3},{3,2},{4,5},{5,4},{6,7},{7,6},{8,9},{9,8},{10,11... | collective-permute-start | bytes 1179656 | tf_op jit(solution)/shard_map/ppermute | solution.py:430
  28.5 0.8 %collective-permute-start.9 = (bf16[256,256]{1,0:T(8,128)(2,1)S(1)}, bf16[256,256]{1,0:T(8,128)(2,1)S(1)}, u32[]{:S(2)}, u32[]{:S(2)}) collective-permute-start(bf16[256,256]{1,0:T(8,128)(2,1)S(1)} %get-tuple-element.106), channel_id=1, source_target_pairs={{1,2},{3,4},{5,6},{7,8},{9,10},{11,12},{13,14},{2,1},{4,3},{6,5},{... | collective-permute-start | bytes 393224 | tf_op jit(solution)/shard_map/ppermute | solution.py:430
  29.8 3.2 %collective-permute-start.6 = (bf16[64,768]{1,0:T(8,128)(2,1)S(1)}, bf16[64,768]{1,0:T(8,128)(2,1)S(1)}, u32[]{:S(2)}, u32[]{:S(2)}) collective-permute-start(bf16[64,768]{1,0:T(8,128)(2,1)S(1)} %get-tuple-element.94), channel_id=1, source_target_pairs={{0,2},{1,3},{2,0},{3,1},{4,6},{5,7},{6,4},{7,5},{8,10},{9,11},{10,... | collective-permute-start | bytes 294920 | tf_op jit(solution)/shard_map/ppermute | solution.py:430
  33.0 0.9 %shard_map.115 = (bf16[2,256,128]{2,1,0:T(8,128)(2,1)S(1)}, f32[2,256,128]{2,1,0:T(8,128)S(1)}) custom-call(bf16[2,256,256]{2,1,0:T(8,128)(2,1)S(1)} %get-tuple-element.96.mid_ref, bf16[2,256,256]{2,1,0:T(8,128)(2,1)S(1)} %get-tuple-element.97.edge_ref, bf16[3,384,256]{2,1,0:T(8,128)(2,1)S(1)} %bitcast.17), custom_call_target="tpu_custom_call" | custom-call | tf_op jit(solution)/shard_map/pallas_call | solution.py:46
  33.9 1.2 %shard_map.116 = (bf16[1,256,256]{2,1,0:T(8,128)(2,1)S(1)}, f32[4,256,256]{2,1,0:T(8,128)S(1)}) custom-call(s32[1]{0:T(128)} %bitcast.index_ref.par_ref, bf16[2,256,128]{2,1,0:T(8,128)(2,1)S(1)} %get-tuple-element.98.ce_ref.mid_ref, bf16[4,256,256]{2,1,0:T(8,128)(2,1)S(1)} %copy-done.2, bf16[4,256,256]{2,1,0:T(8,128)(2,1)S(1)} %copy-done.1, ...), custom_call_target="tpu_custom_call" | custom-call | tf_op jit(solution)/shard_map/pallas_call | solution.py:46
  35.0 1.2 %shard_map.117 = (bf16[1,256,256]{2,1,0:T(8,128)(2,1)S(1)}, f32[4,256,256]{2,1,0:T(8,128)S(1)}) custom-call(s32[1]{0:T(128)} %bitcast.index_ref.par_ref, bf16[2,256,128]{2,1,0:T(8,128)(2,1)S(1)} %get-tuple-element.98.ce_ref.mid_ref, bf16[4,256,256]{2,1,0:T(8,128)(2,1)S(1)} %copy-done.2, ...), custom_call_target="tpu_custom_call", output_to_operand_aliasing={{1}: (6, {})} | custom-call | tf_op jit(solution)/shard_map/pallas_call | solution.py:46
  36.2 1.3 %collective-permute-done.6.got_ref = bf16[64,768]{1,0:T(8,128)(2,1)S(1)} collective-permute-done((bf16[64,768]{1,0:T(8,128)(2,1)S(1)}, bf16[64,768]{1,0:T(8,128)(2,1)S(1)}, u32[]{:S(2)}, u32[]{:S(2)}) %collective-permute-start.6) | collective-permute-done | bytes 98336 | tf_op jit(solution)/shard_map/ppermute | solution.py:430
  38.8 5.1 %collective-permute-start.7 = (bf16[32,768]{1,0:T(8,128)(2,1)S(1)}, bf16[32,768]{1,0:T(8,128)(2,1)S(1)}, u32[]{:S(2)}, u32[]{:S(2)}) collective-permute-start(bf16[32,768]{1,0:T(8,128)(2,1)S(1)} %get-tuple-element.102), channel_id=1, source_target_pairs={{0,4},{1,5},{2,6},{3,7},{4,0},{5,1},{6,2},{7,3},{8,12},{9,13},{10,... | collective-permute-start | bytes 147464 | tf_op jit(solution)/shard_map/ppermute | solution.py:430
  44.8 7.2 %collective-permute-done.7.got_ref = bf16[32,768]{1,0:T(8,128)(2,1)S(1)} collective-permute-done((bf16[32,768]{1,0:T(8,128)(2,1)S(1)}, bf16[32,768]{1,0:T(8,128)(2,1)S(1)}, u32[]{:S(2)}, u32[]{:S(2)}) %collective-permute-start.7) | collective-permute-done | bytes 49184 | tf_op jit(solution)/shard_map/ppermute | solution.py:430
  52.0 3.2 %collective-permute-start.10 = (bf16[32,768]{1,0:T(8,128)(2,1)S(1)}, bf16[32,768]{1,0:T(8,128)(2,1)S(1)}, u32[]{:S(2)}, u32[]{:S(2)}) collective-permute-start(bf16[32,768]{1,0:T(8,128)(2,1)S(1)} %get-tuple-element.114), channel_id=1, source_target_pairs={{0,8},{1,9},{2,10},{3,11},{4,12},{5,13},{6,14},{7,15},{8,0},{9,1},... | collective-permute-start | bytes 147464 | tf_op jit(solution)/shard_map/ppermute | solution.py:430
  55.3 1.2 %shard_map.121 = (bf16[1,256,256]{2,1,0:T(8,128)(2,1)S(1)}, f32[4,256,256]{2,1,0:T(8,128)S(1)}) custom-call(s32[1]{0:T(128)} %bitcast.index_ref.par_ref, bf16[2,256,128]{2,1,0:T(8,128)(2,1)S(1)} %get-tuple-element.119.ce_ref, bf16[4,256,256]{2,1,0:T(8,128)(2,1)S(1)} %copy-done.2, ...), custom_call_target="tpu_custom_call", output_to_operand_aliasing={{1}: (6, {})} | custom-call | tf_op jit(solution)/shard_map/pallas_call | solution.py:46
  56.4 0.9 %collective-permute-done.10.got_ref = bf16[32,768]{1,0:T(8,128)(2,1)S(1)} collective-permute-done((bf16[32,768]{1,0:T(8,128)(2,1)S(1)}, bf16[32,768]{1,0:T(8,128)(2,1)S(1)}, u32[]{:S(2)}, u32[]{:S(2)}) %collective-permute-start.10) | collective-permute-done | bytes 49184 | tf_op jit(solution)/shard_map/ppermute | solution.py:430
  57.6 1.2 %collective-permute-done.11.got_ref = f32[8,128]{1,0:T(8,128)S(1)} collective-permute-done((f32[8,128]{1,0:T(8,128)S(1)}, f32[8,128]{1,0:T(8,128)S(1)}, u32[]{:S(2)}, u32[]{:S(2)}) %collective-permute-start.11) | collective-permute-done | bytes 4128 | tf_op jit(solution)/shard_map/ppermute | solution.py:430
  58.7 2.1 %shard_map.124 = (bf16[4,256,256]{2,1,0:T(8,128)(2,1)}, f32[4,256,256]{2,1,0:T(8,128)S(1)}) custom-call(s32[1]{0:T(128)} %bitcast.index_ref.par_ref, bf16[2,256,128]{2,1,0:T(8,128)(2,1)S(1)} %get-tuple-element.119.ce_ref, bf16[4,256,256]{2,1,0:T(8,128)(2,1)S(1)} %copy-done.2, bf16[4,256,256]{2,1,0:T(8,128)(2,1)S(1)} %copy-done.1, ...), custom_call_target="tpu_custom_call", output_to_operand_aliasing={{1}: (6, {})} | custom-call | tf_op jit(solution)/shard_map/pallas_call | solution.py:46
  60.9 1.4 %shard_map.125.old_ref = f32[4,256,256]{2,1,0:T(8,128)S(1)} custom-call(s32[1]{0:T(128)} %bitcast.index_ref.par_ref, bf16[256,128]{1,0:T(8,128)(2,1)S(1)} %collective-permute-done.13.bands_ref, bf16[4,256,256]{2,1,0:T(8,128)(2,1)S(1)} %collective-permute-done.2.rows_ref, f32[4,256,256]{2,1,0:T(8,128)S(1)} %get-tuple-element.128.old_ref), custom_call_target="tpu_custom_call", output_to_operand_aliasing={{}: (3, {})} | custom-call | tf_op jit(solution)/shard_map/pallas_call | solution.py:46
  62.3 0.9 %collective-permute-start.14 = (f32[8,128]{1,0:T(8,128)S(1)}, f32[8,128]{1,0:T(8,128)S(1)}, u32[]{:S(2)}, u32[]{:S(2)}) collective-permute-start(f32[8,128]{1,0:T(8,128)S(1)} %shard_map.126.sq_ref), channel_id=1, source_target_pairs={{0,4},{1,5},{2,6},{3,7},{4,0},{5,1},{6,2},{7,3},{8,12},{9,13},{10,... | collective-permute-start | bytes 12296 | tf_op jit(solution)/shard_map/ppermute | solution.py:430
  63.2 2.4 %shard_map.127 = bf16[4,256,256]{2,1,0:T(8,128)(2,1)} custom-call(s32[1]{0:T(128)} %bitcast.index_ref.par_ref, bf16[256,128]{1,0:T(8,128)(2,1)S(1)} %collective-permute-done.15.bands_ref, bf16[4,256,256]{2,1,0:T(8,128)(2,1)S(1)} %collective-permute-done.16.rows_ref, f32[4,256,256]{2,1,0:T(8,128)S(1)} %shard_map.125.old_ref), custom_call_target="tpu_custom_call" | custom-call | tf_op jit(solution)/shard_map/pallas_call | solution.py:46
  (50 shorter events, 7.6 us)
Async XLA Ops:
  0.6 8.0 %copy-start = (bf16[9,81,256]{2,1,0:T(8,128)(2,1)S(1)}, bf16[9,81,256]{2,1,0:T(8,128)(2,1)}, u32[]{:S(2)}) copy-start(bf16[9,81,256]{2,1,0:T(8,128)(2,1)} %param.11) | copy-start | bytes 1119748
  0.6 8.3 %copy-start.1 = (bf16[4,256,256]{2,1,0:T(8,128)(2,1)S(1)}, bf16[4,256,256]{2,1,0:T(8,128)(2,1)}, u32[]{:S(2)}) copy-start(bf16[4,256,256]{2,1,0:T(8,128)(2,1)} %second_ref.7) | copy-start | bytes 1572868
  0.7 8.3 %copy-start.2 = (bf16[4,256,256]{2,1,0:T(8,128)(2,1)S(1)}, bf16[4,256,256]{2,1,0:T(8,128)(2,1)}, u32[]{:S(2)}) copy-start(bf16[4,256,256]{2,1,0:T(8,128)(2,1)} %first_ref.9) | copy-start | bytes 1572868
  0.7 12.4 %collective-permute-start.1 = (bf16[4,256,256]{2,1,0:T(8,128)(2,1)}, bf16[4,256,256]{2,1,0:T(8,128)(2,1)S(1)}, u32[]{:S(2)}, u32[]{:S(2)}) collective-permute-start(bf16[4,256,256]{2,1,0:T(8,128)(2,1)} %second_ref.7), channel_id=1, source_target_pairs={{1,2},{3,4},{5,6},{7,8},{9,10},{11,12},{13,14},{2,1},{4,3},{6,5},{... | collective-permute-start | bytes 1572872 | tf_op jit(solution)/shard_map/ppermute | solution.py:430
  1.5 7.5 %collective-permute-start = (bf16[4,256,256]{2,1,0:T(8,128)(2,1)}, bf16[4,256,256]{2,1,0:T(8,128)(2,1)S(1)}, u32[]{:S(2)}, u32[]{:S(2)}) collective-permute-start(bf16[4,256,256]{2,1,0:T(8,128)(2,1)} %second_ref.7), channel_id=1, source_target_pairs={{0,1},{1,0},{2,3},{3,2},{4,5},{5,4},{6,7},{7,6},{8,9},{9,8},{10,11... | collective-permute-start | bytes 1572872 | tf_op jit(solution)/shard_map/ppermute | solution.py:430
  5.9 7.2 %collective-permute-start.2 = (bf16[4,256,256]{2,1,0:T(8,128)(2,1)}, bf16[4,256,256]{2,1,0:T(8,128)(2,1)S(1)}, u32[]{:S(2)}, u32[]{:S(2)}) collective-permute-start(bf16[4,256,256]{2,1,0:T(8,128)(2,1)} %first_ref.9), channel_id=1, source_target_pairs={{0,1},{1,0},{2,3},{3,2},{4,5},{5,4},{6,7},{7,6},{8,9},{9,8},{10,11... | collective-permute-start | bytes 1572872 | tf_op jit(solution)/shard_map/ppermute | solution.py:430
  9.0 11.4 %copy-start.3 = (f32[2,4,256]{2,1,0:T(4,128)S(1)}, f32[2,4,256]{2,1,0:T(4,128)}, u32[]{:S(2)}) copy-start(f32[2,4,256]{2,1,0:T(4,128)} %target_ref.3) | copy-start | bytes 24580
  14.8 8.2 %collective-permute-start.3 = (bf16[256,128]{1,0:T(8,128)(2,1)S(1)}, bf16[256,128]{1,0:T(8,128)(2,1)S(1)}, u32[]{:S(2)}, u32[]{:S(2)}) collective-permute-start(bf16[256,128]{1,0:T(8,128)(2,1)S(1)} %get-tuple-element.77), channel_id=1, source_target_pairs={{0,1},{1,0},{2,3},{3,2},{4,5},{5,4},{6,7},{7,6},{8,9},{9,8},{10,11... | collective-permute-start | bytes 196616 | tf_op jit(solution)/shard_map/ppermute | solution.py:430
  19.7 3.3 %collective-permute-start.4 = (bf16[256,128]{1,0:T(8,128)(2,1)S(1)}, bf16[256,128]{1,0:T(8,128)(2,1)S(1)}, u32[]{:S(2)}, u32[]{:S(2)}) collective-permute-start(bf16[256,128]{1,0:T(8,128)(2,1)S(1)} %get-tuple-element.78), channel_id=1, source_target_pairs={{1,2},{3,4},{5,6},{7,8},{9,10},{11,12},{13,14},{2,1},{4,3},{6,5},{... | collective-permute-start | bytes 196616 | tf_op jit(solution)/shard_map/ppermute | solution.py:430
  24.8 4.9 %collective-permute-start.5 = (f32[128,768]{1,0:T(8,128)S(1)}, f32[128,768]{1,0:T(8,128)S(1)}, u32[]{:S(2)}, u32[]{:S(2)}) collective-permute-start(f32[128,768]{1,0:T(8,128)S(1)} %get-tuple-element.92), channel_id=1, source_target_pairs={{0,1},{1,0},{2,3},{3,2},{4,5},{5,4},{6,7},{7,6},{8,9},{9,8},{10,11... | collective-permute-start | bytes 1179656 | tf_op jit(solution)/shard_map/ppermute | solution.py:430
  28.4 9.2 %collective-permute-start.8 = (bf16[256,256]{1,0:T(8,128)(2,1)S(1)}, bf16[256,256]{1,0:T(8,128)(2,1)S(1)}, u32[]{:S(2)}, u32[]{:S(2)}) collective-permute-start(bf16[256,256]{1,0:T(8,128)(2,1)S(1)} %get-tuple-element.105), channel_id=1, source_target_pairs={{0,1},{1,0},{2,3},{3,2},{4,5},{5,4},{6,7},{7,6},{8,9},{9,8},{10,11... | collective-permute-start | bytes 393224 | tf_op jit(solution)/shard_map/ppermute | solution.py:430
  28.5 9.1 %collective-permute-start.9 = (bf16[256,256]{1,0:T(8,128)(2,1)S(1)}, bf16[256,256]{1,0:T(8,128)(2,1)S(1)}, u32[]{:S(2)}, u32[]{:S(2)}) collective-permute-start(bf16[256,256]{1,0:T(8,128)(2,1)S(1)} %get-tuple-element.106), channel_id=1, source_target_pairs={{1,2},{3,4},{5,6},{7,8},{9,10},{11,12},{13,14},{2,1},{4,3},{6,5},{... | collective-permute-start | bytes 393224 | tf_op jit(solution)/shard_map/ppermute | solution.py:430
  29.8 7.8 %collective-permute-start.6 = (bf16[64,768]{1,0:T(8,128)(2,1)S(1)}, bf16[64,768]{1,0:T(8,128)(2,1)S(1)}, u32[]{:S(2)}, u32[]{:S(2)}) collective-permute-start(bf16[64,768]{1,0:T(8,128)(2,1)S(1)} %get-tuple-element.94), channel_id=1, source_target_pairs={{0,2},{1,3},{2,0},{3,1},{4,6},{5,7},{6,4},{7,5},{8,10},{9,11},{10,... | collective-permute-start | bytes 294920 | tf_op jit(solution)/shard_map/ppermute | solution.py:430
  38.1 25.2 %collective-permute-start.16 = (bf16[4,256,256]{2,1,0:T(8,128)(2,1)S(1)}, bf16[4,256,256]{2,1,0:T(8,128)(2,1)S(1)}, u32[]{:S(2)}, u32[]{:S(2)}) collective-permute-start(bf16[4,256,256]{2,1,0:T(8,128)(2,1)S(1)} %copy-done.2), channel_id=1, source_target_pairs={{1,2},{3,4},{5,6},{7,8},{9,10},{11,12},{13,14},{2,1},{4,3},{6,5},{... | collective-permute-start | bytes 1572872 | tf_op jit(solution)/shard_map/ppermute | solution.py:430
  38.8 13.2 %collective-permute-start.7 = (bf16[32,768]{1,0:T(8,128)(2,1)S(1)}, bf16[32,768]{1,0:T(8,128)(2,1)S(1)}, u32[]{:S(2)}, u32[]{:S(2)}) collective-permute-start(bf16[32,768]{1,0:T(8,128)(2,1)S(1)} %get-tuple-element.102), channel_id=1, source_target_pairs={{0,4},{1,5},{2,6},{3,7},{4,0},{5,1},{6,2},{7,3},{8,12},{9,13},{10,... | collective-permute-start | bytes 147464 | tf_op jit(solution)/shard_map/ppermute | solution.py:430
  43.9 14.8 %collective-permute-start.13 = (bf16[256,128]{1,0:T(8,128)(2,1)S(1)}, bf16[256,128]{1,0:T(8,128)(2,1)S(1)}, u32[]{:S(2)}, u32[]{:S(2)}) collective-permute-start(bf16[256,128]{1,0:T(8,128)(2,1)S(1)} %get-tuple-element.125), channel_id=1, source_target_pairs={{0,1},{1,0},{2,3},{3,2},{4,5},{5,4},{6,7},{7,6},{8,9},{9,8},{10,11... | collective-permute-start | bytes 196616 | tf_op jit(solution)/shard_map/ppermute | solution.py:430
  44.2 19.1 %collective-permute-start.15 = (bf16[256,128]{1,0:T(8,128)(2,1)S(1)}, bf16[256,128]{1,0:T(8,128)(2,1)S(1)}, u32[]{:S(2)}, u32[]{:S(2)}) collective-permute-start(bf16[256,128]{1,0:T(8,128)(2,1)S(1)} %get-tuple-element.130), channel_id=1, source_target_pairs={{1,2},{3,4},{5,6},{7,8},{9,10},{11,12},{13,14},{2,1},{4,3},{6,5},{... | collective-permute-start | bytes 196616 | tf_op jit(solution)/shard_map/ppermute | solution.py:430
  52.0 5.3 %collective-permute-start.10 = (bf16[32,768]{1,0:T(8,128)(2,1)S(1)}, bf16[32,768]{1,0:T(8,128)(2,1)S(1)}, u32[]{:S(2)}, u32[]{:S(2)}) collective-permute-start(bf16[32,768]{1,0:T(8,128)(2,1)S(1)} %get-tuple-element.114), channel_id=1, source_target_pairs={{0,8},{1,9},{2,10},{3,11},{4,12},{5,13},{6,14},{7,15},{8,0},{9,1},... | collective-permute-start | bytes 147464 | tf_op jit(solution)/shard_map/ppermute | solution.py:430
  57.5 1.2 %collective-permute-start.11 = (f32[8,128]{1,0:T(8,128)S(1)}, f32[8,128]{1,0:T(8,128)S(1)}, u32[]{:S(2)}, u32[]{:S(2)}) collective-permute-start(f32[8,128]{1,0:T(8,128)S(1)} %get-tuple-element.118.own_ref), channel_id=1, source_target_pairs={{0,1},{1,0},{2,3},{3,2},{4,5},{5,4},{6,7},{7,6},{8,9},{9,8},{10,11... | collective-permute-start | bytes 12296 | tf_op jit(solution)/shard_map/ppermute | solution.py:430
  58.7 3.6 %collective-permute-start.12 = (f32[8,128]{1,0:T(8,128)S(1)}, f32[8,128]{1,0:T(8,128)S(1)}, u32[]{:S(2)}, u32[]{:S(2)}) collective-permute-start(f32[8,128]{1,0:T(8,128)S(1)} %shard_map.123.own_ref), channel_id=1, source_target_pairs={{0,2},{1,3},{2,0},{3,1},{4,6},{5,7},{6,4},{7,5},{8,10},{9,11},{10,... | collective-permute-start | bytes 12296 | tf_op jit(solution)/shard_map/ppermute | solution.py:430
  62.3 3.7 %collective-permute-start.14 = (f32[8,128]{1,0:T(8,128)S(1)}, f32[8,128]{1,0:T(8,128)S(1)}, u32[]{:S(2)}, u32[]{:S(2)}) collective-permute-start(f32[8,128]{1,0:T(8,128)S(1)} %shard_map.126.sq_ref), channel_id=1, source_target_pairs={{0,4},{1,5},{2,6},{3,7},{4,0},{5,1},{6,2},{7,3},{8,12},{9,13},{10,... | collective-permute-start | bytes 12296 | tf_op jit(solution)/shard_map/ppermute | solution.py:430
